TPU v7x, 32 devices: a whole 2x2x4 slice. The times are simulated.
32 devices in a mesh: seq: 4 (over y, x), head: 8 (over z, core).
Axes of the slice: x: 2, y: 2, z: 4, core: 2. Of those that a mesh axis runs over, the one named last changes fastest.
Arguments:
- inputs: bfloat16 [6144, 2048], P(('seq', 'head')), may hold values from -6 to 6
- segments: int32 [4, 1536], P('seq'), may hold values from 0 to 3, never falling along the last dimension, each value on 1 to 1024 neighbouring positions
- cotangent: bfloat16 [6144, 2048], P(('seq', 'head')), may hold values from -6 to 6
- norm_attn: bfloat16 [2048], P(('seq', 'head')), may hold values from 0.099609375 to 1.8984375
- attn_in: bfloat16 [2048, 1536], P(('seq', 'head')), may hold values from -0.125 to 0.125
- norm_latent: bfloat16 [1024], P(('seq', 'head')), may hold values from 0.099609375 to 1.8984375
- query_up: bfloat16 [1024, 4096], P(None, 'head'), may hold values from -0.1875 to 0.1875
- out_proj: bfloat16 [4096, 2048], P('head'), may hold values from -0.375 to 0.375
- norm_mlp: bfloat16 [2048], P(('seq', 'head')), may hold values from 0.099609375 to 1.8984375
- gate_up: bfloat16 [2048, 11264], P(('seq', 'head')), may hold values from -0.125 to 0.125
- down_proj: bfloat16 [5632, 2048], P(('seq', 'head')), may hold values from -0.078125 to 0.078125
Outputs:
- layer_out: bfloat16 [6144, 2048], P(('seq', 'head'))
- input_grad: float32 [6144, 2048], P(('seq', 'head'))
- attnnorm_grad: float32 [2048], P(('seq', 'head'))
- attnin_grad: float32 [2048, 1536], P(('seq', 'head'))
- latnorm_grad: float32 [1024], P(('seq', 'head'))
- queryup_grad: float32 [1024, 4096], P('seq', 'head')
- outproj_grad: float32 [4096, 2048], P('head', 'seq')
- mlpnorm_grad: float32 [2048], P(('seq', 'head'))
- gateup_grad: float32 [2048, 11264], P(('seq', 'head'))
- downproj_grad: float32 [5632, 2048], P(('seq', 'head'))
Inputs may be any that keep to these rules, and one draw needn't show every extreme that they name: `segments`: in each packed row the ids never fall, every id occurs, and each document holds at most 1024 tokens.
All inputs are finite; a program needn't handle non-finite values.
Results may differ from a plain program's by a relative error of at most 0.018.
Values may be sent and summed in bfloat16 or wider, within the bound.
A program may use at most 320 MiB of HBM per device.

v0:
```python
import jax
import jax.numpy as jnp
from jax import lax
from jax.sharding import PartitionSpec as P

DH = 256
QR = 1024
FF = 5632


EPS = 1e-06
THETA = 10000.0
NEG = -1e30


def contract(left, right):
    return lax.dot_general(
        left, right, (((1,), (1,)), ((), ())), preferred_element_type=jnp.float32
    )


def transposed(left, right):
    return lax.dot_general(
        left, right, (((0,), (0,)), ((), ())), preferred_element_type=jnp.float32
    )


def rms_norm(values_in, gain_vec):
    return (
        values_in
        * lax.rsqrt(jnp.mean(values_in * values_in, axis=-1, keepdims=True) + EPS)
        * gain_vec
    )


def rotary(values_in, cosine, sine):
    half_dim = values_in.shape[-1] // 2
    first_half = values_in[..., :half_dim]
    second_half = values_in[..., half_dim:]
    return jnp.concatenate(
        [first_half * cosine - second_half * sine, second_half * cosine + first_half * sine],
        axis=-1,
    )


def segment_starts(segment_row):
    index = jnp.arange(segment_row.shape[0], dtype=jnp.int32)
    opens = jnp.concatenate([jnp.ones((1,), jnp.bool_), segment_row[1:] != segment_row[:-1]])
    return lax.cummax(jnp.where(opens, index, jnp.zeros_like(index)), axis=0)


def angles(segment_row):
    index = jnp.arange(segment_row.shape[0], dtype=jnp.int32)
    places = (index - segment_starts(segment_row)).astype(jnp.float32)
    exponent = jnp.arange(DH // 2, dtype=jnp.float32) * (-2.0 / DH)
    frequency = jnp.power(jnp.float32(THETA), exponent)
    turned = places[:, None] * frequency[None, :]
    return (jnp.cos(turned), jnp.sin(turned))


def shards(
    inputs,
    segments,
    cotangent,
    norm_attn,
    attn_in,
    norm_latent,
    query_up,
    out_proj,
    norm_mlp,
    gate_up,
    down_proj,
):
    head_count = lax.axis_size("head")
    head_place = lax.axis_index("head")
    shard_rows = inputs.shape[0]
    group_rows = shard_rows * head_count
    heads_dev = query_up.shape[1] // DH
    block_rows = min(512, group_rows)
    block_count = group_rows // block_rows
    score_scale = DH ** (-0.5)
    gathered = (
        lax.all_gather(norm_attn, ("seq", "head"), axis=0, tiled=True),
        lax.all_gather(attn_in, ("seq", "head"), axis=0, tiled=True),
        lax.all_gather(norm_latent, ("seq", "head"), axis=0, tiled=True),
        lax.all_gather(norm_mlp, ("seq", "head"), axis=0, tiled=True),
        lax.all_gather(gate_up, ("seq", "head"), axis=0, tiled=True),
        lax.all_gather(down_proj, ("seq", "head"), axis=0, tiled=True),
    )
    weight_gu = gathered[4]
    weight_down = gathered[5]
    gain_attn = gathered[0].astype(jnp.float32)
    weight_in = gathered[1]
    gain_latent = gathered[2].astype(jnp.float32)
    gain_mlp = gathered[3].astype(jnp.float32)
    segment_row = segments[0]
    cosine, sine = angles(segment_row)
    row_start = head_place * shard_rows
    cos_local = lax.dynamic_slice_in_dim(cosine, row_start, shard_rows, 0)
    sin_local = lax.dynamic_slice_in_dim(sine, row_start, shard_rows, 0)
    inputs_f = inputs.astype(jnp.float32)
    normed = rms_norm(inputs_f, gain_attn).astype(jnp.bfloat16)
    projected = jnp.dot(normed, weight_in, preferred_element_type=jnp.float32)
    latent = projected[:, :QR]
    key_raw = projected[:, QR : QR + DH]
    latent_n = rms_norm(latent, gain_latent).astype(jnp.bfloat16)
    keys_local = rotary(key_raw, cos_local, sin_local).astype(jnp.bfloat16)
    values_local = projected[:, QR + DH :].astype(jnp.bfloat16)
    latent_all, keys, values = (
        lax.all_gather(latent_n, "head", axis=0, tiled=True),
        lax.all_gather(keys_local, "head", axis=0, tiled=True),
        lax.all_gather(values_local, "head", axis=0, tiled=True),
    )
    query_raw = jnp.dot(latent_all, query_up, preferred_element_type=jnp.float32)
    queries = rotary(
        query_raw.reshape(group_rows, heads_dev, DH), cosine[:, None, :], sine[:, None, :]
    ).astype(jnp.bfloat16)

    def lowest():
        return jnp.zeros((), jnp.int32)

    def query_block(source, qblock):
        piece = lax.dynamic_slice_in_dim(source, qblock * block_rows, block_rows, 0)
        return piece.reshape(block_rows * heads_dev, DH)

    def scores_of(query_blk, qblock, kblock):
        key_blk = lax.dynamic_slice_in_dim(keys, kblock * block_rows, block_rows, 0)
        raw = contract(query_blk, key_blk).reshape(block_rows, heads_dev, block_rows) * score_scale
        place_query = qblock * block_rows + jnp.arange(block_rows, dtype=jnp.int32)
        place_key = kblock * block_rows + jnp.arange(block_rows, dtype=jnp.int32)
        seg_query = lax.dynamic_slice_in_dim(segment_row, qblock * block_rows, block_rows, 0)
        seg_key = lax.dynamic_slice_in_dim(segment_row, kblock * block_rows, block_rows, 0)
        allowed = (seg_query[:, None] == seg_key[None, :]) & (
            place_query[:, None] >= place_key[None, :]
        )
        return jnp.where(allowed[:, None, :], raw, NEG)

    def forward_block(qblock):
        query_blk = query_block(queries, qblock)
        first_key = lowest()

        def max_step(kblock, state):
            row_top, row_total = state
            scores = scores_of(query_blk, qblock, kblock)
            new_top = jnp.maximum(row_top, jnp.max(scores, axis=-1))
            row_total = row_total * jnp.exp(row_top - new_top) + jnp.sum(
                jnp.exp(scores - new_top[..., None]), axis=-1
            )
            return (new_top, row_total)

        start_state = (
            jnp.full((block_rows, heads_dev), NEG, jnp.float32),
            jnp.zeros((block_rows, heads_dev), jnp.float32),
        )
        row_top, row_total = lax.fori_loop(first_key, qblock + 1, max_step, start_state)

        def value_step(kblock, accum):
            scores = scores_of(query_blk, qblock, kblock)
            attention = jnp.exp(scores - row_top[..., None]) / row_total[..., None]
            value_blk = lax.dynamic_slice_in_dim(values, kblock * block_rows, block_rows, 0)
            weights_b = attention.astype(jnp.bfloat16).reshape(block_rows * heads_dev, block_rows)
            return accum + jnp.dot(weights_b, value_blk, preferred_element_type=jnp.float32)

        accum = lax.fori_loop(
            first_key, qblock + 1, value_step, jnp.zeros((block_rows * heads_dev, DH), jnp.float32)
        )
        return (accum.astype(jnp.bfloat16).reshape(block_rows, heads_dev * DH), row_top, row_total)

    block_ids = jnp.arange(block_count, dtype=jnp.int32)
    mixed_blocks, row_tops, row_totals = lax.map(forward_block, block_ids)
    mixed = mixed_blocks.reshape(group_rows, heads_dev * DH)
    piece = mixed
    attn_out = lax.psum_scatter(
        jnp.dot(piece, out_proj, preferred_element_type=jnp.float32),
        "head",
        scatter_dimension=0,
        tiled=True,
    )
    hidden = inputs_f + attn_out
    normed_mlp = rms_norm(hidden, gain_mlp).astype(jnp.bfloat16)
    ff_cols = FF
    joined = jnp.dot(normed_mlp, weight_gu, preferred_element_type=jnp.float32)
    gate_part = joined[:, :ff_cols]
    up_part = joined[:, ff_cols:]
    activated = (jax.nn.silu(gate_part) * up_part).astype(jnp.bfloat16)
    down_out = jnp.dot(activated, weight_down, preferred_element_type=jnp.float32)
    layer_out = (hidden + down_out).astype(jnp.bfloat16)
    down_grad = transposed(activated, cotangent)
    grad_act = contract(cotangent, weight_down)
    silu_prod, act_back = jax.vjp(
        lambda gate_in, up_in: jax.nn.silu(gate_in) * up_in, gate_part, up_part
    )
    grad_gate, grad_up = act_back(grad_act)
    grad_gu = jnp.concatenate([grad_gate, grad_up], axis=1).astype(jnp.bfloat16)
    gu_grad = transposed(normed_mlp, grad_gu)
    grad_nmlp = contract(grad_gu, weight_gu)
    norm_value, mlp_back = jax.vjp(rms_norm, hidden, gain_mlp)
    grad_hidden_n, mlpnorm_part = mlp_back(grad_nmlp)
    grad_hidden = cotangent.astype(jnp.float32) + grad_hidden_n
    grad_attn = grad_hidden.astype(jnp.bfloat16)
    grad_attn_all = lax.all_gather(grad_attn, "head", axis=0, tiled=True)
    grad_mixed = contract(grad_attn_all, out_proj).astype(jnp.bfloat16)
    outproj_local = transposed(grad_attn_all, mixed)

    def back_block(state, qblock):
        key_accum, value_accum = state
        query_blk = query_block(queries, qblock)
        grad_out = query_block(grad_mixed, qblock)
        row_top = row_tops[qblock]
        row_total = row_totals[qblock]
        first_key = lowest()

        def weights_and_grads(kblock):
            scores = scores_of(query_blk, qblock, kblock)
            attention = jnp.exp(scores - row_top[..., None]) / row_total[..., None]
            value_blk = lax.dynamic_slice_in_dim(values, kblock * block_rows, block_rows, 0)
            grad_weights = contract(grad_out, value_blk).reshape(block_rows, heads_dev, block_rows)
            return (attention, grad_weights)

        def dots_step(kblock, row_dots):
            attention, grad_weights = weights_and_grads(kblock)
            return row_dots + jnp.sum(attention * grad_weights, axis=-1)

        row_dots = lax.fori_loop(
            first_key, qblock + 1, dots_step, jnp.zeros((block_rows, heads_dev), jnp.float32)
        )

        def grad_step(kblock, inner_state):
            query_grad, key_acc, value_acc = inner_state
            attention, grad_weights = weights_and_grads(kblock)
            grad_scores = (
                (attention * (grad_weights - row_dots[..., None]))
                .astype(jnp.bfloat16)
                .reshape(block_rows * heads_dev, block_rows)
            )
            key_blk = lax.dynamic_slice_in_dim(keys, kblock * block_rows, block_rows, 0)
            query_grad = (
                query_grad
                + jnp.dot(grad_scores, key_blk, preferred_element_type=jnp.float32) * score_scale
            )
            key_part = transposed(grad_scores, query_blk) * score_scale
            weights_b = attention.astype(jnp.bfloat16).reshape(block_rows * heads_dev, block_rows)
            value_part = transposed(weights_b, grad_out)
            key_old = lax.dynamic_slice_in_dim(key_acc, kblock * block_rows, block_rows, 0)
            value_old = lax.dynamic_slice_in_dim(value_acc, kblock * block_rows, block_rows, 0)
            key_acc = lax.dynamic_update_slice_in_dim(
                key_acc, key_old + key_part, kblock * block_rows, 0
            )
            value_acc = lax.dynamic_update_slice_in_dim(
                value_acc, value_old + value_part, kblock * block_rows, 0
            )
            return (query_grad, key_acc, value_acc)

        start_inner = (jnp.zeros((block_rows * heads_dev, DH), jnp.float32), key_accum, value_accum)
        query_grad, key_accum, value_accum = lax.fori_loop(
            first_key, qblock + 1, grad_step, start_inner
        )
        return ((key_accum, value_accum), query_grad)

    start_outer = (
        jnp.zeros((group_rows, DH), jnp.float32),
        jnp.zeros((group_rows, DH), jnp.float32),
    )
    (key_grads, value_grads), query_grads = lax.scan(back_block, start_outer, block_ids)
    query_grads = query_grads.reshape(group_rows, heads_dev, DH)
    turned_query, query_back = jax.vjp(
        lambda query_in: rotary(query_in, cosine[:, None, :], sine[:, None, :]),
        query_raw.reshape(group_rows, heads_dev, DH),
    )
    (grad_query,) = query_back(query_grads)
    grad_query = grad_query.reshape(group_rows, heads_dev * DH).astype(jnp.bfloat16)
    queryup_local = transposed(latent_all, grad_query)
    grad_latent_part = contract(grad_query, query_up)
    grad_latent_n, grad_keys, grad_values = (
        lax.psum_scatter(grad_latent_part, "head", scatter_dimension=0, tiled=True),
        lax.psum_scatter(key_grads, "head", scatter_dimension=0, tiled=True),
        lax.psum_scatter(value_grads, "head", scatter_dimension=0, tiled=True),
    )
    queryup_grad, outproj_turned = (
        lax.psum_scatter(
            queryup_local.astype(jnp.bfloat16), "seq", scatter_dimension=0, tiled=True
        ).astype(jnp.float32),
        lax.psum_scatter(
            outproj_local.astype(jnp.bfloat16), "seq", scatter_dimension=0, tiled=True
        ).astype(jnp.float32),
    )
    outproj_grad = outproj_turned.T
    latent_value, latent_back = jax.vjp(rms_norm, latent, gain_latent)
    grad_latent, latnorm_part = latent_back(grad_latent_n)
    turned_key, key_back = jax.vjp(lambda key_in: rotary(key_in, cos_local, sin_local), key_raw)
    (grad_key_raw,) = key_back(grad_keys)
    grad_proj = jnp.concatenate([grad_latent, grad_key_raw, grad_values], axis=1).astype(
        jnp.bfloat16
    )
    attnin_part = transposed(normed, grad_proj)
    grad_normed = contract(grad_proj, weight_in)
    input_value, input_back = jax.vjp(rms_norm, inputs_f, gain_attn)
    grad_input_n, attnnorm_part = input_back(grad_normed)
    input_grad = grad_hidden + grad_input_n
    gradients = (attnnorm_part, attnin_part, latnorm_part, mlpnorm_part, gu_grad, down_grad)
    gradients = (
        lax.psum_scatter(gradients[0], ("seq", "head"), scatter_dimension=0, tiled=True),
        lax.psum_scatter(gradients[1], ("seq", "head"), scatter_dimension=0, tiled=True),
        lax.psum_scatter(gradients[2], ("seq", "head"), scatter_dimension=0, tiled=True),
        lax.psum_scatter(gradients[3], ("seq", "head"), scatter_dimension=0, tiled=True),
        lax.psum_scatter(gradients[4], ("seq", "head"), scatter_dimension=0, tiled=True),
        lax.psum_scatter(gradients[5], ("seq", "head"), scatter_dimension=0, tiled=True),
    )
    attnnorm_grad = gradients[0]
    attnin_grad = gradients[1]
    latnorm_grad = gradients[2]
    mlpnorm_grad = gradients[3]
    gateup_grad = gradients[4]
    downproj_grad = gradients[5]
    return (
        layer_out,
        input_grad,
        attnnorm_grad,
        attnin_grad,
        latnorm_grad,
        queryup_grad,
        outproj_grad,
        mlpnorm_grad,
        gateup_grad,
        downproj_grad,
    )


def solution(mesh):
    in_specs = (
        P(("seq", "head"), None),
        P("seq", None),
        P(("seq", "head"), None),
        P(("seq", "head")),
        P(("seq", "head"), None),
        P(("seq", "head")),
        P(None, "head"),
        P("head", None),
        P(("seq", "head")),
        P(("seq", "head"), None),
        P(("seq", "head"), None),
    )
    out_specs = (
        P(("seq", "head"), None),
        P(("seq", "head"), None),
        P(("seq", "head")),
        P(("seq", "head"), None),
        P(("seq", "head")),
        P("seq", "head"),
        P("head", "seq"),
        P(("seq", "head")),
        P(("seq", "head"), None),
        P(("seq", "head"), None),
    )
    return jax.shard_map(shards, mesh=mesh, in_specs=in_specs, out_specs=out_specs, check_vma=False)
```

profile of v0, /device:TPU:0, one launch (start us, length us, event | category | flops | bytes accessed | tf_op | source)
XLA Modules:
  0.0 2958.4 jit_solution(5514717080655293126)
XLA Ops:
  10.5 43.2 %all-reduce.11 = (bf16[2048]{0:T(1024)(128)(2,1)S(1)}, bf16[1024]{0:T(1024)(128)(2,1)S(1)}, bf16[2048]{0:T(1024)(128)(2,1)}) all-reduce(bf16[2048]{0:T(1024)(128)(2,1)S(1)} %dynamic-update-slice, bf16[1024]{0:T(1024)(128)(2,1)S(1)} %dynamic-update-slice.1, ...), channel_id=1, replica_groups=mesh['seq'=4,'head'=8] {'seq','head'}, use_global_device_ids=true, to_apply=%add.4 | all-reduce | flops 5120 | bytes 20480
  55.7 27.9 all-gather.6.cloned.1.call-done
  94.7 19.8 all_gather.34
  114.5 20.2 all_gather.35
  158.3 161.5 %while.87 = (s32[]{:T(128)}, bf16[3,512,512]{2,1,0:T(8,128)(2,1)}, f32[3,512,2]{2,1,0:T(8,128)}, f32[3,512,2]{2,1,0:T(8,128)}, s32[3]{0:T(128)S(1)}, /*index=5*/...) while((s32[]{:T(128)}, bf16[3,512,512]{2,1,0:T(8,128)(2,1)}, ...), condition=%wide.region_11.12_spmd, body=%wide.region_4.11_spmd.sunk | while | flops 812650496 | bytes 23046252 | solution.py:170
  163.4 11.7 while.91
  196.6 23.5 while.91
  222.5 17.9 while.92
  250.4 35.2 %while.91 = (s32[]{:T(128)}, f32[512,2]{1,0:T(8,128)S(1)}, f32[512,2]{1,0:T(8,128)}, s32[]{:T(128)}, s32[512]{0:T(512)S(1)}, /*index=5*/s32[1536]{0:T(1024)S(1)}...) while((s32[]{:T(128)}, f32[512,2]{1,0:T(8,128)S(1)}, ...), condition=%wide.region_8.8_spmd, body=%wide.region_5.7_spmd.sunk | while | flops 271846400 | bytes 8777979 | solution.py:155
  288.1 26.8 while.92
  329.4 126.2 %reduce-scatter.10.cloned.1.call-done = f32[192,2048]{1,0:T(8,128)} async-done(((f32[1536,2048]{1,0:T(8,128)}), f32[192,2048]{1,0:T(8,128)}) %reduce-scatter.10.cloned.1.call-update) | async-done | bytes 1572880 | tf_op jit(solution)/shard_map/reduce_scatter | solution.py:173
  458.4 253.6 %all-gather.10.cloned.1.call-done = bf16[2048,11264]{1,0:T(8,128)(2,1)} async-done(((bf16[64,11264]{1,0:T(8,128)(2,1)}), bf16[2048,11264]{1,0:T(8,128)(2,1)}) %all-gather.10.cloned.1.call-update) | async-done | bytes 46137360 | tf_op jit(solution)/shard_map/all_gather | solution.py:87
  712.0 21.3 fusion.70
  733.3 124.2 %all-gather.12.cloned.1.call-done = bf16[5632,2048]{1,0:T(8,128)(2,1)} async-done(((bf16[176,2048]{1,0:T(8,128)(2,1)}), bf16[5632,2048]{1,0:T(8,128)(2,1)}) %all-gather.12.cloned.1.call-update) | async-done | bytes 23068688 | tf_op jit(solution)/shard_map/all_gather | solution.py:88
  857.6 16.8 fusion.43
  874.3 23.5 multiply_reduce_fusion
  901.2 63.0 %all-gather.14.cloned.1.call-done = bf16[1536,2048]{1,0:T(8,128)(2,1)} async-done(((bf16[192,2048]{1,0:T(8,128)(2,1)}), bf16[1536,2048]{1,0:T(8,128)(2,1)}) %all-gather.14.cloned.1.call-update) | async-done | bytes 6291472 | tf_op jit(solution)/shard_map/all_gather | solution.py:201
  974.3 145.5 %while.90 = (s32[]{:T(128)}, f32[1536,256]{1,0:T(8,128)}, f32[1536,256]{1,0:T(8,128)}, f32[3,1024,256]{2,1,0:T(8,128)}, s32[3]{0:T(128)S(1)}, /*index=5*/bf16[15...) while((s32[]{:T(128)}, f32[1536,256]{1,0:T(8,128)}, ...), condition=%wide.region_21.22_spmd, body=%wide.region_15.21_spmd.sunk | while | flops 1888880640 | bytes 70727152 | solution.py:264
  994.5 9.8 while.94
  1015.6 13.1 while.93
  1033.2 19.5 while.94
  1064.1 19.7 while.93
  1088.2 29.3 while.94
  1153.8 33.5 %reduce-scatter.14.cloned.1.call-done = f32[192,256]{1,0:T(8,128)} async-done(((f32[1536,256]{1,0:T(8,128)}), f32[192,256]{1,0:T(8,128)}) %reduce-scatter.14.cloned.1.call-update) | async-done | bytes 196624 | tf_op jit(solution)/shard_map/reduce_scatter | solution.py:276
  1188.3 69.1 %reduce-scatter.12.cloned.1.call-done = f32[192,1024]{1,0:T(8,128)} async-done(((f32[1536,1024]{1,0:T(8,128)}), f32[192,1024]{1,0:T(8,128)}) %reduce-scatter.12.cloned.1.call-update) | async-done | bytes 786448 | tf_op jit(solution)/shard_map/reduce_scatter | solution.py:275
  1266.7 20.0 fusion.77
  1288.1 35.6 %fusion.45 = f32[2048,11264]{1,0:T(8,128)} fusion(bf16[192,5632]{1,0:T(8,128)(2,1)} %get-tuple-element.872, bf16[192,5632]{1,0:T(8,128)(2,1)} %get-tuple-element.871, f32[192,2048]{1,0:T(8,128)S(1)} %copy-done.18, f32[2048]{0:T(1024)S(1)} %copy-done.32, f32[192]{0:T(256)S(1)} %copy-done.35), kind=kOutput, calls=%fused_computation.89 | convolution fusion | flops 8868200448 | bytes 98181888 | tf_op jit(solution)/shard_map/dot_general | solution.py:23
  1323.7 13.8 fusion.47
  1348.4 38.1 %all-reduce.10 = (f32[2048]{0:T(1024)S(1)}, f32[1024]{0:T(1024)S(1)}, f32[2048]{0:T(1024)S(1)}) all-reduce(f32[2048]{0:T(1024)S(1)} %get-tuple-element.709, f32[1024]{0:T(1024)S(1)} %get-tuple-element.711, f32[2048]{0:T(1024)S(1)} %copy-done.51), channel_id=6, replica_groups=mesh['seq'=4,'head'=8] {'seq','head'}, use_global_device_ids=true, to_apply=%region_28.29.clone | all-reduce | flops 5120 | bytes 40960
  1393.0 94.1 %reduce-scatter.18.cloned.1.call-done = f32[64,1536]{1,0:T(8,128)} async-done(((f32[2048,1536]{1,0:T(8,128)}), f32[64,1536]{1,0:T(8,128)}) %reduce-scatter.18.cloned.1.call-update) | async-done | bytes 393232 | tf_op jit(solution)/shard_map/reduce_scatter | solution.py:303
  1487.1 494.0 %reduce-scatter.26.cloned.1.call-done = f32[176,2048]{1,0:T(8,128)} async-done(((f32[5632,2048]{1,0:T(8,128)}), f32[176,2048]{1,0:T(8,128)}) %reduce-scatter.26.cloned.1.call-update) | async-done | bytes 1441808 | tf_op jit(solution)/shard_map/reduce_scatter | solution.py:307
  1981.1 970.3 %reduce-scatter.24.cloned.1.call-done = f32[64,11264]{1,0:T(8,128)} async-done(((f32[2048,11264]{1,0:T(8,128)}), f32[64,11264]{1,0:T(8,128)}) %reduce-scatter.24.cloned.1.call-update) | async-done | bytes 2883600 | tf_op jit(solution)/shard_map/reduce_scatter | solution.py:306
  (669 shorter events, 434.8 us)
Async XLA Ops:
  7.2 312.7 %copy-start = (bf16[512,2048]{1,0:T(8,128)(2,1)S(1)}, bf16[512,2048]{1,0:T(8,128)(2,1)}, u32[]{:S(2)}) copy-start(bf16[512,2048]{1,0:T(8,128)(2,1)} %param.30) | copy-start | bytes 6291460
  7.2 76.4 %all-gather.6.cloned.1.call-start = ((), (), s32[]{:S(2)}) async-start(), calls=%async_computation.9 | async-start | bytes 6488064 | tf_op jit(solution)/shard_map/all_gather | solution.py:84
  7.9 130.9 %all-gather.8.cloned.1.call-start = ((), (), s32[]{:S(2)}) async-start(), calls=%async_computation.10 | async-start | bytes 3538944 | tf_op jit(solution)/shard_map/all_gather | solution.py:110
  53.8 34.3 %copy-start.36 = (f32[2048]{0:T(1024)}, f32[2048]{0:T(1024)S(1)}, u32[]{:S(2)}) copy-start(f32[2048]{0:T(1024)S(1)} %convert_element_type.86) | copy-start | bytes 24580
  53.8 35.2 %copy-start.38 = (f32[1024]{0:T(1024)}, f32[1024]{0:T(1024)S(1)}, u32[]{:S(2)}) copy-start(f32[1024]{0:T(1024)S(1)} %convert_element_type.88) | copy-start | bytes 12292
  55.7 27.9 copy-start.41
  89.9 365.7 %reduce-scatter.10.cloned.1.call-start = ((), (), s32[]{:S(2)}) async-start(), calls=%async_computation.11 | async-start | bytes 14155776 | tf_op jit(solution)/shard_map/reduce_scatter | solution.py:173
  327.7 127.9 %copy-start.19 = (bf16[192,2048]{1,0:T(8,128)(2,1)S(1)}, bf16[192,2048]{1,0:T(8,128)(2,1)}, u32[]{:S(2)}) copy-start(bf16[192,2048]{1,0:T(8,128)(2,1)} %param.23) | copy-start | bytes 2359300
  327.7 384.3 %all-gather.10.cloned.1.call-start = ((), (), s32[]{:S(2)}) async-start(), calls=%async_computation.12 | async-start | bytes 47579136 | tf_op jit(solution)/shard_map/all_gather | solution.py:87
  328.3 529.2 %all-gather.12.cloned.1.call-start = ((), (), s32[]{:S(2)}) async-start(), calls=%async_computation.13 | async-start | bytes 23789568 | tf_op jit(solution)/shard_map/all_gather | solution.py:88
  328.9 635.4 %all-gather.14.cloned.1.call-start = ((), (), s32[]{:S(2)}) async-start(), calls=%async_computation.14 | async-start | bytes 7077888 | tf_op jit(solution)/shard_map/all_gather | solution.py:201
  329.4 568.5 %copy-start.31 = (f32[2048]{0:T(1024)}, f32[2048]{0:T(1024)S(1)}, u32[]{:S(2)}) copy-start(f32[2048]{0:T(1024)S(1)} %convert_element_type.91) | copy-start | bytes 24580
  458.4 439.4 %copy-start.34 = (f32[192]{0:T(256)}, f32[192]{0:T(256)S(1)}, u32[]{:S(2)}) copy-start(f32[192]{0:T(256)S(1)} %fusion.65) | copy-start | bytes 2308
  712.0 145.5 %copy-start.28 = (bf16[192,2048]{1,0:T(8,128)(2,1)S(1)}, bf16[192,2048]{1,0:T(8,128)(2,1)}, u32[]{:S(2)}) copy-start(bf16[192,2048]{1,0:T(8,128)(2,1)} %param.25) | copy-start | bytes 2359300
  901.2 251.6 %reduce-scatter.16.cloned.1.call-start = ((), (), s32[]{:S(2)}) async-start(), calls=%async_computation.17 | async-start | bytes 1769472 | tf_op jit(solution)/shard_map/reduce_scatter | solution.py:277
  1119.8 67.5 %reduce-scatter.14.cloned.1.call-start = ((), (), s32[]{:S(2)}) async-start(), calls=%async_computation.16 | async-start | bytes 1769472 | tf_op jit(solution)/shard_map/reduce_scatter | solution.py:276
  1120.5 136.9 %reduce-scatter.12.cloned.1.call-start = ((), (), s32[]{:S(2)}) async-start(), calls=%async_computation.15 | async-start | bytes 7077888 | tf_op jit(solution)/shard_map/reduce_scatter | solution.py:275
  1136.5 201.1 %reduce-scatter.20.cloned.1.call-start = ((), (), s32[]{:S(2)}) async-start(), calls=%async_computation.19 | async-start | bytes 1310720 | tf_op jit(solution)/shard_map/reduce_scatter | solution.py:280
  1141.8 197.6 %reduce-scatter.22.cloned.1.call-start = ((), (), s32[]{:S(2)}) async-start(), calls=%async_computation.20 | async-start | bytes 2621440 | tf_op jit(solution)/shard_map/reduce_scatter | solution.py:283
  1149.9 107.5 %copy-start.22 = (f32[192,1536]{1,0:T(8,128)S(1)}, f32[192,1536]{1,0:T(8,128)}, u32[]{:S(2)}) copy-start(f32[192,1536]{1,0:T(8,128)} %copy-done.21) | copy-start | bytes 3538948
  1149.9 107.5 %copy-start.39 = (f32[1024]{0:T(1024)S(1)}, f32[1024]{0:T(1024)}, u32[]{:S(2)}) copy-start(f32[1024]{0:T(1024)} %copy-done.38) | copy-start | bytes 12292
  1149.9 107.5 %copy-start.44 = (f32[192]{0:T(256)S(1)}, f32[192]{0:T(256)}, u32[]{:S(2)}) copy-start(f32[192]{0:T(256)} %copy-done.43) | copy-start | bytes 2308
  1149.9 108.9 %copy-start.50 = (f32[192]{0:T(256)S(1)}, f32[192]{0:T(256)}, u32[]{:S(2)}) copy-start(f32[192]{0:T(256)} %copy-done.49) | copy-start | bytes 2308
  1149.9 337.2 %reduce-scatter.18.cloned.1.call-start = ((), (), s32[]{:S(2)}) async-start(), calls=%async_computation.18 | async-start | bytes 12976128 | tf_op jit(solution)/shard_map/reduce_scatter | solution.py:303
  1188.3 70.8 %copy-start.20 = (bf16[192,2048]{1,0:T(8,128)(2,1)S(1)}, bf16[192,2048]{1,0:T(8,128)(2,1)}, u32[]{:S(2)}) copy-start(bf16[192,2048]{1,0:T(8,128)(2,1)} %param.23) | copy-start | bytes 2359300
  1188.3 70.8 %copy-start.37 = (f32[2048]{0:T(1024)S(1)}, f32[2048]{0:T(1024)}, u32[]{:S(2)}) copy-start(f32[2048]{0:T(1024)} %copy-done.36) | copy-start | bytes 24580
  1188.3 70.8 %copy-start.42 = (f32[192]{0:T(256)S(1)}, f32[192]{0:T(256)}, u32[]{:S(2)}) copy-start(f32[192]{0:T(256)} %copy-done.41) | copy-start | bytes 2308
  1265.6 715.6 %reduce-scatter.26.cloned.1.call-start = ((), (), s32[]{:S(2)}) async-start(), calls=%async_computation.22 | async-start | bytes 47579136 | tf_op jit(solution)/shard_map/reduce_scatter | solution.py:307
  1286.7 1664.7 %reduce-scatter.24.cloned.1.call-start = ((), (), s32[]{:S(2)}) async-start(), calls=%async_computation.21 | async-start | bytes 95158272 | tf_op jit(solution)/shard_map/reduce_scatter | solution.py:306
  1341.9 46.4 %copy-start.48 = (f32[192]{0:T(256)S(1)}, f32[192]{0:T(256)}, u32[]{:S(2)}) copy-start(f32[192]{0:T(256)} %copy-done.47) | copy-start | bytes 2308
  1341.9 46.4 %copy-start.46 = (f32[192]{0:T(256)S(1)}, f32[192]{0:T(256)}, u32[]{:S(2)}) copy-start(f32[192]{0:T(256)} %copy-done.45) | copy-start | bytes 2308
  1388.3 1563.2 %copy-start.1 = (bf16[512,2048]{1,0:T(8,128)(2,1)S(1)}, bf16[512,2048]{1,0:T(8,128)(2,1)}, u32[]{:S(2)}) copy-start(bf16[512,2048]{1,0:T(8,128)(2,1)} %param.30) | copy-start | bytes 6291460
  (96 other events, 190.0 us)
Sparse Core Ops, SparseCore 0:
  11.0 72.4 all-gather.5
  90.0 48.8 all-gather.7
  327.8 127.7 reduce-scatter.9
  458.3 253.6 all-gather.9
  714.7 142.7 all-gather.11
  901.3 62.9 all-gather.13
  1119.9 32.8 reduce-scatter.15
  1155.1 32.1 reduce-scatter.13
  1189.6 67.8 reduce-scatter.11
  1260.7 26.0 reduce-scatter.19
  1290.1 35.1 reduce-scatter.21
  1331.8 155.3 reduce-scatter.17
  1490.1 490.9 reduce-scatter.25
  1984.0 967.3 reduce-scatter.23
where the time goes:
time: 2970 us; the launch traced here: 2960 us
  waiting for transfers between devices  2270 us (76%)
  matrix products  262 us (9%)
  local copies, waits for them, and re-layouts  221 us (7%)
  blocking collectives  121 us (4%)
  other arithmetic  57.3 us (2%)
    reduce_scatter x1, waiting for transfers between devices, shards(): lax.psum_scatter(gradients[4], ('seq', 'head'), scatter_dimension=0, tile...  970 us
    reduce_scatter x1, waiting for transfers between devices, shards(): lax.psum_scatter(gradients[5], ('seq', 'head'), scatter_dimension=0, tile...  494 us
    all_gather x1, waiting for transfers between devices, shards(): lax.all_gather(gate_up, ('seq', 'head'), axis=0, tiled=True)  254 us
    reduce_scatter x1, waiting for transfers between devices, shards(): lax.psum_scatter(jnp.dot(piece, out_proj, preferred_element_type=jnp.floa...  126 us
    all_gather x1, waiting for transfers between devices, shards(): lax.all_gather(down_proj, ('seq', 'head'), axis=0, tiled=True)  124 us
    dot_general x35, matrix products, contract(): lax.dot_general(left, right, (((1,), (1,)), ((), ())), preferred_element_...  104 us
    reduce_scatter x1, waiting for transfers between devices, shards(): lax.psum_scatter(gradients[1], ('seq', 'head'), scatter_dimension=0, tile...  94.1 us
    broadcast_in_dim x72, local copies, waits for them, and re-layouts, scores_of(): return jnp.where(allowed[:, None, :], raw, NEG)  93.4 us
  transfers between devices with their start and end apart: 14, of which 12 were waited for; matrix products, arithmetic and copies ran while one was open for 5% of the time, Pallas kernels for 0%

commit v1 on v0

--- a/solution.py
+++ b/solution.py
@@ -79,20 +79,37 @@
     block_rows = min(512, group_rows)
     block_count = group_rows // block_rows
     score_scale = DH ** (-0.5)
-    gathered = (
-        lax.all_gather(norm_attn, ("seq", "head"), axis=0, tiled=True),
-        lax.all_gather(attn_in, ("seq", "head"), axis=0, tiled=True),
-        lax.all_gather(norm_latent, ("seq", "head"), axis=0, tiled=True),
-        lax.all_gather(norm_mlp, ("seq", "head"), axis=0, tiled=True),
-        lax.all_gather(gate_up, ("seq", "head"), axis=0, tiled=True),
-        lax.all_gather(down_proj, ("seq", "head"), axis=0, tiled=True),
-    )
-    weight_gu = gathered[4]
-    weight_down = gathered[5]
-    gain_attn = gathered[0].astype(jnp.float32)
-    weight_in = gathered[1]
-    gain_latent = gathered[2].astype(jnp.float32)
-    gain_mlp = gathered[3].astype(jnp.float32)
+    seq_count = lax.axis_size("seq")
+    own_rows = attn_in.shape[0]
+    own_latent = norm_latent.shape[0]
+    own_units = down_proj.shape[0]
+    units = seq_count * own_units
+    device_count = seq_count * head_count
+    proj_cols = attn_in.shape[1]
+    gain_cols = jnp.stack(
+        [norm_attn, norm_mlp, jnp.pad(norm_latent, (0, own_rows - own_latent))], axis=1
+    )
+    packed = jnp.concatenate([attn_in, jnp.pad(gain_cols, ((0, 0), (0, 125)))], axis=1)
+    packed_all = lax.all_gather(packed, ("seq", "head"), axis=0, tiled=True)
+    weight_in = packed_all[:, :proj_cols]
+    gain_attn = packed_all[:, proj_cols].astype(jnp.float32)
+    gain_mlp = packed_all[:, proj_cols + 1].astype(jnp.float32)
+    gain_latent = (
+        packed_all[:, proj_cols + 2]
+        .reshape(device_count, own_rows)[:, :own_latent]
+        .reshape(device_count * own_latent)
+        .astype(jnp.float32)
+    )
+    pieces = gate_up.reshape(own_rows, 2, seq_count, head_count, own_units)
+    pieces = pieces.transpose(3, 0, 1, 2, 4).reshape(head_count, own_rows, 2 * units)
+    turned = lax.all_to_all(pieces, "head", split_axis=0, concat_axis=0, tiled=True)
+    weight_gu = lax.all_gather(
+        turned.reshape(head_count * own_rows, 2 * units), "seq", axis=0, tiled=True
+    )
+    weight_gate = weight_gu[:, :units]
+    weight_up = weight_gu[:, units:]
+    weight_down = lax.all_gather(down_proj, "seq", axis=0, tiled=True)
+    cot_all = lax.all_gather(cotangent, "head", axis=0, tiled=True)
     segment_row = segments[0]
     cosine, sine = angles(segment_row)
     row_start = head_place * shard_rows
@@ -106,10 +123,13 @@
     latent_n = rms_norm(latent, gain_latent).astype(jnp.bfloat16)
     keys_local = rotary(key_raw, cos_local, sin_local).astype(jnp.bfloat16)
     values_local = projected[:, QR + DH :].astype(jnp.bfloat16)
+    joined_all = lax.all_gather(
+        jnp.concatenate([latent_n, keys_local, values_local], axis=1), "head", axis=0, tiled=True
+    )
     latent_all, keys, values = (
-        lax.all_gather(latent_n, "head", axis=0, tiled=True),
-        lax.all_gather(keys_local, "head", axis=0, tiled=True),
-        lax.all_gather(values_local, "head", axis=0, tiled=True),
+        joined_all[:, :QR],
+        joined_all[:, QR : QR + DH],
+        joined_all[:, QR + DH :],
     )
     query_raw = jnp.dot(latent_all, query_up, preferred_element_type=jnp.float32)
     queries = rotary(
@@ -171,29 +191,60 @@
     mixed = mixed_blocks.reshape(group_rows, heads_dev * DH)
     piece = mixed
     attn_out = lax.psum_scatter(
-        jnp.dot(piece, out_proj, preferred_element_type=jnp.float32),
+        jnp.dot(piece, out_proj, preferred_element_type=jnp.float32).astype(jnp.bfloat16),
         "head",
         scatter_dimension=0,
         tiled=True,
-    )
+    ).astype(jnp.float32)
     hidden = inputs_f + attn_out
     normed_mlp = rms_norm(hidden, gain_mlp).astype(jnp.bfloat16)
-    ff_cols = FF
-    joined = jnp.dot(normed_mlp, weight_gu, preferred_element_type=jnp.float32)
-    gate_part = joined[:, :ff_cols]
-    up_part = joined[:, ff_cols:]
+    nmlp_all = lax.all_gather(normed_mlp, "head", axis=0, tiled=True)
+    gate_part = jnp.dot(nmlp_all, weight_gate, preferred_element_type=jnp.float32)
+    up_part = jnp.dot(nmlp_all, weight_up, preferred_element_type=jnp.float32)
     activated = (jax.nn.silu(gate_part) * up_part).astype(jnp.bfloat16)
-    down_out = jnp.dot(activated, weight_down, preferred_element_type=jnp.float32)
-    layer_out = (hidden + down_out).astype(jnp.bfloat16)
-    down_grad = transposed(activated, cotangent)
-    grad_act = contract(cotangent, weight_down)
+    down_part = jnp.dot(activated, weight_down, preferred_element_type=jnp.float32)
+    grad_act = contract(cot_all, weight_down)
     silu_prod, act_back = jax.vjp(
         lambda gate_in, up_in: jax.nn.silu(gate_in) * up_in, gate_part, up_part
     )
     grad_gate, grad_up = act_back(grad_act)
-    grad_gu = jnp.concatenate([grad_gate, grad_up], axis=1).astype(jnp.bfloat16)
-    gu_grad = transposed(normed_mlp, grad_gu)
-    grad_nmlp = contract(grad_gu, weight_gu)
+    grad_gate = grad_gate.astype(jnp.bfloat16)
+    grad_up = grad_up.astype(jnp.bfloat16)
+    grad_nmlp = lax.psum_scatter(
+        (contract(grad_gate, weight_gate) + contract(grad_up, weight_up)).astype(jnp.bfloat16),
+        "head",
+        scatter_dimension=0,
+        tiled=True,
+    ).astype(jnp.float32)
+    down_out = lax.psum_scatter(
+        down_part.astype(jnp.bfloat16), "head", scatter_dimension=0, tiled=True
+    ).astype(jnp.float32)
+    layer_out = (hidden + down_out).astype(jnp.bfloat16)
+    down_grad = transposed(activated, cot_all).astype(jnp.bfloat16)
+    gu_grad = jnp.concatenate(
+        [
+            transposed(nmlp_all, grad_gate).astype(jnp.bfloat16),
+            transposed(nmlp_all, grad_up).astype(jnp.bfloat16),
+        ],
+        axis=1,
+    )
+    downproj_grad = lax.psum_scatter(
+        down_grad, "seq", scatter_dimension=0, tiled=True
+    ).astype(jnp.float32)
+    gu_rows = lax.psum_scatter(gu_grad, "seq", scatter_dimension=0, tiled=True)
+    gu_back = lax.all_to_all(
+        gu_rows.reshape(head_count, own_rows, 2 * units),
+        "head",
+        split_axis=0,
+        concat_axis=0,
+        tiled=True,
+    )
+    gateup_grad = (
+        gu_back.reshape(head_count, own_rows, 2, seq_count, own_units)
+        .transpose(1, 2, 3, 0, 4)
+        .reshape(own_rows, 2 * device_count * own_units)
+        .astype(jnp.float32)
+    )
     norm_value, mlp_back = jax.vjp(rms_norm, hidden, gain_mlp)
     grad_hidden_n, mlpnorm_part = mlp_back(grad_nmlp)
     grad_hidden = cotangent.astype(jnp.float32) + grad_hidden_n
@@ -271,10 +322,16 @@
     grad_query = grad_query.reshape(group_rows, heads_dev * DH).astype(jnp.bfloat16)
     queryup_local = transposed(latent_all, grad_query)
     grad_latent_part = contract(grad_query, query_up)
+    received = lax.psum_scatter(
+        jnp.concatenate([grad_latent_part, key_grads, value_grads], axis=1).astype(jnp.bfloat16),
+        "head",
+        scatter_dimension=0,
+        tiled=True,
+    ).astype(jnp.float32)
     grad_latent_n, grad_keys, grad_values = (
-        lax.psum_scatter(grad_latent_part, "head", scatter_dimension=0, tiled=True),
-        lax.psum_scatter(key_grads, "head", scatter_dimension=0, tiled=True),
-        lax.psum_scatter(value_grads, "head", scatter_dimension=0, tiled=True),
+        received[:, :QR],
+        received[:, QR : QR + DH],
+        received[:, QR + DH :],
     )
     queryup_grad, outproj_turned = (
         lax.psum_scatter(
@@ -297,21 +354,20 @@
     input_value, input_back = jax.vjp(rms_norm, inputs_f, gain_attn)
     grad_input_n, attnnorm_part = input_back(grad_normed)
     input_grad = grad_hidden + grad_input_n
-    gradients = (attnnorm_part, attnin_part, latnorm_part, mlpnorm_part, gu_grad, down_grad)
-    gradients = (
-        lax.psum_scatter(gradients[0], ("seq", "head"), scatter_dimension=0, tiled=True),
-        lax.psum_scatter(gradients[1], ("seq", "head"), scatter_dimension=0, tiled=True),
-        lax.psum_scatter(gradients[2], ("seq", "head"), scatter_dimension=0, tiled=True),
-        lax.psum_scatter(gradients[3], ("seq", "head"), scatter_dimension=0, tiled=True),
-        lax.psum_scatter(gradients[4], ("seq", "head"), scatter_dimension=0, tiled=True),
-        lax.psum_scatter(gradients[5], ("seq", "head"), scatter_dimension=0, tiled=True),
-    )
-    attnnorm_grad = gradients[0]
-    attnin_grad = gradients[1]
-    latnorm_grad = gradients[2]
-    mlpnorm_grad = gradients[3]
-    gateup_grad = gradients[4]
-    downproj_grad = gradients[5]
+    latent_col = jnp.pad(
+        latnorm_part.reshape(device_count, own_latent), ((0, 0), (0, own_rows - own_latent))
+    ).reshape(device_count * own_rows)
+    gain_parts = jnp.stack([attnnorm_part, mlpnorm_part, latent_col], axis=1)
+    packed_part = jnp.concatenate(
+        [attnin_part, jnp.pad(gain_parts, ((0, 0), (0, 125)))], axis=1
+    ).astype(jnp.bfloat16)
+    packed_grad = lax.psum_scatter(
+        packed_part, ("seq", "head"), scatter_dimension=0, tiled=True
+    ).astype(jnp.float32)
+    attnin_grad = packed_grad[:, :proj_cols]
+    attnnorm_grad = packed_grad[:, proj_cols]
+    mlpnorm_grad = packed_grad[:, proj_cols + 1]
+    latnorm_grad = packed_grad[:own_latent, proj_cols + 2]
     return (
         layer_out,
         input_grad,

time: 2970 us -> 1490 us (0.50)
  waiting for transfers between devices: 2270 us -> 799 us
  blocking collectives: 121 us -> 63 us
  local copies, waits for them, and re-layouts: 221 us -> 252 us
    reduce_scatter x6 -> x5, waiting for transfers between devices: 1660 us -> 209 us  [the longest x1 68.6 us: shards(): lax.psum_scatter((contract(grad_gate, weight_gate) + contract(grad_up, we...]
    unnamed x14 -> x17, waiting for transfers between devices: 2.6 us -> 146 us
    reduce_scatter x1, waiting for transfers between devices: 126 us -> 12.8 us  [shards(): lax.psum_scatter(jnp.dot(piece, out_proj, preferred_element_type=jnp.floa...]
    all_gather x4 -> x6, waiting for transfers between devices: 410 us -> 323 us  [the longest x1 67.5 us: shards(): packed_all = lax.all_gather(packed, ('seq', 'head'), axis=0, tiled=True)]
    unnamed x2 -> x0, blocking collectives: 81.3 us -> none
    all_to_all x0 -> x1, blocking collectives: none -> 63 us  [shards(): lax.all_to_all(pieces, 'head', split_axis=0, concat_axis=0, tiled=True)]
    all_gather x2 -> x0, blocking collectives: 40 us -> none  [the longest x1 20.2 us: shards(): lax.all_gather(values_local, 'head', axis=0, tiled=True)]
    reduce_scatter x1, waiting for transfers between devices: 0.01 us -> 36.5 us  [shards(): lax.psum_scatter(outproj_local.astype(jnp.bfloat16), 'seq', scatter_dimen...]
  transfers between devices with their start and end apart: 14 -> 17, of which waited for: 12 -> 16; matrix products, arithmetic and copies ran while one was open for 5% -> 11% of each run, Pallas kernels for 0% -> 0%
where the time goes in v1:
time: 1490 us; the launch traced here: 1480 us
  waiting for transfers between devices  799 us (54%)
  local copies, waits for them, and re-layouts  252 us (17%)
  matrix products  242 us (16%)
  other arithmetic  84.4 us (6%)
  blocking collectives  63 us (4%)
  between operations  16.5 us (1%)
  loops' own time  16.2 us (1%)
    unnamed x17, waiting for transfers between devices  146 us
    dot_general x36, matrix products, contract(): lax.dot_general(left, right, (((1,), (1,)), ((), ())), preferred_element_...  106 us
    broadcast_in_dim x72, local copies, waits for them, and re-layouts, scores_of(): return jnp.where(allowed[:, None, :], raw, NEG)  93.4 us
    reduce_scatter x1, waiting for transfers between devices, shards(): lax.psum_scatter((contract(grad_gate, weight_gate) + contract(grad_up, we...  68.6 us
    all_gather x1, waiting for transfers between devices, shards(): packed_all = lax.all_gather(packed, ('seq', 'head'), axis=0, tiled=True)  67.5 us
    reduce_scatter x1, waiting for transfers between devices, shards(): lax.psum_scatter(down_part.astype(jnp.bfloat16), 'head', scatter_dimensio...  67.1 us
    all_gather x1, waiting for transfers between devices, shards(): nmlp_all = lax.all_gather(normed_mlp, 'head', axis=0, tiled=True)  66.7 us
    all_gather x1, waiting for transfers between devices, shards(): cot_all = lax.all_gather(cotangent, 'head', axis=0, tiled=True)  66.3 us
  transfers between devices with their start and end apart: 17, of which 16 were waited for; matrix products, arithmetic and copies ran while one was open for 11% of the time, Pallas kernels for 0%

profile of v1, /device:TPU:0, one launch (start us, length us, event | category | flops | bytes accessed | tf_op | source)
XLA Modules:
  0.0 1478.1 jit_solution(10932704634983574341)
XLA Ops:
  19.2 67.5 %all-gather.8.cloned.1.call-done = bf16[2048,1664]{1,0:T(8,128)(2,1)} async-done(((bf16[64,1664]{1,0:T(8,128)(2,1)}), bf16[2048,1664]{1,0:T(8,128)(2,1)}) %all-gather.8.cloned.1.call-update) | async-done | bytes 6815760 | tf_op jit(solution)/shard_map/all_gather | solution.py:93
  100.0 50.3 %all-gather.10.cloned.1.call-done = bf16[1536,1536]{1,0:T(8,128)(2,1)} async-done(((bf16[192,1536]{1,0:T(8,128)(2,1)}), bf16[1536,1536]{1,0:T(8,128)(2,1)}) %all-gather.10.cloned.1.call-update) | async-done | bytes 4718608 | tf_op jit(solution)/shard_map/all_gather | solution.py:126
  172.2 161.6 %while.87 = (s32[]{:T(128)}, bf16[3,512,512]{2,1,0:T(8,128)(2,1)}, f32[3,512,2]{2,1,0:T(8,128)}, f32[3,512,2]{2,1,0:T(8,128)}, s32[3]{0:T(128)S(1)}, /*index=5*/...) while((s32[]{:T(128)}, bf16[3,512,512]{2,1,0:T(8,128)(2,1)}, ...), condition=%wide.region_11.12_spmd, body=%wide.region_4.11_spmd.sunk | while | flops 812650496 | bytes 23047244 | solution.py:190
  177.3 11.7 while.91
  210.6 23.4 %while.91 = (s32[]{:T(128)}, f32[512,2]{1,0:T(8,128)S(1)}, f32[512,2]{1,0:T(8,128)}, s32[]{:T(128)}, s32[512]{0:T(512)S(1)}, /*index=5*/s32[1536]{0:T(1024)S(1)}...) while((s32[]{:T(128)}, f32[512,2]{1,0:T(8,128)S(1)}, ...), condition=%wide.region_8.8_spmd, body=%wide.region_5.7_spmd.sunk | while | flops 271846400 | bytes 8777971 | solution.py:175
  236.4 17.9 %while.92 = (s32[]{:T(128)}, f32[1024,256]{1,0:T(8,128)}, s32[]{:T(128)}, s32[512]{0:T(512)S(1)}, s32[1536]{0:T(1024)S(1)}, /*index=5*/s32[]{:T(128)}, bf16[1536...) while((s32[]{:T(128)}, f32[1024,256]{1,0:T(8,128)}, ...), condition=%wide.wide.region_10.10_spmd, body=%wide.wide.region_9.9_spmd.sunk | while | flops 540541952 | bytes 6841559 | solution.py:184
  264.4 35.2 %while.91 = (s32[]{:T(128)}, f32[512,2]{1,0:T(8,128)S(1)}, f32[512,2]{1,0:T(8,128)}, s32[]{:T(128)}, s32[512]{0:T(512)S(1)}, /*index=5*/s32[1536]{0:T(1024)S(1)}...) while((s32[]{:T(128)}, f32[512,2]{1,0:T(8,128)S(1)}, ...), condition=%wide.region_8.8_spmd, body=%wide.region_5.7_spmd.sunk | while | flops 271846400 | bytes 8777971 | solution.py:175
  302.0 26.8 %while.92 = (s32[]{:T(128)}, f32[1024,256]{1,0:T(8,128)}, s32[]{:T(128)}, s32[512]{0:T(512)S(1)}, s32[1536]{0:T(1024)S(1)}, /*index=5*/s32[]{:T(128)}, bf16[1536...) while((s32[]{:T(128)}, f32[1024,256]{1,0:T(8,128)}, ...), condition=%wide.wide.region_10.10_spmd, body=%wide.wide.region_9.9_spmd.sunk | while | flops 540541952 | bytes 6841559 | solution.py:184
  355.9 63.0 %all_to_all.10 = bf16[8,64,1408]{2,1,0:T(8,128)(2,1)} all-to-all(bf16[8,64,1408]{2,1,0:T(8,128)(2,1)} %reshape.546), channel_id=1, replica_groups=mesh['seq'=4,'head'=8] {'head'}, dimensions={0} | all-to-all | bytes 2883584 | tf_op jit(solution)/shard_map/all_to_all | solution.py:105
  419.0 12.8 reduce-scatter.12.cloned.1.call-done
  436.0 47.6 %all-gather.14.cloned.1.call-done = bf16[2048,1408]{1,0:T(8,128)(2,1)} async-done(((bf16[512,1408]{1,0:T(8,128)(2,1)}), bf16[2048,1408]{1,0:T(8,128)(2,1)}) %all-gather.14.cloned.1.call-update) | async-done | bytes 5767184 | tf_op jit(solution)/shard_map/all_gather | solution.py:106
  483.5 66.7 %all-gather.12.cloned.1.call-done = bf16[1536,2048]{1,0:T(8,128)(2,1)} async-done(((bf16[192,2048]{1,0:T(8,128)(2,1)}), bf16[1536,2048]{1,0:T(8,128)(2,1)}) %all-gather.12.cloned.1.call-update) | async-done | bytes 6291472 | tf_op jit(solution)/shard_map/all_gather | solution.py:201
  550.3 10.8 fusion.50
  567.9 24.4 %all-gather.16.cloned.1.call-done = bf16[704,2048]{1,0:T(8,128)(2,1)} async-done(((bf16[176,2048]{1,0:T(8,128)(2,1)}), bf16[704,2048]{1,0:T(8,128)(2,1)}) %all-gather.16.cloned.1.call-update) | async-done | bytes 2883600 | tf_op jit(solution)/shard_map/all_gather | solution.py:111
  592.3 66.3 %all-gather.18.cloned.1.call-done = bf16[1536,2048]{1,0:T(8,128)(2,1)} async-done(((bf16[192,2048]{1,0:T(8,128)(2,1)}), bf16[1536,2048]{1,0:T(8,128)(2,1)}) %all-gather.18.cloned.1.call-update) | async-done | bytes 6291472 | tf_op jit(solution)/shard_map/all_gather | solution.py:112
  658.6 13.8 multiply_convert_fusion
  681.1 11.8 add_convert_fusion
  692.9 68.6 %reduce-scatter.16.cloned.1.call-done = bf16[192,2048]{1,0:T(8,128)(2,1)} async-done(((bf16[1536,2048]{1,0:T(8,128)(2,1)}), bf16[192,2048]{1,0:T(8,128)(2,1)}) %reduce-scatter.16.cloned.1.call-update) | async-done | bytes 786448 | tf_op jit(solution)/shard_map/reduce_scatter | solution.py:213
  766.1 63.0 %all-gather.20.cloned.1.call-done = bf16[1536,2048]{1,0:T(8,128)(2,1)} async-done(((bf16[192,2048]{1,0:T(8,128)(2,1)}), bf16[1536,2048]{1,0:T(8,128)(2,1)}) %all-gather.20.cloned.1.call-update) | async-done | bytes 6291472 | tf_op jit(solution)/shard_map/all_gather | solution.py:252
  839.0 155.6 %while.90 = (s32[]{:T(128)}, f32[1536,256]{1,0:T(8,128)}, f32[1536,256]{1,0:T(8,128)}, f32[3,1024,256]{2,1,0:T(8,128)}, s32[3]{0:T(128)S(1)}, /*index=5*/bf16[15...) while((s32[]{:T(128)}, f32[1536,256]{1,0:T(8,128)}, ...), condition=%wide.region_23.24_spmd, body=%wide.region_17.23_spmd.sunk | while | flops 1888880640 | bytes 58128244 | solution.py:315
  857.9 12.1 while.94
  880.6 13.6 while.93
  897.6 24.2 %while.94 = (s32[]{:T(128)}, f32[1024,256]{1,0:T(8,128)}, f32[1536,256]{1,0:T(8,128)}, f32[1536,256]{1,0:T(8,128)}, s32[]{:T(128)}, /*index=5*/s32[512]{0:T(512)...) while((s32[]{:T(128)}, f32[1024,256]{1,0:T(8,128)}, ...), condition=%wide.wide.region_22.22_spmd, body=%wide.wide.region_21.21_spmd.sunk | while | flops 1348076544 | bytes 41185668 | solution.py:306
  932.3 20.3 %while.93 = (s32[]{:T(128)}, f32[512,2]{1,0:T(8,128)S(1)}, s32[]{:T(128)}, s32[512]{0:T(512)S(1)}, s32[1536]{0:T(1024)S(1)}, /*index=5*/s32[]{:T(128)}, bf16[153...) while((s32[]{:T(128)}, f32[512,2]{1,0:T(8,128)S(1)}, ...), condition=%wide.wide.region_20.20_spmd, body=%wide.wide.region_18.19_spmd.sunk | while | flops 540804096 | bytes 9486567 | solution.py:275
  956.1 36.2 %while.94 = (s32[]{:T(128)}, f32[1024,256]{1,0:T(8,128)}, f32[1536,256]{1,0:T(8,128)}, f32[1536,256]{1,0:T(8,128)}, s32[]{:T(128)}, /*index=5*/s32[512]{0:T(512)...) while((s32[]{:T(128)}, f32[1024,256]{1,0:T(8,128)}, ...), condition=%wide.wide.region_22.22_spmd, body=%wide.wide.region_21.21_spmd.sunk | while | flops 1348076544 | bytes 41185668 | solution.py:306
  1030.9 9.7 convolution_convert_fusion.6
  1086.8 9.8 copy.54
  1096.7 35.3 %reduce-scatter.24.cloned.1.call-done = bf16[512,1408]{0,1:T(8,128)(2,1)} async-done(((bf16[2048,1408]{0,1:T(8,128)(2,1)}), bf16[512,1408]{0,1:T(8,128)(2,1)}) %reduce-scatter.24.cloned.1.call-update) | async-done | bytes 1441808 | tf_op jit(solution)/shard_map/reduce_scatter | solution.py:234
  1139.4 37.7 %reduce-scatter.26.cloned.1.call-done = bf16[176,2048]{1,0:T(8,128)(2,1)} async-done(((bf16[704,2048]{1,0:T(8,128)(2,1)}), bf16[176,2048]{1,0:T(8,128)(2,1)}) %reduce-scatter.26.cloned.1.call-update) | async-done | bytes 720912 | tf_op jit(solution)/shard_map/reduce_scatter | solution.py:231
  1209.9 36.5 %reduce-scatter.22.cloned.1.call-done = bf16[512,512]{1,0:T(8,128)(2,1)} async-done(((bf16[2048,512]{1,0:T(8,128)(2,1)}), bf16[512,512]{1,0:T(8,128)(2,1)}) %reduce-scatter.22.cloned.1.call-update) | async-done | bytes 524304 | tf_op jit(solution)/shard_map/reduce_scatter | solution.py:340
  1251.2 67.1 %reduce-scatter.14.cloned.1.call-done = bf16[192,2048]{1,0:T(8,128)(2,1)} async-done(((bf16[1536,2048]{1,0:T(8,128)(2,1)}), bf16[192,2048]{1,0:T(8,128)(2,1)}) %reduce-scatter.14.cloned.1.call-update) | async-done | bytes 786448 | tf_op jit(solution)/shard_map/reduce_scatter | solution.py:219
  1322.7 144.3 %reduce-scatter.28.cloned.1.call-done = bf16[64,1664]{1,0:T(8,128)(2,1)} async-done(((bf16[2048,1664]{1,0:T(8,128)(2,1)}), bf16[64,1664]{1,0:T(8,128)(2,1)}) %reduce-scatter.28.cloned.1.call-update) | async-done | bytes 213008
  (674 shorter events, 554.3 us)
Async XLA Ops:
  8.0 325.8 %copy-start = (bf16[512,2048]{1,0:T(8,128)(2,1)S(1)}, bf16[512,2048]{1,0:T(8,128)(2,1)}, u32[]{:S(2)}) copy-start(bf16[512,2048]{1,0:T(8,128)(2,1)} %param.30) | copy-start | bytes 6291460
  8.0 78.7 %all-gather.8.cloned.1.call-start = ((), (), s32[]{:S(2)}) async-start(), calls=%async_computation.11 | async-start | bytes 7028736 | tf_op jit(solution)/shard_map/all_gather | solution.py:93
  9.7 79.5 %copy-start.15 = (bf16[192,2048]{1,0:T(8,128)(2,1)S(1)}, bf16[192,2048]{1,0:T(8,128)(2,1)}, u32[]{:S(2)}) copy-start(bf16[192,2048]{1,0:T(8,128)(2,1)} %param.23) | copy-start | bytes 2359300
  11.4 138.8 %all-gather.10.cloned.1.call-start = ((), (), s32[]{:S(2)}) async-start(), calls=%async_computation.12 | async-start | bytes 5308416 | tf_op jit(solution)/shard_map/all_gather | solution.py:126
  14.3 79.0 %copy-start.40 = (f32[192]{0:T(256)}, f32[192]{0:T(256)S(1)}, u32[]{:S(2)}) copy-start(f32[192]{0:T(256)S(1)} %fusion.86) | copy-start | bytes 2308
  95.0 59.3 %copy-start.43 = (f32[192]{0:T(256)}, f32[192]{0:T(256)S(1)}, u32[]{:S(2)}) copy-start(f32[192]{0:T(256)S(1)} %fusion.87) | copy-start | bytes 2308
  96.6 57.7 %copy-start.35 = (f32[1024]{0:T(1024)}, f32[1024]{0:T(1024)S(1)}, u32[]{:S(2)}) copy-start(f32[1024]{0:T(1024)S(1)} %reshape.552) | copy-start | bytes 12292
  99.9 331.9 %reduce-scatter.12.cloned.1.call-start = ((), (), s32[]{:S(2)}) async-start(), calls=%async_computation.13 | async-start | bytes 7077888 | tf_op jit(solution)/shard_map/reduce_scatter | solution.py:193
  340.5 143.0 %all-gather.14.cloned.1.call-start = ((), (), s32[]{:S(2)}) async-start(), calls=%async_computation.15 | async-start | bytes 7208960 | tf_op jit(solution)/shard_map/all_gather | solution.py:106
  355.9 75.9 %copy-start.16 = (bf16[192,2048]{1,0:T(8,128)(2,1)S(1)}, bf16[192,2048]{1,0:T(8,128)(2,1)}, u32[]{:S(2)}) copy-start(bf16[192,2048]{1,0:T(8,128)(2,1)} %param.23) | copy-start | bytes 2359300
  418.9 14.5 copy-start.31
  418.9 131.3 %all-gather.12.cloned.1.call-start = ((), (), s32[]{:S(2)}) async-start(), calls=%async_computation.14 | async-start | bytes 7077888 | tf_op jit(solution)/shard_map/all_gather | solution.py:201
  433.3 331.0 %copy-start.38 = (f32[192]{0:T(256)}, f32[192]{0:T(256)S(1)}, u32[]{:S(2)}) copy-start(f32[192]{0:T(256)S(1)} %fusion.88) | copy-start | bytes 2308
  434.6 157.7 %all-gather.16.cloned.1.call-start = ((), (), s32[]{:S(2)}) async-start(), calls=%async_computation.16 | async-start | bytes 3604480 | tf_op jit(solution)/shard_map/all_gather | solution.py:111
  435.2 223.4 %all-gather.18.cloned.1.call-start = ((), (), s32[]{:S(2)}) async-start(), calls=%async_computation.18 | async-start | bytes 7077888 | tf_op jit(solution)/shard_map/all_gather | solution.py:112
  435.9 325.6 %reduce-scatter.16.cloned.1.call-start = ((), (), s32[]{:S(2)}) async-start(), calls=%async_computation.19 | async-start | bytes 7077888 | tf_op jit(solution)/shard_map/reduce_scatter | solution.py:213
  550.3 10.8 copy-start.52
  692.9 136.3 %all-gather.20.cloned.1.call-start = ((), (), s32[]{:S(2)}) async-start(), calls=%async_computation.20 | async-start | bytes 7077888 | tf_op jit(solution)/shard_map/all_gather | solution.py:252
  766.1 298.9 %reduce-scatter.18.cloned.1.call-start = ((), (), s32[]{:S(2)}) async-start(), calls=%async_computation.21 | async-start | bytes 5308416 | tf_op jit(solution)/shard_map/reduce_scatter | solution.py:325
  1011.4 120.5 %reduce-scatter.24.cloned.1.call-start = ((), (), s32[]{:S(2)}) async-start(), calls=%async_computation.24 | async-start | bytes 7208960 | tf_op jit(solution)/shard_map/reduce_scatter | solution.py:234
  1030.8 146.2 %reduce-scatter.26.cloned.1.call-start = ((), (), s32[]{:S(2)}) async-start(), calls=%async_computation.25 | async-start | bytes 3604480 | tf_op jit(solution)/shard_map/reduce_scatter | solution.py:231
  1040.7 167.5 %reduce-scatter.20.cloned.1.call-start = ((), (), s32[]{:S(2)}) async-start(), calls=%async_computation.22 | async-start | bytes 1310720 | tf_op jit(solution)/shard_map/reduce_scatter | solution.py:337
  1046.8 199.6 %reduce-scatter.22.cloned.1.call-start = ((), (), s32[]{:S(2)}) async-start(), calls=%async_computation.23 | async-start | bytes 2621440 | tf_op jit(solution)/shard_map/reduce_scatter | solution.py:340
  1055.0 263.2 %reduce-scatter.14.cloned.1.call-start = ((), (), s32[]{:S(2)}) async-start(), calls=%async_computation.17 | async-start | bytes 7077888 | tf_op jit(solution)/shard_map/reduce_scatter | solution.py:219
  1064.3 402.8 %reduce-scatter.28.cloned.1.call-start = ((), (), s32[]{:S(2)}) async-start(), calls=%async_computation.26 | async-start | bytes 7028736
  1134.5 44.9 %all-to-all-start.1 = ((bf16[8,64,1408]{2,1,0:T(8,128)(2,1)}), bf16[8,64,1408]{2,1,0:T(8,128)(2,1)S(1)}, u32[]{:S(2)}, u32[]{:S(2)}) async-start(bf16[8,64,1408]{2,1,0:T(8,128)(2,1)} %bitcast.25), calls=%async_computation.8 | async-start | bytes 2883584 | tf_op jit(solution)/shard_map/all_to_all | solution.py:235
  1199.1 52.1 %copy-start.48 = (f32[192]{0:T(256)S(1)}, f32[192]{0:T(256)}, u32[]{:S(2)}) copy-start(f32[192]{0:T(256)} %copy-done.47) | copy-start | bytes 2308
  1199.1 119.2 %copy-start.20 = (bf16[192,2048]{1,0:T(8,128)(2,1)S(1)}, bf16[192,2048]{1,0:T(8,128)(2,1)}, u32[]{:S(2)}) copy-start(bf16[192,2048]{1,0:T(8,128)(2,1)} %reduce-scatter.12.cloned.1.call-done) | copy-start | bytes 2359300
  1199.1 119.2 %copy-start.27 = (bf16[192,2048]{1,0:T(8,128)(2,1)S(1)}, bf16[192,2048]{1,0:T(8,128)(2,1)}, u32[]{:S(2)}) copy-start(bf16[192,2048]{1,0:T(8,128)(2,1)} %param.25) | copy-start | bytes 2359300
  1199.1 119.2 %copy-start.32 = (f32[2048]{0:T(1024)S(1)}, f32[2048]{0:T(1024)}, u32[]{:S(2)}) copy-start(f32[2048]{0:T(1024)} %get-tuple-element.707) | copy-start | bytes 24580
  1199.1 119.2 %copy-start.39 = (f32[192]{0:T(256)S(1)}, f32[192]{0:T(256)}, u32[]{:S(2)}) copy-start(f32[192]{0:T(256)} %copy-done.38) | copy-start | bytes 2308
  1199.1 119.2 %copy-start.46 = (f32[192]{0:T(256)S(1)}, f32[192]{0:T(256)}, u32[]{:S(2)}) copy-start(f32[192]{0:T(256)} %copy-done.45) | copy-start | bytes 2308
  (84 other events, 222.1 us)
Sparse Core Ops, SparseCore 0:
  12.3 74.3 all-gather.7
  100.0 50.2 all-gather.9
  340.7 91.0 reduce-scatter.11
  693.0 68.4 reduce-scatter.15
Sparse Core Ops, SparseCore 1:
  419.0 64.5 all-gather.13
  485.6 64.6 all-gather.11
  552.0 40.3 all-gather.15
  594.0 64.6 all-gather.17
  766.2 62.9 all-gather.19
  1011.5 53.4 reduce-scatter.17
  1067.8 64.1 reduce-scatter.23
  1135.5 41.6 reduce-scatter.25
  1180.4 27.7 reduce-scatter.19
  1211.4 35.0 reduce-scatter.21
  1248.6 69.6 reduce-scatter.13
  1320.6 146.3 reduce-scatter.27

commit v2 on v1

v2 whole, which is shorter than its diff:
```python
import functools

import jax
import jax.numpy as jnp
from jax import lax
from jax.experimental import pallas as pl
from jax.experimental.pallas import tpu as pltpu
from jax.sharding import PartitionSpec as P

DH = 256
QR = 1024
HALF = DH // 2


EPS = 1e-06
THETA = 10000.0
NEG = -1e30


def contract(left, right):
    return lax.dot_general(
        left, right, (((1,), (1,)), ((), ())), preferred_element_type=jnp.float32
    )


def transposed(left, right):
    return lax.dot_general(
        left, right, (((0,), (0,)), ((), ())), preferred_element_type=jnp.float32
    )


def matmul(left, right):
    return jnp.dot(left, right, preferred_element_type=jnp.float32)


def rms_norm(values_in, gain_vec):
    return (
        values_in
        * lax.rsqrt(jnp.mean(values_in * values_in, axis=-1, keepdims=True) + EPS)
        * gain_vec
    )


def rotary(values_in, cosine, sine):
    half_dim = values_in.shape[-1] // 2
    first_half = values_in[..., :half_dim]
    second_half = values_in[..., half_dim:]
    return jnp.concatenate(
        [first_half * cosine - second_half * sine, second_half * cosine + first_half * sine],
        axis=-1,
    )


def segment_starts(segment_row):
    index = jnp.arange(segment_row.shape[0], dtype=jnp.int32)
    opens = jnp.concatenate([jnp.ones((1,), jnp.bool_), segment_row[1:] != segment_row[:-1]])
    return lax.cummax(jnp.where(opens, index, jnp.zeros_like(index)), axis=0)


def angles(starts):
    index = jnp.arange(starts.shape[0], dtype=jnp.int32)
    places = (index - starts).astype(jnp.float32)
    exponent = jnp.arange(DH // 2, dtype=jnp.float32) * (-2.0 / DH)
    frequency = jnp.power(jnp.float32(THETA), exponent)
    turned = places[:, None] * frequency[None, :]
    return (jnp.cos(turned), jnp.sin(turned))


def stacked(values_in, heads):
    return jnp.concatenate([values_in[:, h * DH : (h + 1) * DH] for h in range(heads)], axis=0)


def side_by_side(values_in, heads):
    rows = values_in.shape[0] // heads
    return jnp.concatenate([values_in[h * rows : (h + 1) * rows] for h in range(heads)], axis=1)


def block_mask(starts, query_row, key_row, heads, rows, cols):
    place_query = query_row + lax.broadcasted_iota(jnp.int32, (rows, cols), 0)
    place_key = key_row + lax.broadcasted_iota(jnp.int32, (rows, cols), 1)
    allowed = (place_key >= starts) & (place_key <= place_query)
    return jnp.concatenate([allowed] * heads, axis=0) if heads > 1 else allowed


def forward_kernel(
    heads,
    block,
    first_ref,
    joined_ref,
    starts_ref,
    cos_ref,
    sin_ref,
    queryup_ref,
    outproj_ref,
    part_ref,
    query_ref,
    mixed_ref,
    stats_ref,
    top_ref,
    total_ref,
    accum_ref,
):
    qblock = pl.program_id(0)
    query_row = pl.multiple_of(qblock * block, block)
    cosine = cos_ref[...]
    sine = sin_ref[...]
    raw = matmul(joined_ref[pl.ds(query_row, block), :QR], queryup_ref[...])
    turned = []
    for h in range(heads):
        one = raw[:, h * DH : h * DH + HALF]
        two = raw[:, h * DH + HALF : (h + 1) * DH]
        turned += [one * cosine - two * sine, two * cosine + one * sine]
    queries = (jnp.concatenate(turned, axis=1)).astype(jnp.bfloat16) * jnp.bfloat16(DH**-0.5)
    query_ref[...] = queries
    rows = stacked(queries, heads)
    starts = starts_ref[...]
    top_ref[...] = jnp.full_like(top_ref, NEG)
    total_ref[...] = jnp.zeros_like(total_ref)
    accum_ref[...] = jnp.zeros_like(accum_ref)

    def key_step(kblock, carry):
        key_row = pl.multiple_of(kblock * block, block)
        keys = joined_ref[pl.ds(key_row, block), QR : QR + DH]
        values = joined_ref[pl.ds(key_row, block), QR + DH :]
        scores = contract(rows, keys)
        allowed = block_mask(starts, query_row, key_row, heads, block, block)
        scores = jnp.where(allowed, scores, NEG)
        old_top = top_ref[...]
        new_top = jnp.maximum(old_top, jnp.max(scores, axis=1, keepdims=True))
        weights = jnp.exp(scores - new_top)
        shrink = jnp.exp(old_top - new_top)
        top_ref[...] = new_top
        total_ref[...] = total_ref[...] * shrink + jnp.sum(weights, axis=1, keepdims=True)
        accum_ref[...] = accum_ref[...] * shrink + matmul(weights.astype(jnp.bfloat16), values)
        return carry

    lax.fori_loop(first_ref[qblock], qblock + 1, key_step, 0)
    total = total_ref[...]
    mixed = side_by_side((accum_ref[...] / total).astype(jnp.bfloat16), heads)
    mixed_ref[...] = mixed
    stats_ref[...] = jnp.broadcast_to(top_ref[...] + jnp.log(total), (heads * block, 128))
    part_ref[...] = matmul(mixed, outproj_ref[...]).astype(jnp.bfloat16)


def attention_forward(joined, starts, cosine, sine, query_up, out_proj, first_keys, block):
    group, width = joined.shape
    heads = query_up.shape[1] // DH
    model = out_proj.shape[1]
    count = group // block

    def whole(shape):
        return pl.BlockSpec(shape, lambda i, first: (0, 0), pipeline_mode=pl.Buffered(1))

    def rowed(cols, rows=block):
        return pl.BlockSpec((rows, cols), lambda i, first: (i, 0))

    pairs = group * group * heads // 4
    return pl.pallas_call(
        functools.partial(forward_kernel, heads, block),
        grid_spec=pltpu.PrefetchScalarGridSpec(
            num_scalar_prefetch=1,
            grid=(count,),
            in_specs=[
                whole((group, width)),
                rowed(1),
                rowed(HALF),
                rowed(HALF),
                whole(query_up.shape),
                whole(out_proj.shape),
            ],
            out_specs=[
                rowed(model),
                rowed(heads * DH),
                rowed(heads * DH),
                rowed(128, heads * block),
            ],
            scratch_shapes=[
                pltpu.VMEM((heads * block, 1), jnp.float32),
                pltpu.VMEM((heads * block, 1), jnp.float32),
                pltpu.VMEM((heads * block, DH), jnp.float32),
            ],
        ),
        out_shape=[
            jax.ShapeDtypeStruct((group, model), jnp.bfloat16),
            jax.ShapeDtypeStruct((group, heads * DH), jnp.bfloat16),
            jax.ShapeDtypeStruct((group, heads * DH), jnp.bfloat16),
            jax.ShapeDtypeStruct((group * heads, 128), jnp.float32),
        ],
        compiler_params=pltpu.CompilerParams(
            dimension_semantics=("arbitrary",), vmem_limit_bytes=48 * 1024 * 1024
        ),
        cost_estimate=pl.CostEstimate(
            flops=2 * group * heads * DH * (QR + model) + 4 * pairs * DH,
            transcendentals=pairs,
            bytes_accessed=2 * (joined.size + query_up.size + out_proj.size)
            + 2 * group * (model + 2 * heads * DH)
            + 4 * group * heads * 128
            + 8 * group * HALF,
        ),
        name="attention_forward",
    )(first_keys, joined, starts, cosine, sine, query_up, out_proj)


def backward_kernel(
    heads,
    block,
    first_ref,
    joined_ref,
    starts_ref,
    cos_ref,
    sin_ref,
    queryup_ref,
    outproj_ref,
    query_ref,
    mixed_ref,
    stats_ref,
    grad_ref,
    part_ref,
    gradq_ref,
    keyacc_ref,
    valueacc_ref,
    accum_ref,
):
    qblock = pl.program_id(0)
    query_row = pl.multiple_of(qblock * block, block)

    @pl.when(qblock == 0)
    def _():
        keyacc_ref[...] = jnp.zeros_like(keyacc_ref)
        valueacc_ref[...] = jnp.zeros_like(valueacc_ref)

    grad_mixed = contract(grad_ref[...], outproj_ref[...]).astype(jnp.bfloat16)
    products = grad_mixed.astype(jnp.float32) * mixed_ref[...].astype(jnp.float32)
    dots = jnp.sum(stacked(products, heads), axis=1, keepdims=True)
    grads = stacked(grad_mixed, heads)
    rows = stacked(query_ref[...], heads)
    level = stats_ref[:, 0:1]
    starts = starts_ref[...]
    accum_ref[...] = jnp.zeros_like(accum_ref)

    def key_step(kblock, carry):
        key_row = pl.multiple_of(kblock * block, block)
        keys = joined_ref[pl.ds(key_row, block), QR : QR + DH]
        values = joined_ref[pl.ds(key_row, block), QR + DH :]
        scores = contract(rows, keys)
        allowed = block_mask(starts, query_row, key_row, heads, block, block)
        weights = jnp.exp(jnp.where(allowed, scores, NEG) - level)
        grad_weights = contract(grads, values)
        grad_scores = (weights * (grad_weights - dots)).astype(jnp.bfloat16)
        accum_ref[...] += matmul(grad_scores, keys)
        keyacc_ref[pl.ds(key_row, block), :] += transposed(grad_scores, rows)
        valueacc_ref[pl.ds(key_row, block), :] += transposed(weights.astype(jnp.bfloat16), grads)
        return carry

    lax.fori_loop(first_ref[qblock], qblock + 1, key_step, 0)
    cosine = cos_ref[...]
    sine = sin_ref[...]
    grad_turned = side_by_side(accum_ref[...] * DH**-0.5, heads)
    back = []
    for h in range(heads):
        one = grad_turned[:, h * DH : h * DH + HALF]
        two = grad_turned[:, h * DH + HALF : (h + 1) * DH]
        back += [one * cosine + two * sine, two * cosine - one * sine]
    grad_query = jnp.concatenate(back, axis=1).astype(jnp.bfloat16)
    gradq_ref[...] = grad_query
    part_ref[pl.ds(query_row, block), :QR] = contract(grad_query, queryup_ref[...]).astype(
        jnp.bfloat16
    )

    @pl.when(qblock == pl.num_programs(0) - 1)
    def _():
        part_ref[:, QR : QR + DH] = keyacc_ref[...].astype(jnp.bfloat16)
        part_ref[:, QR + DH :] = valueacc_ref[...].astype(jnp.bfloat16)


def attention_backward(
    joined, starts, cosine, sine, query_up, out_proj, queries, mixed, stats, grads, first_keys, block
):
    group, width = joined.shape
    heads = query_up.shape[1] // DH
    model = out_proj.shape[1]
    count = group // block

    def whole(shape):
        return pl.BlockSpec(shape, lambda i, first: (0, 0), pipeline_mode=pl.Buffered(1))

    def rowed(cols, rows=block):
        return pl.BlockSpec((rows, cols), lambda i, first: (i, 0))

    pairs = group * group * heads // 4
    return pl.pallas_call(
        functools.partial(backward_kernel, heads, block),
        grid_spec=pltpu.PrefetchScalarGridSpec(
            num_scalar_prefetch=1,
            grid=(count,),
            in_specs=[
                whole((group, width)),
                rowed(1),
                rowed(HALF),
                rowed(HALF),
                whole(query_up.shape),
                whole(out_proj.shape),
                rowed(heads * DH),
                rowed(heads * DH),
                rowed(128, heads * block),
                rowed(model),
            ],
            out_specs=[
                pl.BlockSpec((group, width), lambda i, first: (0, 0)),
                rowed(heads * DH),
            ],
            scratch_shapes=[
                pltpu.VMEM((group, DH), jnp.float32),
                pltpu.VMEM((group, DH), jnp.float32),
                pltpu.VMEM((heads * block, DH), jnp.float32),
            ],
        ),
        out_shape=[
            jax.ShapeDtypeStruct((group, width), jnp.bfloat16),
            jax.ShapeDtypeStruct((group, heads * DH), jnp.bfloat16),
        ],
        compiler_params=pltpu.CompilerParams(
            dimension_semantics=("arbitrary",), vmem_limit_bytes=56 * 1024 * 1024
        ),
        cost_estimate=pl.CostEstimate(
            flops=2 * group * heads * DH * (QR + model) + 10 * pairs * DH,
            transcendentals=pairs,
            bytes_accessed=2 * (2 * joined.size + query_up.size + out_proj.size)
            + 2 * group * (model + 3 * heads * DH)
            + 4 * group * heads * 128
            + 8 * group * HALF,
        ),
        name="attention_backward",
    )(
        first_keys,
        joined,
        starts,
        cosine,
        sine,
        query_up,
        out_proj,
        queries,
        mixed,
        stats,
        grads,
    )


def tie(value, *others):
    return lax.optimization_barrier((value,) + others)[0]


def exchange(pieces, place, count):
    arrived = [lax.dynamic_index_in_dim(pieces, place, 0, keepdims=False)]
    for shift in range(1, count):
        sent = lax.dynamic_index_in_dim(
            pieces, lax.rem(place + shift, count), 0, keepdims=False
        )
        route = [(i, (i + shift) % count) for i in range(count)]
        arrived.append(lax.ppermute(sent, "head", route))
    stack = jnp.stack(arrived)
    order = lax.rem(place - jnp.arange(count, dtype=jnp.int32) + count, count)
    return jnp.stack(
        [lax.dynamic_index_in_dim(stack, order[i], 0, keepdims=False) for i in range(count)]
    )


def feed_kernel(
    normed_ref, cot_ref, gu_ref, down_ref, nmlp_ref, out_ref, act_ref, ggate_ref, gup_ref
):
    pieces, _, depth, _ = gu_ref.shape
    normed = normed_ref[...]
    gate = matmul(normed[:, :depth], gu_ref[0, 0])
    up = matmul(normed[:, :depth], gu_ref[0, 1])
    for s in range(1, pieces):
        part = normed[:, s * depth : (s + 1) * depth]
        gate += matmul(part, gu_ref[s, 0])
        up += matmul(part, gu_ref[s, 1])
    grad_act = contract(cot_ref[...], down_ref[...])
    sigmoid = 1.0 / (1.0 + jnp.exp(-gate))
    silu = gate * sigmoid
    activated = (silu * up).astype(jnp.bfloat16)
    act_ref[...] = activated
    grad_gate = (grad_act * up * (sigmoid * (1.0 + gate * (1.0 - sigmoid)))).astype(jnp.bfloat16)
    grad_up = (grad_act * silu).astype(jnp.bfloat16)
    ggate_ref[...] = grad_gate
    gup_ref[...] = grad_up
    for s in range(pieces):
        back = contract(grad_gate, gu_ref[s, 0]) + contract(grad_up, gu_ref[s, 1])
        nmlp_ref[:, s * depth : (s + 1) * depth] = back.astype(jnp.bfloat16)
    out_ref[...] = matmul(activated, down_ref[...]).astype(jnp.bfloat16)


def feed_forward(normed, cot, weight_gu, weight_down, block):
    group, model = normed.shape
    units = weight_down.shape[0]

    def rowed(cols):
        return pl.BlockSpec((block, cols), lambda i: (i, 0))

    return pl.pallas_call(
        feed_kernel,
        grid=(group // block,),
        in_specs=[
            rowed(model),
            rowed(model),
            pl.BlockSpec(weight_gu.shape, lambda i: (0, 0, 0, 0), pipeline_mode=pl.Buffered(1)),
            pl.BlockSpec(weight_down.shape, lambda i: (0, 0), pipeline_mode=pl.Buffered(1)),
        ],
        out_specs=[rowed(model), rowed(model), rowed(units), rowed(units), rowed(units)],
        out_shape=[
            jax.ShapeDtypeStruct((group, model), jnp.bfloat16),
            jax.ShapeDtypeStruct((group, model), jnp.bfloat16),
            jax.ShapeDtypeStruct((group, units), jnp.bfloat16),
            jax.ShapeDtypeStruct((group, units), jnp.bfloat16),
            jax.ShapeDtypeStruct((group, units), jnp.bfloat16),
        ],
        compiler_params=pltpu.CompilerParams(
            dimension_semantics=("arbitrary",), vmem_limit_bytes=56 * 1024 * 1024
        ),
        cost_estimate=pl.CostEstimate(
            flops=12 * group * model * units,
            transcendentals=group * units,
            bytes_accessed=2 * (4 * group * model + 3 * group * units + 3 * model * units),
        ),
        name="feed_forward",
    )(normed, cot, weight_gu, weight_down)


def weights_kernel(left_ref, right_ref, out_ref):
    product = transposed(left_ref[...], right_ref[...])
    out_ref[...] = product.astype(jnp.bfloat16).reshape(out_ref.shape)


def weight_product(left, right, rows, cols, out_shape, out_block, out_map, height=None):
    tokens = left.shape[0]
    height = height or left.shape[1]
    width = right.shape[1]
    return pl.pallas_call(
        weights_kernel,
        grid=(height // rows, width // cols),
        in_specs=[
            pl.BlockSpec((tokens, rows), lambda i, j: (0, i)),
            pl.BlockSpec((tokens, cols), lambda i, j: (0, j)),
        ],
        out_specs=pl.BlockSpec(out_block, out_map),
        out_shape=jax.ShapeDtypeStruct(out_shape, jnp.bfloat16),
        compiler_params=pltpu.CompilerParams(
            dimension_semantics=("arbitrary", "arbitrary"), vmem_limit_bytes=40 * 1024 * 1024
        ),
        cost_estimate=pl.CostEstimate(
            flops=2 * tokens * height * width,
            transcendentals=0,
            bytes_accessed=2 * (tokens * (height + width) + height * width),
        ),
        name="weight_product",
    )(left, right)


def packed_kernel(left_ref, right_ref, gains_ref, out_ref):
    cols = right_ref.shape[1]
    out_ref[:, :cols] = transposed(left_ref[...], right_ref[...]).astype(jnp.bfloat16)
    out_ref[:, cols:] = gains_ref[...]


def packed_product(left, right, gains, rows):
    tokens, model = left.shape
    cols = right.shape[1]
    width = cols + gains.shape[1]
    return pl.pallas_call(
        packed_kernel,
        grid=(model // rows,),
        in_specs=[
            pl.BlockSpec((tokens, rows), lambda i: (0, i)),
            pl.BlockSpec((tokens, cols), lambda i: (0, 0)),
            pl.BlockSpec((rows, gains.shape[1]), lambda i: (i, 0)),
        ],
        out_specs=pl.BlockSpec((rows, width), lambda i: (i, 0)),
        out_shape=jax.ShapeDtypeStruct((model, width), jnp.bfloat16),
        compiler_params=pltpu.CompilerParams(
            dimension_semantics=("arbitrary",), vmem_limit_bytes=32 * 1024 * 1024
        ),
        cost_estimate=pl.CostEstimate(
            flops=2 * tokens * model * cols,
            transcendentals=0,
            bytes_accessed=2 * (left.size + right.size + model * width),
        ),
        name="packed_product",
    )(left, right, gains)


def gu_kernel(left_ref, gate_ref, up_ref, out_ref):
    left = left_ref[...]
    out_ref[0, 0] = transposed(left, gate_ref[...]).astype(jnp.bfloat16)
    out_ref[0, 1] = transposed(left, up_ref[...]).astype(jnp.bfloat16)


def gu_product(normed, grad_gate, grad_up, pieces, split):
    tokens, model = normed.shape
    units = grad_gate.shape[1]
    depth = model // pieces
    rows = depth // split
    return pl.pallas_call(
        gu_kernel,
        grid=(pieces, split),
        in_specs=[
            pl.BlockSpec((tokens, rows), lambda s, i: (0, s * split + i)),
            pl.BlockSpec((tokens, units), lambda s, i: (0, 0), pipeline_mode=pl.Buffered(1)),
            pl.BlockSpec((tokens, units), lambda s, i: (0, 0), pipeline_mode=pl.Buffered(1)),
        ],
        out_specs=pl.BlockSpec((1, 2, rows, units), lambda s, i: (s, 0, i, 0)),
        out_shape=jax.ShapeDtypeStruct((pieces, 2, depth, units), jnp.bfloat16),
        compiler_params=pltpu.CompilerParams(
            dimension_semantics=("arbitrary", "arbitrary"), vmem_limit_bytes=40 * 1024 * 1024
        ),
        cost_estimate=pl.CostEstimate(
            flops=4 * tokens * model * units,
            transcendentals=0,
            bytes_accessed=2 * (normed.size + 2 * grad_gate.size + 2 * model * units),
        ),
        name="gu_product",
    )(normed, grad_gate, grad_up)


def shards(
    inputs,
    segments,
    cotangent,
    norm_attn,
    attn_in,
    norm_latent,
    query_up,
    out_proj,
    norm_mlp,
    gate_up,
    down_proj,
):
    head_count = lax.axis_size("head")
    head_place = lax.axis_index("head")
    shard_rows, model = inputs.shape
    group_rows = shard_rows * head_count
    block_rows = min(512, group_rows)
    seq_count = lax.axis_size("seq")
    own_rows = attn_in.shape[0]
    own_latent = norm_latent.shape[0]
    own_units = down_proj.shape[0]
    units = seq_count * own_units
    device_count = seq_count * head_count
    proj_cols = attn_in.shape[1]
    gain_cols = jnp.stack(
        [norm_attn, norm_mlp, jnp.pad(norm_latent, (0, own_rows - own_latent))], axis=1
    )
    packed = jnp.concatenate([attn_in, jnp.pad(gain_cols, ((0, 0), (0, 125)))], axis=1)
    packed_all = lax.all_gather(packed, ("seq", "head"), axis=0, tiled=True)
    pieces = gate_up.reshape(own_rows, 2, seq_count, head_count, own_units)
    pieces = pieces.transpose(3, 1, 0, 2, 4).reshape(head_count, 2, own_rows, units)
    turned = exchange(pieces, head_place, head_count)
    turned = turned.transpose(1, 0, 2, 3).reshape(1, 2, head_count * own_rows, units)
    weight_gu = lax.all_gather(turned, "seq", axis=0, tiled=True)
    weight_down = lax.all_gather(down_proj, "seq", axis=0, tiled=True)
    cot_all = lax.all_gather(cotangent, "head", axis=0, tiled=True)
    packed_all = tie(packed_all, cot_all, turned)
    weight_in = packed_all[:, :proj_cols]
    gain_attn = packed_all[:, proj_cols].astype(jnp.float32)
    gain_mlp = packed_all[:, proj_cols + 1].astype(jnp.float32)
    gain_latent = (
        packed_all[:, proj_cols + 2]
        .reshape(device_count, own_rows)[:, :own_latent]
        .reshape(device_count * own_latent)
        .astype(jnp.float32)
    )
    starts = segment_starts(segments[0])
    first_keys = starts[::block_rows] // block_rows
    cosine, sine = angles(starts)
    row_start = head_place * shard_rows
    cos_local = lax.dynamic_slice_in_dim(cosine, row_start, shard_rows, 0)
    sin_local = lax.dynamic_slice_in_dim(sine, row_start, shard_rows, 0)
    inputs_f = inputs.astype(jnp.float32)
    normed = rms_norm(inputs_f, gain_attn).astype(jnp.bfloat16)
    projected = jnp.dot(normed, weight_in, preferred_element_type=jnp.float32)
    latent = projected[:, :QR]
    key_raw = projected[:, QR : QR + DH]
    latent_n = rms_norm(latent, gain_latent).astype(jnp.bfloat16)
    keys_local = rotary(key_raw, cos_local, sin_local).astype(jnp.bfloat16)
    values_local = projected[:, QR + DH :].astype(jnp.bfloat16)
    joined_all = lax.all_gather(
        jnp.concatenate([latent_n, keys_local, values_local], axis=1), "head", axis=0, tiled=True
    )
    joined_all = tie(joined_all, weight_gu, weight_down)
    attn_part, queries, mixed, stats = attention_forward(
        joined_all, starts[:, None], cosine, sine, query_up, out_proj, first_keys, block_rows
    )
    attn_out = lax.psum_scatter(
        attn_part,
        "head",
        scatter_dimension=0,
        tiled=True,
    ).astype(jnp.float32)
    hidden = inputs_f + attn_out
    normed_mlp = rms_norm(hidden, gain_mlp).astype(jnp.bfloat16)
    nmlp_all = lax.all_gather(normed_mlp, "head", axis=0, tiled=True)
    nmlp_part, down_part, activated, grad_gate, grad_up = feed_forward(
        nmlp_all, cot_all, weight_gu, weight_down, 256
    )
    grad_nmlp = lax.psum_scatter(nmlp_part, "head", scatter_dimension=0, tiled=True)
    gu_part = gu_product(nmlp_all, grad_gate, grad_up, seq_count, 2)
    down_grad = weight_product(
        activated,
        cot_all,
        units,
        512,
        (seq_count, own_units, model),
        (seq_count, own_units, 512),
        lambda i, j: (0, 0, j),
    )
    grad_nmlp = tie(grad_nmlp, gu_part, down_grad).astype(jnp.float32)
    down_out = lax.psum_scatter(down_part, "head", scatter_dimension=0, tiled=True)
    gu_rows = lax.psum_scatter(gu_part, "seq", scatter_dimension=0, tiled=True)
    down_rows = lax.psum_scatter(down_grad, "seq", scatter_dimension=0, tiled=True)
    norm_value, mlp_back = jax.vjp(rms_norm, hidden, gain_mlp)
    grad_hidden_n, mlpnorm_part = mlp_back(grad_nmlp)
    grad_hidden = cotangent.astype(jnp.float32) + grad_hidden_n
    grad_attn = grad_hidden.astype(jnp.bfloat16)
    grad_attn_all = lax.all_gather(grad_attn, "head", axis=0, tiled=True)
    grad_part, grad_query = attention_backward(
        joined_all,
        starts[:, None],
        cosine,
        sine,
        query_up,
        out_proj,
        queries,
        mixed,
        stats,
        grad_attn_all,
        first_keys,
        block_rows,
    )
    received = lax.psum_scatter(grad_part, "head", scatter_dimension=0, tiled=True)
    head_cols = query_up.shape[1]
    queryup_part = weight_product(
        joined_all,
        grad_query,
        QR // seq_count,
        head_cols,
        (seq_count, QR // seq_count, head_cols),
        (1, QR // seq_count, head_cols),
        lambda i, j: (i, 0, 0),
        height=QR,
    )
    outproj_part = weight_product(
        mixed,
        grad_attn_all,
        head_cols,
        model // seq_count,
        (seq_count, head_cols, model // seq_count),
        (1, head_cols, model // seq_count),
        lambda i, j: (j, 0, 0),
    )
    received = tie(received, queryup_part, outproj_part, down_out, gu_rows, down_rows)
    received = received.astype(jnp.float32)
    grad_latent_n, grad_keys, grad_values = (
        received[:, :QR],
        received[:, QR : QR + DH],
        received[:, QR + DH :],
    )
    layer_out = (hidden + down_out.astype(jnp.float32)).astype(jnp.bfloat16)
    downproj_grad = down_rows[0].astype(jnp.float32)
    queryup_grad = lax.psum_scatter(queryup_part, "seq", scatter_dimension=0, tiled=True)
    queryup_grad = queryup_grad[0].astype(jnp.float32)
    outproj_grad = lax.psum_scatter(outproj_part, "seq", scatter_dimension=0, tiled=True)
    outproj_grad = outproj_grad[0].astype(jnp.float32)
    gu_back = exchange(
        gu_rows.reshape(2, head_count, own_rows, units).transpose(1, 0, 2, 3),
        head_place,
        head_count,
    )
    gateup_grad = (
        gu_back.reshape(head_count, 2, own_rows, seq_count, own_units)
        .transpose(2, 1, 3, 0, 4)
        .reshape(own_rows, 2 * device_count * own_units)
        .astype(jnp.float32)
    )
    latent_value, latent_back = jax.vjp(rms_norm, latent, gain_latent)
    grad_latent, latnorm_part = latent_back(grad_latent_n)
    turned_key, key_back = jax.vjp(lambda key_in: rotary(key_in, cos_local, sin_local), key_raw)
    (grad_key_raw,) = key_back(grad_keys)
    grad_proj = jnp.concatenate([grad_latent, grad_key_raw, grad_values], axis=1).astype(
        jnp.bfloat16
    )
    grad_normed = contract(grad_proj, weight_in)
    input_value, input_back = jax.vjp(rms_norm, inputs_f, gain_attn)
    grad_input_n, attnnorm_part = input_back(grad_normed)
    input_grad = grad_hidden + grad_input_n
    latent_col = jnp.pad(
        latnorm_part.reshape(device_count, own_latent), ((0, 0), (0, own_rows - own_latent))
    ).reshape(device_count * own_rows)
    gain_parts = jnp.stack([attnnorm_part, mlpnorm_part, latent_col], axis=1)
    gain_parts = jnp.pad(gain_parts, ((0, 0), (0, 125))).astype(jnp.bfloat16)
    packed_part = packed_product(normed, grad_proj, gain_parts, min(512, model))
    packed_rows = lax.psum_scatter(packed_part, "seq", scatter_dimension=0, tiled=True)
    packed_grad = lax.psum_scatter(
        packed_rows, "head", scatter_dimension=0, tiled=True
    ).astype(jnp.float32)
    attnin_grad = packed_grad[:, :proj_cols]
    attnnorm_grad = packed_grad[:, proj_cols]
    mlpnorm_grad = packed_grad[:, proj_cols + 1]
    latnorm_grad = packed_grad[:own_latent, proj_cols + 2]
    return (
        layer_out,
        input_grad,
        attnnorm_grad,
        attnin_grad,
        latnorm_grad,
        queryup_grad,
        outproj_grad,
        mlpnorm_grad,
        gateup_grad,
        downproj_grad,
    )


def solution(mesh):
    in_specs = (
        P(("seq", "head"), None),
        P("seq", None),
        P(("seq", "head"), None),
        P(("seq", "head")),
        P(("seq", "head"), None),
        P(("seq", "head")),
        P(None, "head"),
        P("head", None),
        P(("seq", "head")),
        P(("seq", "head"), None),
        P(("seq", "head"), None),
    )
    out_specs = (
        P(("seq", "head"), None),
        P(("seq", "head"), None),
        P(("seq", "head")),
        P(("seq", "head"), None),
        P(("seq", "head")),
        P("seq", "head"),
        P("head", "seq"),
        P(("seq", "head")),
        P(("seq", "head"), None),
        P(("seq", "head"), None),
    )
    return jax.shard_map(shards, mesh=mesh, in_specs=in_specs, out_specs=out_specs, check_vma=False)
```

time: 1490 us -> 1140 us (0.77)
  matrix products: 242 us -> 10.9 us
  local copies, waits for them, and re-layouts: 252 us -> 100 us
  Pallas kernels: 0 us -> 121 us
  blocking collectives: 63 us -> 0 us
  other arithmetic: 84.4 us -> 28.6 us
  starting transfers between devices: 5.78 us -> 32.2 us
  loops' own time: 16.2 us -> 0 us
    dot_general x35 -> x0, matrix products: 131 us -> none  [the longest x18 62.2 us: transposed(): lax.dot_general(left, right, (((0,), (0,)), ((), ())), preferred_element_...]
    pallas_call x0 -> x8, Pallas kernels: none -> 121 us  [the longest x1 38.5 us: feed_forward(): pl.pallas_call(feed_kernel, grid=(group // block,), in_specs=[rowed(model...]
    dot_general x36 -> x1, matrix products: 106 us -> 6.7 us  [contract(): lax.dot_general(left, right, (((1,), (1,)), ((), ())), preferred_element_...]
    broadcast_in_dim x75 -> x0, local copies, waits for them, and re-layouts: 96.3 us -> none  [the longest x72 93.4 us: scores_of(): return jnp.where(allowed[:, None, :], raw, NEG)]
    all_gather x1, waiting for transfers between devices: 66.3 us -> 0.02 us  [shards(): cot_all = lax.all_gather(cotangent, 'head', axis=0, tiled=True)]
    all_to_all x1 -> x0, blocking collectives: 63 us -> none  [shards(): lax.all_to_all(pieces, 'head', split_axis=0, concat_axis=0, tiled=True)]
    ppermute x0 -> x14, waiting for transfers between devices: none -> 60 us  [exchange(): arrived.append(lax.ppermute(sent, 'head', route))]
    reduce_scatter x8 -> x6, waiting for transfers between devices: 267 us -> 303 us  [the longest x1 72 us: shards(): lax.psum_scatter(down_part, 'head', scatter_dimension=0, tiled=True)]
  transfers between devices with their start and end apart: 17 -> 31, of which waited for: 16 -> 21; matrix products, arithmetic and copies ran while one was open for 11% -> 8% of each run, Pallas kernels for 0% -> 5%
where the time goes in v2:
time: 1140 us; the launch traced here: 1130 us
  waiting for transfers between devices  809 us (71%)
  Pallas kernels  121 us (11%)
  local copies, waits for them, and re-layouts  100 us (9%)
  starting transfers between devices  32.2 us (3%)
  between operations  30.7 us (3%)
  other arithmetic  28.6 us (3%)
    unnamed x21, waiting for transfers between devices  113 us
    reduce_scatter x1, waiting for transfers between devices, shards(): lax.psum_scatter(down_part, 'head', scatter_dimension=0, tiled=True)  72 us
    all_gather x1, waiting for transfers between devices, shards(): packed_all = lax.all_gather(packed, ('seq', 'head'), axis=0, tiled=True)  71.8 us
    reduce_scatter x1, waiting for transfers between devices, shards(): lax.psum_scatter(attn_part, 'head', scatter_dimension=0, tiled=True)  68.7 us
    all_gather x1, waiting for transfers between devices, shards(): weight_gu = lax.all_gather(turned, 'seq', axis=0, tiled=True)  68.1 us
    ppermute x14, waiting for transfers between devices, exchange(): arrived.append(lax.ppermute(sent, 'head', route))  60 us
    reduce_scatter x1, waiting for transfers between devices, shards(): lax.psum_scatter(grad_part, 'head', scatter_dimension=0, tiled=True)  55.6 us
    all_gather x1, waiting for transfers between devices, shards(): nmlp_all = lax.all_gather(normed_mlp, 'head', axis=0, tiled=True)  54.8 us
  transfers between devices with their start and end apart: 31, of which 21 were waited for; matrix products, arithmetic and copies ran while one was open for 8% of the time, Pallas kernels for 5%

profile of v2, /device:TPU:0, one launch (start us, length us, event | category | flops | bytes accessed | tf_op | source)
XLA Modules:
  0.0 1133.0 jit_solution(6593860336402121440)
XLA Ops:
  11.9 5.0 reshape.201
  48.0 16.5 %collective-permute-done = bf16[2,64,704]{2,1,0:T(8,128)(2,1)} collective-permute-done((bf16[2,64,704]{2,1,0:T(8,128)(2,1)S(1)}, bf16[2,64,704]{2,1,0:T(8,128)(2,1)}, u32[]{:S(2)}, u32[]{:S(2)}) %collective-permute-start) | collective-permute-done | bytes 180256 | tf_op jit(solution)/shard_map/ppermute | solution.py:360
  66.9 10.7 collective-permute-done.1
  77.6 11.5 %collective-permute-start.2 = (bf16[2,64,704]{2,1,0:T(8,128)(2,1)S(1)}, bf16[2,64,704]{2,1,0:T(8,128)(2,1)S(1)}, u32[]{:S(2)}, u32[]{:S(2)}) collective-permute-start(bf16[2,64,704]{2,1,0:T(8,128)(2,1)S(1)} %get-tuple-element.69), channel_id=1, source_target_pairs={{0,3},{1,4},{2,5},{3,6},{4,7},{5,0},{6,1},{7,2},{8,11},{9,12},{10,... | collective-permute-start | bytes 540680 | tf_op jit(solution)/shard_map/ppermute | solution.py:360
  89.2 15.8 %collective-permute-done.2 = bf16[2,64,704]{2,1,0:T(8,128)(2,1)S(1)} collective-permute-done((bf16[2,64,704]{2,1,0:T(8,128)(2,1)S(1)}, bf16[2,64,704]{2,1,0:T(8,128)(2,1)S(1)}, u32[]{:S(2)}, u32[]{:S(2)}) %collective-permute-start.2) | collective-permute-done | bytes 180256 | tf_op jit(solution)/shard_map/ppermute | solution.py:360
  112.4 71.8 %all-gather.8.cloned.1.call-done = bf16[2048,1664]{1,0:T(8,128)(2,1)} async-done(((bf16[64,1664]{1,0:T(8,128)(2,1)}), bf16[2048,1664]{1,0:T(8,128)(2,1)}) %all-gather.8.cloned.1.call-update) | async-done | bytes 6815760 | tf_op jit(solution)/shard_map/all_gather | solution.py:554
  194.7 31.6 %all-gather.16.cloned.1.call-done.down_ref = bf16[704,2048]{1,0:T(8,128)(2,1)} async-done(((bf16[176,2048]{1,0:T(8,128)(2,1)}), bf16[704,2048]{1,0:T(8,128)(2,1)}) %all-gather.16.cloned.1.call-update) | async-done | bytes 2883600 | tf_op jit(solution)/shard_map/all_gather | solution.py:560
  226.4 68.1 %all-gather.14.cloned.1.call-done = bf16[4,2,512,704]{2,3,1,0:T(8,128)(2,1)} async-done(((bf16[1,2,512,704]{2,3,1,0:T(8,128)(2,1)}), bf16[4,2,512,704]{2,3,1,0:T(8,128)(2,1)}) %all-gather.14.cloned.1.call-update) | async-done | bytes 5767184 | tf_op jit(solution)/shard_map/all_gather | solution.py:559
  294.5 53.8 %all-gather.12.cloned.1.call-done.joined_ref.left_ref = bf16[1536,1536]{1,0:T(8,128)(2,1)} async-done(((bf16[192,1536]{1,0:T(8,128)(2,1)}), bf16[1536,1536]{1,0:T(8,128)(2,1)}) %all-gather.12.cloned.1.call-update) | async-done | bytes 4718608 | tf_op jit(solution)/shard_map/all_gather | solution.py:586
  349.5 26.1 %attention_forward.1 = (bf16[1536,2048]{1,0:T(8,128)(2,1)}, bf16[1536,512]{1,0:T(8,128)(2,1)S(1)}, bf16[1536,512]{1,0:T(8,128)(2,1)}, f32[3072,128]{1,0:T(8,128)}) custom-call(s32[3]{0:T(128)S(1)} %and_select_fusion.first_ref, bf16[1536,1536]{1,0:T(8,128)(2,1)} %all-gather.12.cloned.1.call-done.joined_ref.left_ref, s32[1536,1]{1,0:T(8,128)S(1)} %bitcast.106, ...), custom_call_target="tpu_custom_call" | custom-call | flops 6039797760 | bytes 20447232 | tf_op jit(solution)/shard_map/attention_forward/pallas_call | solution.py:158
  376.9 68.7 %reduce-scatter.19.cloned.1.call-done = bf16[192,2048]{1,0:T(8,128)(2,1)} async-done(((bf16[1536,2048]{1,0:T(8,128)(2,1)}), bf16[192,2048]{1,0:T(8,128)(2,1)}) %reduce-scatter.19.cloned.1.call-update) | async-done | bytes 786448 | tf_op jit(solution)/shard_map/reduce_scatter | solution.py:593
  448.5 8.4 copy.59.gu_ref
  456.9 54.8 %all-gather.18.cloned.1.call-done.normed_ref.left_ref = bf16[1536,2048]{1,0:T(8,128)(2,1)} async-done(((bf16[192,2048]{1,0:T(8,128)(2,1)}), bf16[1536,2048]{1,0:T(8,128)(2,1)}) %all-gather.18.cloned.1.call-update) | async-done | bytes 6291472 | tf_op jit(solution)/shard_map/all_gather | solution.py:601
  511.7 38.5 %feed_forward.1 = (bf16[1536,2048]{1,0:T(8,128)(2,1)}, bf16[1536,2048]{1,0:T(8,128)(2,1)}, bf16[1536,704]{1,0:T(8,128)(2,1)}, bf16[1536,704]{1,0:T(8,128)(2,1)}, bf16[1536,704]{1,0:T(8,128)(2,1)}) custom-call(bf16[1536,2048]{1,0:T(8,128)(2,1)} %all-gather.18.cloned.1.call-done.normed_ref.left_ref, ...), custom_call_target="tpu_custom_call" | custom-call | flops 26575110144 | bytes 40304640 | tf_op jit(solution)/shard_map/feed_forward/pallas_call | solution.py:401
  554.7 5.9 weight_product.3
  565.6 13.0 %gu_product.1 = bf16[4,2,512,704]{3,2,1,0:T(8,128)(2,1)S(1)} custom-call(bf16[1536,2048]{1,0:T(8,128)(2,1)} %all-gather.18.cloned.1.call-done.normed_ref.left_ref, bf16[1536,704]{1,0:T(8,128)(2,1)S(1)} %copy-done.15, bf16[1536,704]{1,0:T(8,128)(2,1)S(1)} %copy-done.16), custom_call_target="tpu_custom_call" | custom-call | flops 8858370048 | bytes 16384000 | tf_op jit(solution)/shard_map/gu_product/pallas_call | solution.py:503
  581.3 37.6 %reduce-scatter.23.cloned.1.call-done = bf16[192,2048]{1,0:T(8,128)(2,1)} async-done(((bf16[1536,2048]{1,0:T(8,128)(2,1)}), bf16[192,2048]{1,0:T(8,128)(2,1)}) %reduce-scatter.23.cloned.1.call-update) | async-done | bytes 786448 | tf_op jit(solution)/shard_map/reduce_scatter | solution.py:605
  623.2 8.8 copy.61
  632.6 53.2 %all-gather.20.cloned.1.call-done.grad_ref.right_ref = bf16[1536,2048]{1,0:T(8,128)(2,1)} async-done(((bf16[192,2048]{1,0:T(8,128)(2,1)}), bf16[1536,2048]{1,0:T(8,128)(2,1)}) %all-gather.20.cloned.1.call-update) | async-done | bytes 6291472 | tf_op jit(solution)/shard_map/all_gather | solution.py:624
  685.8 26.1 %attention_backward.1 = (bf16[1536,1536]{1,0:T(8,128)(2,1)}, bf16[1536,512]{1,0:T(8,128)(2,1)}) custom-call(s32[3]{0:T(128)} %copy-done.11, bf16[1536,1536]{1,0:T(8,128)(2,1)} %all-gather.12.cloned.1.call-done.joined_ref.left_ref, s32[1536,1]{1,0:T(8,128)} %bitcast.107, f32[1536,128]{1,0:T(8,128)} %copy-done.5, f32[1536,128]{1,0:T(8,128)} %copy-done.6, ...), custom_call_target="tpu_custom_call" | custom-call | flops 7851737088 | bytes 26738688 | tf_op jit(solution)/shard_map/attention_backward/pallas_call | solution.py:291
  723.2 5.4 weight_product.5
  729.7 68.8 %reduce-scatter.31.cloned.1.call-done = bf16[1,2,512,704]{2,3,1,0:T(8,128)(2,1)} async-done(((bf16[4,2,512,704]{2,3,1,0:T(8,128)(2,1)}), bf16[1,2,512,704]{2,3,1,0:T(8,128)(2,1)}) %reduce-scatter.31.cloned.1.call-update) | async-done | bytes 1441808
  798.6 72.0 %reduce-scatter.21.cloned.1.call-done = bf16[192,2048]{1,0:T(8,128)(2,1)} async-done(((bf16[1536,2048]{1,0:T(8,128)(2,1)}), bf16[192,2048]{1,0:T(8,128)(2,1)}) %reduce-scatter.21.cloned.1.call-update) | async-done | bytes 786448 | tf_op jit(solution)/shard_map/reduce_scatter | solution.py:617
  870.6 55.6 %reduce-scatter.25.cloned.1.call-done = bf16[192,1536]{1,0:T(8,128)(2,1)} async-done(((bf16[1536,1536]{1,0:T(8,128)(2,1)}), bf16[192,1536]{1,0:T(8,128)(2,1)}) %reduce-scatter.25.cloned.1.call-update) | async-done | bytes 589840 | tf_op jit(solution)/shard_map/reduce_scatter | solution.py:639
  929.7 6.7 fusion.9
  955.5 16.7 %collective-permute-done.8 = bf16[2,64,704]{2,1,0:T(8,128)(2,1)S(1)} collective-permute-done((bf16[2,64,704]{2,1,0:T(8,128)(2,1)S(1)}, bf16[2,64,704]{2,1,0:T(8,128)(2,1)S(1)}, u32[]{:S(2)}, u32[]{:S(2)}) %collective-permute-start.8) | collective-permute-done | bytes 180256 | tf_op jit(solution)/shard_map/ppermute | solution.py:360
  976.9 38.7 %reduce-scatter.27.cloned.1.call-done = bf16[512,1664]{1,0:T(8,128)(2,1)} async-done(((bf16[2048,1664]{1,0:T(8,128)(2,1)}), bf16[512,1664]{1,0:T(8,128)(2,1)}) %reduce-scatter.27.cloned.1.call-update) | async-done | bytes 1703952 | tf_op jit(solution)/shard_map/reduce_scatter | solution.py:701
  1026.8 5.0 reshape.213
  1031.8 6.7 copy.64
  1038.4 5.5 reshape.211
  1048.5 36.5 %reduce-scatter.37.cloned.1.call-done = bf16[1,512,512]{2,1,0:T(8,128)(2,1)} async-done(((bf16[4,512,512]{2,1,0:T(8,128)(2,1)}), bf16[1,512,512]{2,1,0:T(8,128)(2,1)}) %reduce-scatter.37.cloned.1.call-update) | async-done | bytes 524304
  1091.4 30.5 %reduce-scatter.29.cloned.1.call-done = bf16[64,1664]{1,0:T(8,128)(2,1)} async-done(((bf16[512,1664]{1,0:T(8,128)(2,1)}), bf16[64,1664]{1,0:T(8,128)(2,1)}) %reduce-scatter.29.cloned.1.call-update) | async-done | bytes 213008 | tf_op jit(solution)/shard_map/reduce_scatter | solution.py:702
  (244 shorter events, 128.2 us)
Async XLA Ops:
  7.2 105.2 %all-gather.10.cloned.1.call-start = ((), (), s32[]{:S(2)}) async-start(), calls=%async_computation.11 | async-start | bytes 7077888 | tf_op jit(solution)/shard_map/all_gather | solution.py:561
  7.9 176.2 %all-gather.8.cloned.1.call-start = ((), (), s32[]{:S(2)}) async-start(), calls=%async_computation.10 | async-start | bytes 7028736 | tf_op jit(solution)/shard_map/all_gather | solution.py:554
  11.1 215.3 %all-gather.16.cloned.1.call-start = ((), (), s32[]{:S(2)}) async-start(), calls=%async_computation.14 | async-start | bytes 3604480 | tf_op jit(solution)/shard_map/all_gather | solution.py:560
  11.8 282.7 %all-gather.14.cloned.1.call-start = ((), (), s32[]{:S(2)}) async-start(), calls=%async_computation.13 | async-start | bytes 7208960 | tf_op jit(solution)/shard_map/all_gather | solution.py:559
  23.9 82.1 %collective-permute-start.6 = (bf16[2,64,704]{2,1,0:T(8,128)(2,1)S(1)}, bf16[2,64,704]{2,1,0:T(8,128)(2,1)S(1)}, u32[]{:S(2)}, u32[]{:S(2)}) collective-permute-start(bf16[2,64,704]{2,1,0:T(8,128)(2,1)S(1)} %get-tuple-element.65), channel_id=1, source_target_pairs={{0,7},{1,0},{2,1},{3,2},{4,3},{5,4},{6,5},{7,6},{8,15},{9,8},{10,9... | collective-permute-start | bytes 540680 | tf_op jit(solution)/shard_map/ppermute | solution.py:360
  28.6 77.4 %collective-permute-start.5 = (bf16[2,64,704]{2,1,0:T(8,128)(2,1)S(1)}, bf16[2,64,704]{2,1,0:T(8,128)(2,1)S(1)}, u32[]{:S(2)}, u32[]{:S(2)}) collective-permute-start(bf16[2,64,704]{2,1,0:T(8,128)(2,1)S(1)} %get-tuple-element.66), channel_id=1, source_target_pairs={{0,6},{1,7},{2,0},{3,1},{4,2},{5,3},{6,4},{7,5},{8,14},{9,15},{10,... | collective-permute-start | bytes 540680 | tf_op jit(solution)/shard_map/ppermute | solution.py:360
  29.2 76.7 %collective-permute-start.4 = (bf16[2,64,704]{2,1,0:T(8,128)(2,1)S(1)}, bf16[2,64,704]{2,1,0:T(8,128)(2,1)S(1)}, u32[]{:S(2)}, u32[]{:S(2)}) collective-permute-start(bf16[2,64,704]{2,1,0:T(8,128)(2,1)S(1)} %get-tuple-element.67), channel_id=1, source_target_pairs={{0,5},{1,6},{2,7},{3,0},{4,1},{5,2},{6,3},{7,4},{8,13},{9,14},{10,... | collective-permute-start | bytes 540680 | tf_op jit(solution)/shard_map/ppermute | solution.py:360
  29.2 75.8 %collective-permute-start.3 = (bf16[2,64,704]{2,1,0:T(8,128)(2,1)S(1)}, bf16[2,64,704]{2,1,0:T(8,128)(2,1)}, u32[]{:S(2)}, u32[]{:S(2)}) collective-permute-start(bf16[2,64,704]{2,1,0:T(8,128)(2,1)S(1)} %get-tuple-element.68), channel_id=1, source_target_pairs={{0,4},{1,5},{2,6},{3,7},{4,0},{5,1},{6,2},{7,3},{8,12},{9,13},{10,... | collective-permute-start | bytes 540680 | tf_op jit(solution)/shard_map/ppermute | solution.py:360
  31.9 32.6 %collective-permute-start = (bf16[2,64,704]{2,1,0:T(8,128)(2,1)S(1)}, bf16[2,64,704]{2,1,0:T(8,128)(2,1)}, u32[]{:S(2)}, u32[]{:S(2)}) collective-permute-start(bf16[2,64,704]{2,1,0:T(8,128)(2,1)S(1)} %get-tuple-element.71), channel_id=1, source_target_pairs={{0,1},{1,2},{2,3},{3,4},{4,5},{5,6},{6,7},{7,0},{8,9},{9,10},{10,1... | collective-permute-start | bytes 540680 | tf_op jit(solution)/shard_map/ppermute | solution.py:360
  64.5 13.1 %collective-permute-start.1 = (bf16[2,64,704]{2,1,0:T(8,128)(2,1)S(1)}, bf16[2,64,704]{2,1,0:T(8,128)(2,1)S(1)}, u32[]{:S(2)}, u32[]{:S(2)}) collective-permute-start(bf16[2,64,704]{2,1,0:T(8,128)(2,1)S(1)} %get-tuple-element.70), channel_id=1, source_target_pairs={{0,2},{1,3},{2,4},{3,5},{4,6},{5,7},{6,0},{7,1},{8,10},{9,11},{10,... | collective-permute-start | bytes 540680 | tf_op jit(solution)/shard_map/ppermute | solution.py:360
  77.6 27.3 %collective-permute-start.2 = (bf16[2,64,704]{2,1,0:T(8,128)(2,1)S(1)}, bf16[2,64,704]{2,1,0:T(8,128)(2,1)S(1)}, u32[]{:S(2)}, u32[]{:S(2)}) collective-permute-start(bf16[2,64,704]{2,1,0:T(8,128)(2,1)S(1)} %get-tuple-element.69), channel_id=1, source_target_pairs={{0,3},{1,4},{2,5},{3,6},{4,7},{5,0},{6,1},{7,2},{8,11},{9,12},{10,... | collective-permute-start | bytes 540680 | tf_op jit(solution)/shard_map/ppermute | solution.py:360
  107.9 240.3 %all-gather.12.cloned.1.call-start = ((), (), s32[]{:S(2)}) async-start(), calls=%async_computation.12 | async-start | bytes 5308416 | tf_op jit(solution)/shard_map/all_gather | solution.py:586
  108.9 820.8 %copy-start.36 = (f32[192]{0:T(256)}, f32[192]{0:T(256)S(1)}, u32[]{:S(2)}) copy-start(f32[192]{0:T(256)S(1)} %fusion.19) | copy-start | bytes 2308
  194.0 251.6 %reduce-scatter.19.cloned.1.call-start = ((), (), s32[]{:S(2)}) async-start(), calls=%async_computation.15 | async-start | bytes 7077888 | tf_op jit(solution)/shard_map/reduce_scatter | solution.py:593
  376.9 134.9 %all-gather.18.cloned.1.call-start = ((), (), s32[]{:S(2)}) async-start(), calls=%async_computation.16 | async-start | bytes 7077888 | tf_op jit(solution)/shard_map/all_gather | solution.py:601
  448.5 170.4 %reduce-scatter.23.cloned.1.call-start = ((), (), s32[]{:S(2)}) async-start(), calls=%async_computation.18 | async-start | bytes 7077888 | tf_op jit(solution)/shard_map/reduce_scatter | solution.py:605
  550.3 135.5 %all-gather.20.cloned.1.call-start = ((), (), s32[]{:S(2)}) async-start(), calls=%async_computation.19 | async-start | bytes 7077888 | tf_op jit(solution)/shard_map/all_gather | solution.py:624
  622.5 107.2 %reduce-scatter.33.cloned.1.call-start = ((), (), s32[]{:S(2)}) async-start(), calls=%async_computation.24 | async-start | bytes 3604480
  623.1 175.5 %reduce-scatter.31.cloned.1.call-start = ((), (), s32[]{:S(2)}) async-start(), calls=%async_computation.23 | async-start | bytes 7208960
  631.9 238.6 %reduce-scatter.21.cloned.1.call-start = ((), (), s32[]{:S(2)}) async-start(), calls=%async_computation.17 | async-start | bytes 7077888 | tf_op jit(solution)/shard_map/reduce_scatter | solution.py:617
  632.5 293.7 %reduce-scatter.25.cloned.1.call-start = ((), (), s32[]{:S(2)}) async-start(), calls=%async_computation.20 | async-start | bytes 5308416 | tf_op jit(solution)/shard_map/reduce_scatter | solution.py:639
  711.9 303.7 %reduce-scatter.27.cloned.1.call-start = ((), (), s32[]{:S(2)}) async-start(), calls=%async_computation.21 | async-start | bytes 8519680 | tf_op jit(solution)/shard_map/reduce_scatter | solution.py:701
  942.5 104.2 %reduce-scatter.35.cloned.1.call-start = ((), (), s32[]{:S(2)}) async-start(), calls=%async_computation.25 | async-start | bytes 1310720
  943.1 141.9 %reduce-scatter.37.cloned.1.call-start = ((), (), s32[]{:S(2)}) async-start(), calls=%async_computation.26 | async-start | bytes 2621440
  943.7 178.2 %reduce-scatter.29.cloned.1.call-start = ((), (), s32[]{:S(2)}) async-start(), calls=%async_computation.22 | async-start | bytes 1916928 | tf_op jit(solution)/shard_map/reduce_scatter | solution.py:702
  946.3 8.5 collective-permute-start.7
  948.0 70.4 %collective-permute-start.13 = (bf16[2,64,704]{2,1,0:T(8,128)(2,1)S(1)}, bf16[2,64,704]{2,1,0:T(8,128)(2,1)S(1)}, u32[]{:S(2)}, u32[]{:S(2)}) collective-permute-start(bf16[2,64,704]{2,1,0:T(8,128)(2,1)S(1)} %get-tuple-element.56), channel_id=1, source_target_pairs={{0,7},{1,0},{2,1},{3,2},{4,3},{5,4},{6,5},{7,6},{8,15},{9,8},{10,9... | collective-permute-start | bytes 540680 | tf_op jit(solution)/shard_map/ppermute | solution.py:360
  951.1 66.7 %collective-permute-start.12 = (bf16[2,64,704]{2,1,0:T(8,128)(2,1)S(1)}, bf16[2,64,704]{2,1,0:T(8,128)(2,1)S(1)}, u32[]{:S(2)}, u32[]{:S(2)}) collective-permute-start(bf16[2,64,704]{2,1,0:T(8,128)(2,1)S(1)} %get-tuple-element.57), channel_id=1, source_target_pairs={{0,6},{1,7},{2,0},{3,1},{4,2},{5,3},{6,4},{7,5},{8,14},{9,15},{10,... | collective-permute-start | bytes 540680 | tf_op jit(solution)/shard_map/ppermute | solution.py:360
  951.1 66.0 %collective-permute-start.11 = (bf16[2,64,704]{2,1,0:T(8,128)(2,1)}, bf16[2,64,704]{2,1,0:T(8,128)(2,1)S(1)}, u32[]{:S(2)}, u32[]{:S(2)}) collective-permute-start(bf16[2,64,704]{2,1,0:T(8,128)(2,1)} %get-tuple-element.58), channel_id=1, source_target_pairs={{0,5},{1,6},{2,7},{3,0},{4,1},{5,2},{6,3},{7,4},{8,13},{9,14},{10,... | collective-permute-start | bytes 540680 | tf_op jit(solution)/shard_map/ppermute | solution.py:360
  951.1 65.3 %collective-permute-start.10 = (bf16[2,64,704]{2,1,0:T(8,128)(2,1)}, bf16[2,64,704]{2,1,0:T(8,128)(2,1)S(1)}, u32[]{:S(2)}, u32[]{:S(2)}) collective-permute-start(bf16[2,64,704]{2,1,0:T(8,128)(2,1)} %get-tuple-element.59), channel_id=1, source_target_pairs={{0,4},{1,5},{2,6},{3,7},{4,0},{5,1},{6,2},{7,3},{8,12},{9,13},{10,... | collective-permute-start | bytes 540680 | tf_op jit(solution)/shard_map/ppermute | solution.py:360
  954.8 17.4 %collective-permute-start.8 = (bf16[2,64,704]{2,1,0:T(8,128)(2,1)S(1)}, bf16[2,64,704]{2,1,0:T(8,128)(2,1)S(1)}, u32[]{:S(2)}, u32[]{:S(2)}) collective-permute-start(bf16[2,64,704]{2,1,0:T(8,128)(2,1)S(1)} %get-tuple-element.61), channel_id=1, source_target_pairs={{0,2},{1,3},{2,4},{3,5},{4,6},{5,7},{6,0},{7,1},{8,10},{9,11},{10,... | collective-permute-start | bytes 540680 | tf_op jit(solution)/shard_map/ppermute | solution.py:360
  972.2 43.4 %collective-permute-start.9 = (bf16[2,64,704]{2,1,0:T(8,128)(2,1)}, bf16[2,64,704]{2,1,0:T(8,128)(2,1)S(1)}, u32[]{:S(2)}, u32[]{:S(2)}) collective-permute-start(bf16[2,64,704]{2,1,0:T(8,128)(2,1)} %get-tuple-element.60), channel_id=1, source_target_pairs={{0,3},{1,4},{2,5},{3,6},{4,7},{5,0},{6,1},{7,2},{8,11},{9,12},{10,... | collective-permute-start | bytes 540680 | tf_op jit(solution)/shard_map/ppermute | solution.py:360
  (38 other events, 2345.9 us)
Sparse Core Ops, SparseCore 0:
  9.7 100.7 all-gather.9
  113.8 70.2 all-gather.7
  186.0 40.3 all-gather.15
  228.6 65.7 all-gather.13
  296.5 51.6 all-gather.11
  377.0 68.6 reduce-scatter.18
  448.6 63.1 all-gather.17
  550.4 68.4 reduce-scatter.22
  622.6 63.1 all-gather.19
  689.3 40.4 reduce-scatter.32
  732.7 65.8 reduce-scatter.30
  800.7 69.7 reduce-scatter.20
  872.9 53.2 reduce-scatter.24
  942.6 72.9 reduce-scatter.26
  1018.9 27.6 reduce-scatter.34
  1049.8 35.1 reduce-scatter.36
  1087.2 34.7 reduce-scatter.28

commit v3 on v2

--- a/solution.py
+++ b/solution.py
@@ -350,19 +350,588 @@
     return lax.optimization_barrier((value,) + others)[0]
 
 
-def exchange(pieces, place, count):
-    arrived = [lax.dynamic_index_in_dim(pieces, place, 0, keepdims=False)]
+MESH = pl.DeviceIdType.MESH
+ANY = pl.BlockSpec(memory_space=pl.ANY)
+
+
+def send(source, target, send_sem, recv_sem, place):
+    return pltpu.make_async_remote_copy(
+        src_ref=source,
+        dst_ref=target,
+        send_sem=send_sem,
+        recv_sem=recv_sem,
+        device_id={"head": place},
+        device_id_type=MESH,
+    )
+
+
+def greet(place, spot, chips, sibling):
+    barrier = pltpu.get_barrier_semaphore()
+    pl.semaphore_signal(barrier, inc=1, device_id={"head": sibling}, device_id_type=MESH)
+
+    @pl.when(spot > 0)
+    def _():
+        pl.semaphore_signal(barrier, inc=1, device_id={"head": place - 2}, device_id_type=MESH)
+
+    @pl.when(spot < chips - 1)
+    def _():
+        pl.semaphore_signal(barrier, inc=1, device_id={"head": place + 2}, device_id_type=MESH)
+
+    below = (spot + chips - 1) // chips
+    above = (2 * chips - 2 - spot) // chips
+    pl.semaphore_wait(barrier, 1 + below + above)
+
+
+def line_places():
+    place = lax.axis_index("head")
+    chips = lax.axis_size("head") // 2
+    spot = place // 2
+    core = lax.rem(place, 2)
+    return place, chips, spot, core, place + 1 - 2 * core
+
+
+CUTS = 4
+
+
+def gather_line(piece_ref, whole_ref, local_sem, up_sem, down_sem, side_sem, recv_sem):
+    place, chips, spot, core, sibling = line_places()
+    rows = piece_ref.shape[0] // CUTS
+
+    def slot(chip, which, cut):
+        return whole_ref.at[2 * chip + which, pl.ds(cut * rows, rows)]
+
+    def mine(cut):
+        return piece_ref.at[pl.ds(cut * rows, rows)]
+
+    def up(chip, cut, source):
+        received = recv_sem.at[2 * chip + core, cut]
+        return send(source, slot(chip, core, cut), up_sem.at[chip, cut], received, place + 2)
+
+    def down(chip, cut, source):
+        received = recv_sem.at[2 * chip + core, cut]
+        return send(source, slot(chip, core, cut), down_sem.at[chip, cut], received, place - 2)
+
+    def side(chip, cut, source):
+        received = recv_sem.at[2 * chip + core, cut]
+        return send(source, slot(chip, core, cut), side_sem.at[chip, cut], received, sibling)
+
+    own = pltpu.make_async_copy(piece_ref, whole_ref.at[place], local_sem)
+    for cut in range(CUTS):
+
+        @pl.when(spot < chips - 1)
+        def _():
+            up(spot, cut, mine(cut)).start()
+
+        @pl.when(spot > 0)
+        def _():
+            down(spot, cut, mine(cut)).start()
+
+    for cut in range(CUTS):
+        side(spot, cut, mine(cut)).start()
+    own.start()
+    yield
+
+    for k in range(1, chips):
+        below = spot - k
+        above = spot + k
+        for cut in range(CUTS):
+
+            @pl.when(below >= 0)
+            def _():
+                landed = slot(below, core, cut)
+                up(below, cut, landed).wait_recv()
+
+                @pl.when(spot < chips - 1)
+                def _():
+                    up(below, cut, landed).start()
+
+                side(below, cut, landed).start()
+
+            @pl.when(above < chips)
+            def _():
+                landed = slot(above, core, cut)
+                down(above, cut, landed).wait_recv()
+
+                @pl.when(spot > 0)
+                def _():
+                    down(above, cut, landed).start()
+
+                side(above, cut, landed).start()
+
+            yield
+
+    own.wait()
+    for chip in range(chips):
+        for cut in range(CUTS):
+            received = recv_sem.at[2 * chip + 1 - core, cut]
+            send(
+                mine(cut), slot(chip, 1 - core, cut), side_sem.at[chip, cut], received, sibling
+            ).wait_recv()
+            side(chip, cut, mine(cut)).wait_send()
+
+            @pl.when((chip <= spot) & (spot < chips - 1))
+            def _():
+                up(chip, cut, mine(cut)).wait_send()
+
+            @pl.when((chip >= spot) & (spot > 0))
+            def _():
+                down(chip, cut, mine(cut)).wait_send()
+
+
+def together(*lines):
+    active = list(lines)
+    while active:
+        active = [line for line in active if next(line, active) is None]
+
+
+def gather_sems(chips):
+    return [
+        pltpu.SemaphoreType.DMA,
+        pltpu.SemaphoreType.DMA((chips, CUTS)),
+        pltpu.SemaphoreType.DMA((chips, CUTS)),
+        pltpu.SemaphoreType.DMA((chips, CUTS)),
+        pltpu.SemaphoreType.DMA((2 * chips, CUTS)),
+    ]
+
+
+def gather_kernel(piece_ref, whole_ref, *sems):
+    place, chips, spot, core, sibling = line_places()
+    greet(place, spot, chips, sibling)
+    together(gather_line(piece_ref, whole_ref, *sems))
+
+
+def gather_head(piece, head_count, collective_id):
+    rows, width = piece.shape
+    chips = head_count // 2
+    whole = pl.pallas_call(
+        gather_kernel,
+        in_specs=[ANY],
+        out_specs=ANY,
+        out_shape=jax.ShapeDtypeStruct((head_count, rows, width), piece.dtype),
+        scratch_shapes=gather_sems(chips),
+        compiler_params=pltpu.CompilerParams(
+            collective_id=collective_id, has_side_effects=True
+        ),
+        cost_estimate=pl.CostEstimate(
+            flops=0, transcendentals=0, bytes_accessed=2 * head_count * rows * width * 20
+        ),
+        name="gather_head",
+    )(piece)
+    return whole.reshape(head_count * rows, width)
+
+
+def reduce_line(
+    part_ref,
+    out_ref,
+    own_buf,
+    side_buf,
+    below_buf,
+    above_buf,
+    load_sem,
+    side_send,
+    side_recv,
+    up_send,
+    up_recv,
+    down_send,
+    down_recv,
+):
+    place, chips, spot, core, sibling = line_places()
+    rows = own_buf.shape[1] // CUTS
+
+    def cut_of(ref, chip, cut):
+        return ref.at[chip, pl.ds(cut * rows, rows)]
+
+    def side(chip, cut):
+        return send(
+            cut_of(part_ref, 2 * chip + 1 - core, cut),
+            cut_of(side_buf, chip, cut),
+            side_send.at[chip, cut],
+            side_recv.at[chip, cut],
+            sibling,
+        )
+
+    def load(chip, cut):
+        return pltpu.make_async_copy(
+            cut_of(part_ref, 2 * chip + core, cut),
+            cut_of(own_buf, chip, cut),
+            load_sem.at[chip, cut],
+        )
+
+    def up(chip, cut):
+        return send(
+            cut_of(own_buf, chip, cut),
+            cut_of(below_buf, chip, cut),
+            up_send.at[chip, cut],
+            up_recv.at[chip, cut],
+            place + 2,
+        )
+
+    def down(chip, cut):
+        return send(
+            cut_of(own_buf, chip, cut),
+            cut_of(above_buf, chip, cut),
+            down_send.at[chip, cut],
+            down_recv.at[chip, cut],
+            place - 2,
+        )
+
+    order = []
+    for k in range((chips + 1) // 2):
+        order += [k] if k == chips - 1 - k else [chips - 1 - k, k]
+    for chip in order:
+        for cut in range(CUTS):
+            side(chip, cut).start()
+            load(chip, cut).start()
+    yield
+
+    def add(chip, cut, others, target):
+        @pl.loop(0, rows // 16)
+        def _(i):
+            part = pl.ds(pl.multiple_of(cut * rows + i * 16, 16), 16)
+            total = own_buf[chip, part, :].astype(jnp.float32)
+            for other in others:
+                total += other[chip, part, :].astype(jnp.float32)
+            if target is None:
+                own_buf[chip, part, :] = total.astype(own_buf.dtype)
+            else:
+                target[part, :] = total.astype(target.dtype)
+
+    def ready(chip, cut):
+        side(chip, cut).wait_recv()
+        load(chip, cut).wait()
+
+    for k in range(chips - 1):
+        high = chips - 1 - k
+        low = k
+        for cut in range(CUTS):
+
+            @pl.when(spot < high)
+            def _():
+                ready(high, cut)
+
+                @pl.when(spot > 0)
+                def _():
+                    up(high, cut).wait_recv()
+                    add(high, cut, [side_buf, below_buf], None)
+
+                @pl.when(spot == 0)
+                def _():
+                    add(high, cut, [side_buf], None)
+
+                up(high, cut).start()
+
+            @pl.when(spot > low)
+            def _():
+                ready(low, cut)
+
+                @pl.when(spot < chips - 1)
+                def _():
+                    down(low, cut).wait_recv()
+                    add(low, cut, [side_buf, above_buf], None)
+
+                @pl.when(spot == chips - 1)
+                def _():
+                    add(low, cut, [side_buf], None)
+
+                down(low, cut).start()
+
+            yield
+
+    for chip in range(chips):
+
+        @pl.when(spot == chip)
+        def _():
+            for cut in range(CUTS):
+                ready(chip, cut)
+                others = [side_buf]
+                if chip > 0:
+                    up(chip, cut).wait_recv()
+                    others.append(below_buf)
+                if chip < chips - 1:
+                    down(chip, cut).wait_recv()
+                    others.append(above_buf)
+                add(chip, cut, others, out_ref)
+
+        for cut in range(CUTS):
+            side(chip, cut).wait_send()
+
+            @pl.when(spot < chip)
+            def _():
+                up(chip, cut).wait_send()
+
+            @pl.when(spot > chip)
+            def _():
+                down(chip, cut).wait_send()
+
+
+def reduce_scratch(chips, rows, width):
+    return [pltpu.VMEM((chips, rows, width), jnp.bfloat16)] * 4 + [
+        pltpu.SemaphoreType.DMA((chips, CUTS))
+    ] * 7
+
+
+def reduce_kernel(part_ref, out_ref, *scratch):
+    place, chips, spot, core, sibling = line_places()
+    greet(place, spot, chips, sibling)
+    together(reduce_line(part_ref, out_ref, *scratch))
+
+
+def reduce_head(part, head_count, collective_id):
+    group, width = part.shape
+    rows = group // head_count
+    chips = head_count // 2
+    return pl.pallas_call(
+        reduce_kernel,
+        in_specs=[ANY],
+        out_specs=pl.BlockSpec(memory_space=pltpu.VMEM),
+        out_shape=jax.ShapeDtypeStruct((rows, width), jnp.float32),
+        scratch_shapes=reduce_scratch(chips, rows, width),
+        compiler_params=pltpu.CompilerParams(
+            collective_id=collective_id, has_side_effects=True, vmem_limit_bytes=48 * 1024 * 1024
+        ),
+        cost_estimate=pl.CostEstimate(
+            flops=0, transcendentals=0, bytes_accessed=2 * head_count * rows * width * 20
+        ),
+        name="reduce_head",
+    )(part.reshape(head_count, rows, width))
+
+
+def greet_all(with_lines):
+    barrier = pltpu.get_barrier_semaphore()
+    waits = 0
+    for axis in ("head", "seq") if with_lines else ("head",):
+        own = lax.axis_index(axis)
+        count = lax.axis_size(axis)
+        for shift in range(1, count):
+            peer = lax.rem(own + shift, count)
+            pl.semaphore_signal(barrier, inc=1, device_id={axis: peer}, device_id_type=MESH)
+        waits += count - 1
+    pl.semaphore_wait(barrier, waits)
+
+
+def swap_line(scatter, piece_ref, out_ref, local_sem, send_sem, recv_sem):
+    place = lax.axis_index("head")
+    count = lax.axis_size("head")
+    rows = piece_ref.shape[2] if scatter else piece_ref.shape[1] // count
+
+    def source(index):
+        if scatter:
+            return piece_ref.at[index]
+        return piece_ref.at[:, pl.ds(pl.multiple_of(index * rows, rows), rows), :]
+
+    def target(index):
+        if scatter:
+            return out_ref.at[:, pl.ds(pl.multiple_of(index * rows, rows), rows), :]
+        return out_ref.at[index]
+
+    own = pltpu.make_async_copy(source(place), target(place), local_sem)
+    own.start()
+    copies = []
     for shift in range(1, count):
-        sent = lax.dynamic_index_in_dim(
-            pieces, lax.rem(place + shift, count), 0, keepdims=False
+        peer = lax.rem(place + shift, count)
+        copy = send(
+            source(peer), target(place), send_sem.at[shift], recv_sem.at[shift], peer
         )
-        route = [(i, (i + shift) % count) for i in range(count)]
-        arrived.append(lax.ppermute(sent, "head", route))
-    stack = jnp.stack(arrived)
-    order = lax.rem(place - jnp.arange(count, dtype=jnp.int32) + count, count)
-    return jnp.stack(
-        [lax.dynamic_index_in_dim(stack, order[i], 0, keepdims=False) for i in range(count)]
-    )
+        copy.start()
+        copies.append(copy)
+    yield
+    own.wait()
+    for copy in copies:
+        copy.wait()
+
+
+def swap_sems(count):
+    return [
+        pltpu.SemaphoreType.DMA,
+        pltpu.SemaphoreType.DMA((count,)),
+        pltpu.SemaphoreType.DMA((count,)),
+    ]
+
+
+def gather_mesh(piece_ref, whole_ref, local_sem, up_sem, down_sem, seq_sem, side_sem, recv_sem):
+    place, chips, spot, core, sibling = line_places()
+    line = lax.axis_index("seq")
+    lines = lax.axis_size("seq")
+
+    def slot(row, chip, which):
+        return whole_ref.at[row, 2 * chip + which]
+
+    def to(axis, where, row, chip, source, sem):
+        return pltpu.make_async_remote_copy(
+            src_ref=source,
+            dst_ref=slot(row, chip, core),
+            send_sem=sem,
+            recv_sem=recv_sem.at[row, 2 * chip + core],
+            device_id={axis: where},
+            device_id_type=MESH,
+        )
+
+    def up(chip, source):
+        return to("head", place + 2, line, chip, source, up_sem.at[chip])
+
+    def down(chip, source):
+        return to("head", place - 2, line, chip, source, down_sem.at[chip])
+
+    def across(shift, chip, source):
+        where = lax.rem(line + shift, lines)
+        return to("seq", where, line, chip, source, seq_sem.at[shift, chip])
+
+    def side(row, chip, source):
+        return to("head", sibling, row, chip, source, side_sem.at[row, chip])
+
+    def spread(chip, source):
+        for shift in range(1, lines):
+            across(shift, chip, source).start()
+        side(line, chip, source).start()
+
+    own = pltpu.make_async_copy(piece_ref, slot(line, spot, core), local_sem)
+
+    @pl.when(spot < chips - 1)
+    def _():
+        up(spot, piece_ref).start()
+
+    @pl.when(spot > 0)
+    def _():
+        down(spot, piece_ref).start()
+
+    spread(spot, piece_ref)
+    own.start()
+    yield
+
+    for k in range(1, chips):
+        below = spot - k
+        above = spot + k
+
+        @pl.when(below >= 0)
+        def _():
+            landed = slot(line, below, core)
+            up(below, landed).wait_recv()
+
+            @pl.when(spot < chips - 1)
+            def _():
+                up(below, landed).start()
+
+            spread(below, landed)
+
+        @pl.when(above < chips)
+        def _():
+            landed = slot(line, above, core)
+            down(above, landed).wait_recv()
+
+            @pl.when(spot > 0)
+            def _():
+                down(above, landed).start()
+
+            spread(above, landed)
+
+        yield
+
+    for chip in range(chips):
+        for shift in range(1, lines):
+            row = lax.rem(line + shift, lines)
+            landed = slot(row, chip, core)
+            to("seq", row, row, chip, landed, seq_sem.at[shift, chip]).wait_recv()
+            side(row, chip, landed).start()
+        yield
+
+    own.wait()
+    for chip in range(chips):
+        for row in range(lines):
+            landed = slot(row, chip, 1 - core)
+            pltpu.make_async_remote_copy(
+                src_ref=landed,
+                dst_ref=landed,
+                send_sem=side_sem.at[row, chip],
+                recv_sem=recv_sem.at[row, 2 * chip + 1 - core],
+                device_id={"head": sibling},
+                device_id_type=MESH,
+            ).wait_recv()
+            side(row, chip, piece_ref).wait_send()
+        for shift in range(1, lines):
+            across(shift, chip, piece_ref).wait_send()
+
+        @pl.when((chip <= spot) & (spot < chips - 1))
+        def _():
+            up(chip, piece_ref).wait_send()
+
+        @pl.when((chip >= spot) & (spot > 0))
+        def _():
+            down(chip, piece_ref).wait_send()
+
+
+def mesh_sems(lines, chips):
+    return [
+        pltpu.SemaphoreType.DMA,
+        pltpu.SemaphoreType.DMA((chips,)),
+        pltpu.SemaphoreType.DMA((chips,)),
+        pltpu.SemaphoreType.DMA((lines, chips)),
+        pltpu.SemaphoreType.DMA((lines, chips)),
+        pltpu.SemaphoreType.DMA((lines, 2 * chips)),
+    ]
+
+
+def start_kernel(piece_ref, parts_ref, whole_ref, swapped_ref, *sems):
+    greet_all(True)
+    together(
+        gather_mesh(piece_ref, whole_ref, *sems[:6]),
+        swap_line(True, parts_ref, swapped_ref, *sems[6:]),
+    )
+
+
+def gather_and_swap(piece, parts, seq_count, head_count, collective_id):
+    rows, width = piece.shape
+    chips = head_count // 2
+    _, two, depth, units = parts.shape
+    whole, swapped = pl.pallas_call(
+        start_kernel,
+        in_specs=[ANY, ANY],
+        out_specs=[ANY, ANY],
+        out_shape=[
+            jax.ShapeDtypeStruct((seq_count, head_count, rows, width), piece.dtype),
+            jax.ShapeDtypeStruct((two, head_count * depth, units), parts.dtype),
+        ],
+        scratch_shapes=mesh_sems(seq_count, chips) + swap_sems(head_count),
+        compiler_params=pltpu.CompilerParams(
+            collective_id=collective_id, has_side_effects=True
+        ),
+        cost_estimate=pl.CostEstimate(
+            flops=0, transcendentals=0, bytes_accessed=parts.size * 80
+        ),
+        name="gather_and_swap",
+    )(piece, parts)
+    return whole.reshape(seq_count * head_count * rows, width), swapped
+
+
+def finish_kernel(part_ref, parts_ref, out_ref, swapped_ref, *scratch):
+    greet_all(False)
+    together(
+        reduce_line(part_ref, out_ref, *scratch[:11]),
+        swap_line(False, parts_ref, swapped_ref, *scratch[11:]),
+    )
+
+
+def reduce_and_swap(part, parts, head_count, collective_id):
+    group, width = part.shape
+    rows = group // head_count
+    chips = head_count // 2
+    two, depth, units = parts.shape
+    return pl.pallas_call(
+        finish_kernel,
+        in_specs=[ANY, ANY],
+        out_specs=[pl.BlockSpec(memory_space=pltpu.VMEM), ANY],
+        out_shape=[
+            jax.ShapeDtypeStruct((rows, width), jnp.float32),
+            jax.ShapeDtypeStruct((head_count, two, depth // head_count, units), parts.dtype),
+        ],
+        scratch_shapes=reduce_scratch(chips, rows, width) + swap_sems(head_count),
+        compiler_params=pltpu.CompilerParams(
+            collective_id=collective_id, has_side_effects=True, vmem_limit_bytes=48 * 1024 * 1024
+        ),
+        cost_estimate=pl.CostEstimate(
+            flops=0, transcendentals=0, bytes_accessed=2 * head_count * rows * width * 30
+        ),
+        name="reduce_and_swap",
+    )(part.reshape(head_count, rows, width), parts)
 
 
 def feed_kernel(
@@ -545,21 +1114,21 @@
     own_latent = norm_latent.shape[0]
     own_units = down_proj.shape[0]
     units = seq_count * own_units
+    padded = -(-units // 128) * 128
     device_count = seq_count * head_count
     proj_cols = attn_in.shape[1]
     gain_cols = jnp.stack(
         [norm_attn, norm_mlp, jnp.pad(norm_latent, (0, own_rows - own_latent))], axis=1
     )
     packed = jnp.concatenate([attn_in, jnp.pad(gain_cols, ((0, 0), (0, 125)))], axis=1)
-    packed_all = lax.all_gather(packed, ("seq", "head"), axis=0, tiled=True)
     pieces = gate_up.reshape(own_rows, 2, seq_count, head_count, own_units)
     pieces = pieces.transpose(3, 1, 0, 2, 4).reshape(head_count, 2, own_rows, units)
-    turned = exchange(pieces, head_place, head_count)
-    turned = turned.transpose(1, 0, 2, 3).reshape(1, 2, head_count * own_rows, units)
-    weight_gu = lax.all_gather(turned, "seq", axis=0, tiled=True)
+    pieces = jnp.pad(pieces, ((0, 0), (0, 0), (0, 0), (0, padded - units)))
+    cot_all = lax.all_gather(cotangent, "head", axis=0, tiled=True)
+    packed_all, turned = gather_and_swap(packed, pieces, seq_count, head_count, 0)
+    weight_gu = lax.all_gather(turned[None], "seq", axis=0, tiled=True)
     weight_down = lax.all_gather(down_proj, "seq", axis=0, tiled=True)
-    cot_all = lax.all_gather(cotangent, "head", axis=0, tiled=True)
-    packed_all = tie(packed_all, cot_all, turned)
+    weight_down = jnp.pad(weight_down, ((0, padded - units), (0, 0)))
     weight_in = packed_all[:, :proj_cols]
     gain_attn = packed_all[:, proj_cols].astype(jnp.float32)
     gain_mlp = packed_all[:, proj_cols + 1].astype(jnp.float32)
@@ -583,29 +1152,25 @@
     latent_n = rms_norm(latent, gain_latent).astype(jnp.bfloat16)
     keys_local = rotary(key_raw, cos_local, sin_local).astype(jnp.bfloat16)
     values_local = projected[:, QR + DH :].astype(jnp.bfloat16)
-    joined_all = lax.all_gather(
-        jnp.concatenate([latent_n, keys_local, values_local], axis=1), "head", axis=0, tiled=True
-    )
-    joined_all = tie(joined_all, weight_gu, weight_down)
+    joined_all = gather_head(
+        tie(jnp.concatenate([latent_n, keys_local, values_local], axis=1), cot_all),
+        head_count,
+        1,
+    )
     attn_part, queries, mixed, stats = attention_forward(
         joined_all, starts[:, None], cosine, sine, query_up, out_proj, first_keys, block_rows
     )
-    attn_out = lax.psum_scatter(
-        attn_part,
-        "head",
-        scatter_dimension=0,
-        tiled=True,
-    ).astype(jnp.float32)
+    attn_out = reduce_head(attn_part, head_count, 2)
     hidden = inputs_f + attn_out
     normed_mlp = rms_norm(hidden, gain_mlp).astype(jnp.bfloat16)
-    nmlp_all = lax.all_gather(normed_mlp, "head", axis=0, tiled=True)
+    nmlp_all = gather_head(tie(normed_mlp, weight_gu, weight_down), head_count, 3)
     nmlp_part, down_part, activated, grad_gate, grad_up = feed_forward(
         nmlp_all, cot_all, weight_gu, weight_down, 256
     )
-    grad_nmlp = lax.psum_scatter(nmlp_part, "head", scatter_dimension=0, tiled=True)
+    grad_nmlp = reduce_head(nmlp_part, head_count, 4)
     gu_part = gu_product(nmlp_all, grad_gate, grad_up, seq_count, 2)
     down_grad = weight_product(
-        activated,
+        activated[:, :units],
         cot_all,
         units,
         512,
@@ -613,15 +1178,13 @@
         (seq_count, own_units, 512),
         lambda i, j: (0, 0, j),
     )
-    grad_nmlp = tie(grad_nmlp, gu_part, down_grad).astype(jnp.float32)
-    down_out = lax.psum_scatter(down_part, "head", scatter_dimension=0, tiled=True)
     gu_rows = lax.psum_scatter(gu_part, "seq", scatter_dimension=0, tiled=True)
     down_rows = lax.psum_scatter(down_grad, "seq", scatter_dimension=0, tiled=True)
     norm_value, mlp_back = jax.vjp(rms_norm, hidden, gain_mlp)
     grad_hidden_n, mlpnorm_part = mlp_back(grad_nmlp)
     grad_hidden = cotangent.astype(jnp.float32) + grad_hidden_n
     grad_attn = grad_hidden.astype(jnp.bfloat16)
-    grad_attn_all = lax.all_gather(grad_attn, "head", axis=0, tiled=True)
+    grad_attn_all = gather_head(tie(grad_attn, gu_part, down_grad), head_count, 5)
     grad_part, grad_query = attention_backward(
         joined_all,
         starts[:, None],
@@ -636,7 +1199,7 @@
         first_keys,
         block_rows,
     )
-    received = lax.psum_scatter(grad_part, "head", scatter_dimension=0, tiled=True)
+    received = reduce_head(grad_part, head_count, 6)
     head_cols = query_up.shape[1]
     queryup_part = weight_product(
         joined_all,
@@ -657,30 +1220,17 @@
         (1, head_cols, model // seq_count),
         lambda i, j: (j, 0, 0),
     )
-    received = tie(received, queryup_part, outproj_part, down_out, gu_rows, down_rows)
-    received = received.astype(jnp.float32)
+    received = tie(received, queryup_part, outproj_part, gu_rows, down_rows)
     grad_latent_n, grad_keys, grad_values = (
         received[:, :QR],
         received[:, QR : QR + DH],
         received[:, QR + DH :],
     )
-    layer_out = (hidden + down_out.astype(jnp.float32)).astype(jnp.bfloat16)
     downproj_grad = down_rows[0].astype(jnp.float32)
     queryup_grad = lax.psum_scatter(queryup_part, "seq", scatter_dimension=0, tiled=True)
     queryup_grad = queryup_grad[0].astype(jnp.float32)
     outproj_grad = lax.psum_scatter(outproj_part, "seq", scatter_dimension=0, tiled=True)
     outproj_grad = outproj_grad[0].astype(jnp.float32)
-    gu_back = exchange(
-        gu_rows.reshape(2, head_count, own_rows, units).transpose(1, 0, 2, 3),
-        head_place,
-        head_count,
-    )
-    gateup_grad = (
-        gu_back.reshape(head_count, 2, own_rows, seq_count, own_units)
-        .transpose(2, 1, 3, 0, 4)
-        .reshape(own_rows, 2 * device_count * own_units)
-        .astype(jnp.float32)
-    )
     latent_value, latent_back = jax.vjp(rms_norm, latent, gain_latent)
     grad_latent, latnorm_part = latent_back(grad_latent_n)
     turned_key, key_back = jax.vjp(lambda key_in: rotary(key_in, cos_local, sin_local), key_raw)
@@ -698,9 +1248,20 @@
     gain_parts = jnp.stack([attnnorm_part, mlpnorm_part, latent_col], axis=1)
     gain_parts = jnp.pad(gain_parts, ((0, 0), (0, 125))).astype(jnp.bfloat16)
     packed_part = packed_product(normed, grad_proj, gain_parts, min(512, model))
+    down_out, gu_back = reduce_and_swap(
+        tie(down_part, packed_part), gu_rows[0], head_count, 7
+    )
+    layer_out = (hidden + down_out).astype(jnp.bfloat16)
+    gateup_grad = (
+        gu_back[..., :units]
+        .reshape(head_count, 2, own_rows, seq_count, own_units)
+        .transpose(2, 1, 3, 0, 4)
+        .reshape(own_rows, 2 * device_count * own_units)
+        .astype(jnp.float32)
+    )
     packed_rows = lax.psum_scatter(packed_part, "seq", scatter_dimension=0, tiled=True)
     packed_grad = lax.psum_scatter(
-        packed_rows, "head", scatter_dimension=0, tiled=True
+        tie(packed_rows, down_out), "head", scatter_dimension=0, tiled=True
     ).astype(jnp.float32)
     attnin_grad = packed_grad[:, :proj_cols]
     attnnorm_grad = packed_grad[:, proj_cols]

time: 1140 us -> 840 us (0.74)
  waiting for transfers between devices: 809 us -> 91.6 us
  Pallas kernels: 121 us -> 603 us
  starting transfers between devices: 32.2 us -> 0.36 us
  local copies, waits for them, and re-layouts: 100 us -> 80.1 us
  between operations: 30.7 us -> 15 us
    pallas_call x0 -> x8, Pallas kernels: none -> 491 us  [the longest x3 168 us: gather_head(): pl.pallas_call(gather_kernel, in_specs=[ANY], out_specs=ANY, out_shape=ja...]
    all_gather x5 -> x1, waiting for transfers between devices: 302 us -> 0.01 us  [shards(): weight_gu = lax.all_gather(turned[None], 'seq', axis=0, tiled=True)]
    reduce_scatter x5 -> x1, waiting for transfers between devices: 264 us -> 8.27 us  [shards(): lax.psum_scatter(tie(packed_rows, down_out), 'head', scatter_dimension=0,...]
    ppermute x14 -> x0, waiting for transfers between devices: 60 us -> none  [exchange(): arrived.append(lax.ppermute(sent, 'head', route))]
    unnamed x21 -> x13, waiting for transfers between devices: 113 us -> 61.8 us
    reduce_scatter x1, waiting for transfers between devices: 38.7 us -> 0.01 us  [shards(): lax.psum_scatter(packed_part, 'seq', scatter_dimension=0, tiled=True)]
    all_gather x1, waiting for transfers between devices: 31.6 us -> 0.01 us  [shards(): weight_down = lax.all_gather(down_proj, 'seq', axis=0, tiled=True)]
    ppermute x14 -> x0, starting transfers between devices: 30.8 us -> none  [exchange(): arrived.append(lax.ppermute(sent, 'head', route))]
  transfers between devices with their start and end apart: 31 -> 9, of which waited for: 21 -> 4; matrix products, arithmetic and copies ran while one was open for 8% -> 9% of each run, Pallas kernels for 5% -> 59%
where the time goes in v3:
time: 840 us; the launch traced here: 831 us
  Pallas kernels  603 us (72%)
  waiting for transfers between devices  91.6 us (11%)
  local copies, waits for them, and re-layouts  80.1 us (10%)
  other arithmetic  30.8 us (4%)
  between operations  15 us (2%)
  matrix products  10.3 us (1%)
    pallas_call x3, Pallas kernels, gather_head(): pl.pallas_call(gather_kernel, in_specs=[ANY], out_specs=ANY, out_shape=ja...  168 us
    pallas_call x3, Pallas kernels, reduce_head(): pl.pallas_call(reduce_kernel, in_specs=[ANY], out_specs=pl.BlockSpec(memo...  164 us
    pallas_call x1, Pallas kernels, reduce_and_swap(): pl.pallas_call(finish_kernel, in_specs=[ANY, ANY], out_specs=[pl.BlockSpe...  90.4 us
    pallas_call x1, Pallas kernels, gather_and_swap(): pl.pallas_call(start_kernel, in_specs=[ANY, ANY], out_specs=[ANY, ANY], o...  69.3 us
    unnamed x13, waiting for transfers between devices  61.8 us
    pallas_call x1, Pallas kernels, feed_forward(): pl.pallas_call(feed_kernel, grid=(group // block,), in_specs=[rowed(model...  38.6 us
    unnamed x116, local copies, waits for them, and re-layouts  36.9 us
    pallas_call x1, Pallas kernels, attention_backward(): pl.pallas_call(functools.partial(backward_kernel, heads, block), grid_spe...  22.5 us
  transfers between devices with their start and end apart: 9, of which 4 were waited for; matrix products, arithmetic and copies ran while one was open for 9% of the time, Pallas kernels for 59%

profile of v3, /device:TPU:0, one launch (start us, length us, event | category | flops | bytes accessed | tf_op | source)
XLA Modules:
  0.0 831.1 jit_solution(3813715682816096117)
XLA Ops:
  10.2 5.0 reshape.204
  20.5 3.0 pad.34.parts_ref
  24.2 69.3 %gather_and_swap.1 = (bf16[4,8,64,1664]{3,2,1,0:T(8,128)(2,1)}, bf16[2,512,768]{2,1,0:T(8,128)(2,1)}) custom-call(bf16[64,1664]{1,0:T(8,128)(2,1)} %fusion.14.piece_ref, bf16[8,2,64,768]{3,2,1,0:T(8,128)(2,1)} %pad.34.parts_ref), custom_call_target="tpu_custom_call" | custom-call | bytes 62914560 | tf_op jit(solution)/shard_map/gather_and_swap/pallas_call | solution.py:885
  96.0 3.0 slice_convert_fusion.1
  102.9 4.2 fusion.2
  108.8 3.5 multiply_cosine_fusion
  114.1 4.0 pad.35.down_ref
  118.1 21.6 %all-gather.5.cloned.1.call-done.cot_ref.right_ref = bf16[1536,2048]{1,0:T(8,128)(2,1)} async-done(((bf16[192,2048]{1,0:T(8,128)(2,1)}), bf16[1536,2048]{1,0:T(8,128)(2,1)}) %all-gather.5.cloned.1.call-update) | async-done | bytes 6291472 | tf_op jit(solution)/shard_map/all_gather | solution.py:1127
  139.7 43.2 %gather_head.3 = bf16[8,192,1536]{2,1,0:T(8,128)(2,1)} custom-call(bf16[192,1536]{1,0:T(8,128)(2,1)} %pad_maximum_fusion.piece_ref), custom_call_target="tpu_custom_call" | custom-call | bytes 94371840 | tf_op jit(solution)/shard_map/gather_head/pallas_call | solution.py:506
  184.1 21.4 %attention_forward.1 = (bf16[1536,2048]{1,0:T(8,128)(2,1)}, bf16[1536,512]{1,0:T(8,128)(2,1)S(1)}, bf16[1536,512]{1,0:T(8,128)(2,1)}, f32[3072,128]{1,0:T(8,128)}) custom-call(s32[3]{0:T(128)S(1)} %and_select_fusion.first_ref, bf16[1536,1536]{1,0:T(8,128)(2,1)} %bitcast.50, s32[1536,1]{1,0:T(8,128)S(1)} %bitcast.57, ...), custom_call_target="tpu_custom_call" | custom-call | flops 6039797760 | bytes 20447232 | tf_op jit(solution)/shard_map/attention_forward/pallas_call | solution.py:158
  206.6 56.5 %reduce_head.3 = f32[192,2048]{1,0:T(8,128)S(1)} custom-call(bf16[8,192,2048]{2,1,0:T(8,128)(2,1)} %bitcast.66), custom_call_target="tpu_custom_call" | custom-call | bytes 125829120 | tf_op jit(solution)/shard_map/reduce_head/pallas_call | solution.py:683
  265.6 62.1 %gather_head.4 = bf16[8,192,2048]{2,1,0:T(8,128)(2,1)} custom-call(bf16[192,2048]{1,0:T(8,128)(2,1)} %multiply_convert_fusion.piece_ref), custom_call_target="tpu_custom_call" | custom-call | bytes 125829120 | tf_op jit(solution)/shard_map/gather_head/pallas_call | solution.py:506
  327.8 38.6 %feed_forward.1 = (bf16[1536,2048]{1,0:T(8,128)(2,1)}, bf16[1536,2048]{1,0:T(8,128)(2,1)}, bf16[1536,768]{1,0:T(8,128)(2,1)}, bf16[1536,768]{1,0:T(8,128)(2,1)}, bf16[1536,768]{1,0:T(8,128)(2,1)}) custom-call(bf16[1536,2048]{1,0:T(8,128)(2,1)} %bitcast.62, bf16[1536,2048]{1,0:T(8,128)(2,1)} %all-gather.5.cloned.1.call-done.cot_ref.right_ref, ...), custom_call_target="tpu_custom_call" | custom-call | flops 28991029248 | bytes 41680896 | tf_op jit(solution)/shard_map/feed_forward/pallas_call | solution.py:970
  370.9 5.9 weight_product.3
  381.7 12.9 %gu_product.1 = bf16[4,2,512,768]{3,2,1,0:T(8,128)(2,1)S(1)} custom-call(bf16[1536,2048]{1,0:T(8,128)(2,1)} %bitcast.63, bf16[1536,768]{1,0:T(8,128)(2,1)S(1)} %copy-done.21, bf16[1536,768]{1,0:T(8,128)(2,1)S(1)} %copy-done.22), custom_call_target="tpu_custom_call" | custom-call | flops 9663676416 | bytes 17301504 | tf_op jit(solution)/shard_map/gu_product/pallas_call | solution.py:1072
  397.3 56.7 %reduce_head.4 = f32[192,2048]{1,0:T(8,128)S(1)} custom-call(bf16[8,192,2048]{2,1,0:T(8,128)(2,1)} %bitcast.65), custom_call_target="tpu_custom_call" | custom-call | bytes 125829120 | tf_op jit(solution)/shard_map/reduce_head/pallas_call | solution.py:683
  456.7 62.3 %gather_head.5 = bf16[8,192,2048]{2,1,0:T(8,128)(2,1)} custom-call(bf16[192,2048]{1,0:T(8,128)(2,1)} %fusion.18.piece_ref), custom_call_target="tpu_custom_call" | custom-call | bytes 125829120 | tf_op jit(solution)/shard_map/gather_head/pallas_call | solution.py:506
  519.1 22.5 %attention_backward.1 = (bf16[1536,1536]{1,0:T(8,128)(2,1)}, bf16[1536,512]{1,0:T(8,128)(2,1)}) custom-call(s32[3]{0:T(128)} %copy-done.18, bf16[1536,1536]{1,0:T(8,128)(2,1)} %bitcast.51, s32[1536,1]{1,0:T(8,128)} %bitcast.58, f32[1536,128]{1,0:T(8,128)} %copy-done.12, f32[1536,128]{1,0:T(8,128)} %copy-done.13, bf16[1024,512]{1,0:T(8,128)(2,1)} %queryup_ref.3, ...), custom_call_target="tpu_custom_call" | custom-call | flops 7851737088 | bytes 26738688 | tf_op jit(solution)/shard_map/attention_backward/pallas_call | solution.py:291
  543.9 50.4 %reduce_head.5 = f32[192,1536]{1,0:T(8,128)S(1)} custom-call(bf16[8,192,1536]{2,1,0:T(8,128)(2,1)S(1)} %bitcast.55), custom_call_target="tpu_custom_call" | custom-call | bytes 94371840 | tf_op jit(solution)/shard_map/reduce_head/pallas_call | solution.py:683
  596.7 3.4 weight_product.4
  600.1 2.8 copy-done.3
  604.3 4.6 weight_product.5
  614.4 6.2 fusion.11
  623.8 2.8 copy-done
  629.6 90.4 %reduce_and_swap.1 = (f32[192,2048]{1,0:T(8,128)S(1)}, bf16[8,2,64,768]{3,2,1,0:T(8,128)(2,1)S(1)}) custom-call(bf16[8,192,2048]{2,1,0:T(8,128)(2,1)} %bitcast.64, bf16[2,512,768]{2,1,0:T(8,128)(2,1)S(1)} %bitcast.56), custom_call_target="tpu_custom_call" | custom-call | bytes 188743680 | tf_op jit(solution)/shard_map/reduce_and_swap/pallas_call | solution.py:918
  722.4 22.2 %reduce-scatter.23.cloned.1.call-done = bf16[1,256,512]{2,1,0:T(8,128)(2,1)} async-done(((bf16[4,256,512]{2,1,0:T(8,128)(2,1)}), bf16[1,256,512]{2,1,0:T(8,128)(2,1)}) %reduce-scatter.23.cloned.1.call-update) | async-done | bytes 262160
  746.4 36.7 %reduce-scatter.25.cloned.1.call-done = bf16[1,512,512]{2,1,0:T(8,128)(2,1)} async-done(((bf16[4,512,512]{2,1,0:T(8,128)(2,1)}), bf16[1,512,512]{2,1,0:T(8,128)(2,1)}) %reduce-scatter.25.cloned.1.call-update) | async-done | bytes 524304
  788.6 6.2 reshape.222
  794.9 6.6 copy.47
  801.5 5.6 reshape.220
  807.2 4.6 fusion.9
  811.8 8.3 reduce-scatter.17.cloned.1.call-done
  (197 shorter events, 69.5 us)
Async XLA Ops:
  7.2 106.9 %all-gather.7.cloned.1.call-start = ((), (), s32[]{:S(2)}) async-start(), calls=%async_computation.7 | async-start | bytes 3604480 | tf_op jit(solution)/shard_map/all_gather | solution.py:1130
  7.9 131.7 %all-gather.5.cloned.1.call-start = ((), (), s32[]{:S(2)}) async-start(), calls=%async_computation.6 | async-start | bytes 7077888 | tf_op jit(solution)/shard_map/all_gather | solution.py:1127
  8.7 257.0 %all-gather.9.cloned.1.call-start = ((), (), s32[]{:S(2)}) async-start(), calls=%async_computation.10 | async-start | bytes 7864320 | tf_op jit(solution)/shard_map/all_gather | solution.py:1129
  24.2 69.4 %copy-start.42 = (s32[1,1536]{1,0:T(1,128)S(1)}, s32[1,1536]{1,0:T(1,128)}, u32[]{:S(2)}) copy-start(s32[1,1536]{1,0:T(1,128)} %param.12) | copy-start | bytes 18436
  93.6 516.7 %reduce-scatter.21.cloned.1.call-start = ((), (), s32[]{:S(2)}) async-start(), calls=%async_computation.12 | async-start | bytes 3604480
  96.0 86.9 %copy-start.14 = (s32[1,1536]{0,1:T(8,128)}, s32[1,1536]{0,1:T(8,128)S(1)}, u32[]{:S(2)}) copy-start(s32[1,1536]{0,1:T(8,128)S(1)} %copy.53) | copy-start | bytes 18436
  102.9 5.4 copy-start.55
  108.3 4.1 copy-start.30
  108.3 74.6 %copy-start.18 = (s32[3]{0:T(128)}, s32[3]{0:T(128)S(1)}, u32[]{:S(2)}) copy-start(s32[3]{0:T(128)S(1)} %and_select_fusion.first_ref) | copy-start | bytes 40
  108.8 4.4 copy-start.43
  108.8 4.4 copy-start.36
  112.3 70.6 %copy-start.12 = (f32[1536,128]{1,0:T(8,128)}, f32[1536,128]{1,0:T(8,128)S(1)}, u32[]{:S(2)}) copy-start(f32[1536,128]{1,0:T(8,128)S(1)} %get-tuple-element.73.cos_ref) | copy-start | bytes 2359300
  112.3 70.6 %copy-start.13 = (f32[1536,128]{1,0:T(8,128)}, f32[1536,128]{1,0:T(8,128)S(1)}, u32[]{:S(2)}) copy-start(f32[1536,128]{1,0:T(8,128)S(1)} %get-tuple-element.74.sin_ref) | copy-start | bytes 2359300
  206.6 56.5 %copy-start.26 = (bf16[192,2048]{1,0:T(8,128)(2,1)S(1)}, bf16[192,2048]{1,0:T(8,128)(2,1)}, u32[]{:S(2)}) copy-start(bf16[192,2048]{1,0:T(8,128)(2,1)} %param.11) | copy-start | bytes 2359300
  263.4 191.6 %copy-start.40 = (f32[192]{0:T(256)}, f32[192]{0:T(256)S(1)}, u32[]{:S(2)}) copy-start(f32[192]{0:T(256)S(1)} %fusion.17) | copy-start | bytes 2308
  378.4 231.8 %reduce-scatter.19.cloned.1.call-start = ((), (), s32[]{:S(2)}) async-start(), calls=%async_computation.11 | async-start | bytes 7864320
  397.3 325.1 %reduce-scatter.15.cloned.1.call-start = ((), (), s32[]{:S(2)}) async-start(), calls=%async_computation.8 | async-start | bytes 8519680 | tf_op jit(solution)/shard_map/reduce_scatter | solution.py:1262
  397.3 56.7 %copy-start.24 = (f32[192,2048]{1,0:T(8,128)S(1)}, f32[192,2048]{1,0:T(8,128)}, u32[]{:S(2)}) copy-start(f32[192,2048]{1,0:T(8,128)} %copy-done.23) | copy-start | bytes 4718596
  543.9 50.5 %copy-start.8 = (bf16[1536,512]{1,0:T(8,128)(2,1)S(1)}, bf16[1536,512]{1,0:T(8,128)(2,1)}, u32[]{:S(2)}) copy-start(bf16[1536,512]{1,0:T(8,128)(2,1)} %get-tuple-element.46.right_ref) | copy-start | bytes 4718596
  614.4 6.2 copy-start.54
  614.4 6.4 copy-start.39
  626.7 117.9 %reduce-scatter.23.cloned.1.call-start = ((), (), s32[]{:S(2)}) async-start(), calls=%async_computation.13 | async-start | bytes 1310720
  627.4 155.7 %reduce-scatter.25.cloned.1.call-start = ((), (), s32[]{:S(2)}) async-start(), calls=%async_computation.14 | async-start | bytes 2621440
  628.2 191.9 %reduce-scatter.17.cloned.1.call-start = ((), (), s32[]{:S(2)}) async-start(), calls=%async_computation.9 | async-start | bytes 1916928 | tf_op jit(solution)/shard_map/reduce_scatter | solution.py:1263
  722.4 63.0 %copy-start.35 = (bf16[1,176,2048]{2,1,0:T(8,128)(2,1)S(1)}, bf16[1,176,2048]{2,1,0:T(8,128)(2,1)}, u32[]{:S(2)}) copy-start(bf16[1,176,2048]{2,1,0:T(8,128)(2,1)} %reduce-scatter.21.cloned.1.call-done) | copy-start | bytes 2162692
  783.1 3.5 copy-start.10
  801.5 5.6 copy-start.48
  801.5 5.6 copy-start.28
  801.5 5.6 copy-start.33
  801.5 5.7 copy-start.41
  801.5 5.7 copy-start.46
  801.5 5.7 copy-start.53
  (33 other events, 60.8 us)
Sparse Core Ops, SparseCore 0:
  9.9 56.0 all-gather.6
  67.6 72.0 all-gather.4
  141.5 68.7 all-gather.8
  378.5 46.1 reduce-scatter.20
  427.6 70.1 reduce-scatter.18
  626.8 86.5 reduce-scatter.14
  716.9 27.6 reduce-scatter.22
  747.8 35.2 reduce-scatter.24
  785.4 34.5 reduce-scatter.16

commit v4 on v3

--- a/solution.py
+++ b/solution.py
@@ -902,36 +902,213 @@
     return whole.reshape(seq_count * head_count * rows, width), swapped
 
 
-def finish_kernel(part_ref, parts_ref, out_ref, swapped_ref, *scratch):
-    greet_all(False)
+def reduce_mesh(
+    part_ref,
+    out_ref,
+    own_buf,
+    side_buf,
+    across_buf,
+    line_buf,
+    below_buf,
+    above_buf,
+    load_sem,
+    side_send,
+    side_recv,
+    across_send,
+    across_recv,
+    up_send,
+    up_recv,
+    down_send,
+    down_recv,
+):
+    place, chips, spot, core, sibling = line_places()
+    line = lax.axis_index("seq")
+    lines = lax.axis_size("seq")
+    rows = own_buf.shape[2]
+
+    def row_of(shift):
+        return lax.rem(line + shift, lines)
+
+    def side(shift):
+        row = row_of(shift)
+        return send(
+            part_ref.at[row, :, 1 - core],
+            side_buf.at[row],
+            side_send.at[row],
+            side_recv.at[row],
+            sibling,
+        )
+
+    def load(shift):
+        row = row_of(shift)
+        return pltpu.make_async_copy(part_ref.at[row, :, core], own_buf.at[row], load_sem.at[row])
+
+    def across(shift, chip):
+        return pltpu.make_async_remote_copy(
+            src_ref=own_buf.at[row_of(shift), chip],
+            dst_ref=across_buf.at[shift, chip],
+            send_sem=across_send.at[shift, chip],
+            recv_sem=across_recv.at[shift, chip],
+            device_id={"seq": row_of(shift)},
+            device_id_type=MESH,
+        )
+
+    def hop(chip, target, send_sem, recv_sem, where):
+        return send(
+            line_buf.at[chip], target.at[chip], send_sem.at[chip], recv_sem.at[chip], where
+        )
+
+    def up(chip):
+        return hop(chip, below_buf, up_send, up_recv, place + 2)
+
+    def down(chip):
+        return hop(chip, above_buf, down_send, down_recv, place - 2)
+
+    def add(terms, target):
+        @pl.loop(0, rows // 16)
+        def _(i):
+            part = pl.ds(pl.multiple_of(i * 16, 16), 16)
+            total = terms[0][part, :].astype(jnp.float32)
+            for term in terms[1:]:
+                total += term[part, :].astype(jnp.float32)
+            target[part, :] = total.astype(target.dtype)
+
+    order = []
+    for k in range((chips + 1) // 2):
+        order += [k] if k == chips - 1 - k else [chips - 1 - k, k]
+    shifts = list(range(1, lines)) + [0]
+    for shift in shifts:
+        side(shift).start()
+        load(shift).start()
+    for shift in shifts:
+        side(shift).wait_recv()
+        load(shift).wait()
+        row = row_of(shift)
+        if shift:
+            for chip in order:
+                add([own_buf.at[row, chip], side_buf.at[row, chip]], own_buf.at[row, chip])
+                across(shift, chip).start()
+            yield
+
+    for chip in order:
+        for shift in range(1, lines):
+            across(shift, chip).wait_recv()
+        terms = [own_buf.at[line, chip], side_buf.at[line, chip]]
+        terms += [across_buf.at[shift, chip] for shift in range(1, lines)]
+        add(terms, line_buf.at[chip])
+
+        if chip > 0:
+
+            @pl.when(spot == 0)
+            def _():
+                up(chip).start()
+
+        if chip < chips - 1:
+
+            @pl.when(spot == chips - 1)
+            def _():
+                down(chip).start()
+
+        yield
+
+    for k in range(chips - 1):
+        high = chips - 1 - k
+        low = k
+
+        @pl.when((spot < high) & (spot > 0))
+        def _():
+            up(high).wait_recv()
+            add([line_buf.at[high], below_buf.at[high]], line_buf.at[high])
+            up(high).start()
+
+        @pl.when((spot > low) & (spot < chips - 1))
+        def _():
+            down(low).wait_recv()
+            add([line_buf.at[low], above_buf.at[low]], line_buf.at[low])
+            down(low).start()
+
+        yield
+
+    for chip in range(chips):
+
+        @pl.when(spot == chip)
+        def _():
+            terms = [line_buf.at[chip]]
+            if chip > 0:
+                up(chip).wait_recv()
+                terms.append(below_buf.at[chip])
+            if chip < chips - 1:
+                down(chip).wait_recv()
+                terms.append(above_buf.at[chip])
+            add(terms, out_ref)
+
+        for shift in range(1, lines):
+            across(shift, chip).wait_send()
+
+        @pl.when(spot < chip)
+        def _():
+            up(chip).wait_send()
+
+        @pl.when(spot > chip)
+        def _():
+            down(chip).wait_send()
+
+    for shift in shifts:
+        side(shift).wait_send()
+
+
+def mesh_scratch(lines, chips, rows, width):
+    whole = pltpu.VMEM((lines, chips, rows, width), jnp.bfloat16)
+    line = pltpu.VMEM((chips, rows, width), jnp.bfloat16)
+    per_line = pltpu.SemaphoreType.DMA((lines,))
+    per_chip = pltpu.SemaphoreType.DMA((chips,))
+    both = pltpu.SemaphoreType.DMA((lines, chips))
+    return [whole] * 3 + [line] * 3 + [per_line] * 3 + [both] * 2 + [per_chip] * 4
+
+
+def finish_kernel(
+    packed_ref, part_ref, parts_ref, packed_out_ref, out_ref, swapped_ref, *scratch
+):
+    greet_all(True)
     together(
-        reduce_line(part_ref, out_ref, *scratch[:11]),
-        swap_line(False, parts_ref, swapped_ref, *scratch[11:]),
-    )
-
-
-def reduce_and_swap(part, parts, head_count, collective_id):
+        reduce_mesh(packed_ref, packed_out_ref, *scratch[:15]),
+        reduce_line(part_ref, out_ref, *scratch[15:26]),
+        swap_line(False, parts_ref, swapped_ref, *scratch[26:]),
+    )
+
+
+def reduce_and_swap(packed, part, parts, seq_count, head_count, collective_id):
     group, width = part.shape
     rows = group // head_count
     chips = head_count // 2
     two, depth, units = parts.shape
+    packed_rows = packed.shape[0] // (seq_count * head_count)
+    packed_width = packed.shape[1]
+    vmem = pl.BlockSpec(memory_space=pltpu.VMEM)
     return pl.pallas_call(
         finish_kernel,
-        in_specs=[ANY, ANY],
-        out_specs=[pl.BlockSpec(memory_space=pltpu.VMEM), ANY],
+        in_specs=[ANY, ANY, ANY],
+        out_specs=[vmem, vmem, ANY],
         out_shape=[
+            jax.ShapeDtypeStruct((packed_rows, packed_width), jnp.float32),
             jax.ShapeDtypeStruct((rows, width), jnp.float32),
             jax.ShapeDtypeStruct((head_count, two, depth // head_count, units), parts.dtype),
         ],
-        scratch_shapes=reduce_scratch(chips, rows, width) + swap_sems(head_count),
+        scratch_shapes=mesh_scratch(seq_count, chips, packed_rows, packed_width)
+        + reduce_scratch(chips, rows, width)
+        + swap_sems(head_count),
         compiler_params=pltpu.CompilerParams(
-            collective_id=collective_id, has_side_effects=True, vmem_limit_bytes=48 * 1024 * 1024
+            collective_id=collective_id, has_side_effects=True, vmem_limit_bytes=56 * 1024 * 1024
         ),
         cost_estimate=pl.CostEstimate(
             flops=0, transcendentals=0, bytes_accessed=2 * head_count * rows * width * 30
         ),
         name="reduce_and_swap",
-    )(part.reshape(head_count, rows, width), parts)
+    )(
+        packed.reshape(seq_count, chips, 2, packed_rows, packed_width),
+        part.reshape(head_count, rows, width),
+        parts,
+    )
 
 
 def feed_kernel(
@@ -1127,7 +1304,7 @@
     cot_all = lax.all_gather(cotangent, "head", axis=0, tiled=True)
     packed_all, turned = gather_and_swap(packed, pieces, seq_count, head_count, 0)
     weight_gu = lax.all_gather(turned[None], "seq", axis=0, tiled=True)
-    weight_down = lax.all_gather(down_proj, "seq", axis=0, tiled=True)
+    weight_down = lax.all_gather(tie(down_proj, turned), "seq", axis=0, tiled=True)
     weight_down = jnp.pad(weight_down, ((0, padded - units), (0, 0)))
     weight_in = packed_all[:, :proj_cols]
     gain_attn = packed_all[:, proj_cols].astype(jnp.float32)
@@ -1199,7 +1376,6 @@
         first_keys,
         block_rows,
     )
-    received = reduce_head(grad_part, head_count, 6)
     head_cols = query_up.shape[1]
     queryup_part = weight_product(
         joined_all,
@@ -1220,7 +1396,8 @@
         (1, head_cols, model // seq_count),
         lambda i, j: (j, 0, 0),
     )
-    received = tie(received, queryup_part, outproj_part, gu_rows, down_rows)
+    received = reduce_head(tie(grad_part, queryup_part, outproj_part), head_count, 6)
+    received = tie(received, gu_rows, down_rows)
     grad_latent_n, grad_keys, grad_values = (
         received[:, :QR],
         received[:, QR : QR + DH],
@@ -1248,8 +1425,8 @@
     gain_parts = jnp.stack([attnnorm_part, mlpnorm_part, latent_col], axis=1)
     gain_parts = jnp.pad(gain_parts, ((0, 0), (0, 125))).astype(jnp.bfloat16)
     packed_part = packed_product(normed, grad_proj, gain_parts, min(512, model))
-    down_out, gu_back = reduce_and_swap(
-        tie(down_part, packed_part), gu_rows[0], head_count, 7
+    packed_grad, down_out, gu_back = reduce_and_swap(
+        packed_part, down_part, gu_rows[0], seq_count, head_count, 7
     )
     layer_out = (hidden + down_out).astype(jnp.bfloat16)
     gateup_grad = (
@@ -1259,10 +1436,6 @@
         .reshape(own_rows, 2 * device_count * own_units)
         .astype(jnp.float32)
     )
-    packed_rows = lax.psum_scatter(packed_part, "seq", scatter_dimension=0, tiled=True)
-    packed_grad = lax.psum_scatter(
-        tie(packed_rows, down_out), "head", scatter_dimension=0, tiled=True
-    ).astype(jnp.float32)
     attnin_grad = packed_grad[:, :proj_cols]
     attnnorm_grad = packed_grad[:, proj_cols]
     mlpnorm_grad = packed_grad[:, proj_cols + 1]

time: 840 us -> 982 us (1.17)
  waiting for transfers between devices: 91.6 us -> 207 us
  Pallas kernels: 603 us -> 629 us
    unnamed x13 -> x11, waiting for transfers between devices: 61.8 us -> 123 us
    all_gather x1, waiting for transfers between devices: 21.6 us -> 62.5 us  [shards(): cot_all = lax.all_gather(cotangent, 'head', axis=0, tiled=True)]
    pallas_call x1, Pallas kernels: 90.4 us -> 116 us  [reduce_and_swap(): pl.pallas_call(finish_kernel, in_specs=[ANY, ANY, ANY], out_specs=[vmem,...]
    all_gather x1, waiting for transfers between devices: 0.01 us -> 21.8 us  [shards(): lax.all_gather(tie(down_proj, turned), 'seq', axis=0, tiled=True)]
    unnamed x116 -> x104, local copies, waits for them, and re-layouts: 36.9 us -> 33.4 us
  transfers between devices with their start and end apart: 9 -> 7, of which waited for: 4 -> 5; matrix products, arithmetic and copies ran while one was open for 9% -> 3% of each run, Pallas kernels for 59% -> 18%
where the time goes in v4:
time: 982 us; the launch traced here: 973 us
  Pallas kernels  629 us (64%)
  waiting for transfers between devices  207 us (21%)
  local copies, waits for them, and re-layouts  78.5 us (8%)
  other arithmetic  32.3 us (3%)
  between operations  15.3 us (2%)
  matrix products  10.3 us (1%)
    pallas_call x3, Pallas kernels, gather_head(): pl.pallas_call(gather_kernel, in_specs=[ANY], out_specs=ANY, out_shape=ja...  167 us
    pallas_call x3, Pallas kernels, reduce_head(): pl.pallas_call(reduce_kernel, in_specs=[ANY], out_specs=pl.BlockSpec(memo...  164 us
    unnamed x11, waiting for transfers between devices  123 us
    pallas_call x1, Pallas kernels, reduce_and_swap(): pl.pallas_call(finish_kernel, in_specs=[ANY, ANY, ANY], out_specs=[vmem,...  116 us
    pallas_call x1, Pallas kernels, gather_and_swap(): pl.pallas_call(start_kernel, in_specs=[ANY, ANY], out_specs=[ANY, ANY], o...  69.5 us
    all_gather x1, waiting for transfers between devices, shards(): cot_all = lax.all_gather(cotangent, 'head', axis=0, tiled=True)  62.5 us
    pallas_call x1, Pallas kernels, feed_forward(): pl.pallas_call(feed_kernel, grid=(group // block,), in_specs=[rowed(model...  38.6 us
    unnamed x104, local copies, waits for them, and re-layouts  33.4 us
  transfers between devices with their start and end apart: 7, of which 5 were waited for; matrix products, arithmetic and copies ran while one was open for 3% of the time, Pallas kernels for 18%

profile of v4, /device:TPU:0, one launch (start us, length us, event | category | flops | bytes accessed | tf_op | source)
XLA Modules:
  0.0 972.5 jit_solution(7684659740376242851)
XLA Ops:
  8.7 5.8 reshape.207
  23.2 69.5 %gather_and_swap.1 = (bf16[4,8,64,1664]{3,2,1,0:T(8,128)(2,1)}, bf16[2,512,768]{2,1,0:T(8,128)(2,1)}) custom-call(bf16[64,1664]{1,0:T(8,128)(2,1)} %fusion.14.piece_ref, bf16[8,2,64,768]{3,2,1,0:T(8,128)(2,1)} %pad.34.parts_ref), custom_call_target="tpu_custom_call" | custom-call | bytes 62914560 | tf_op jit(solution)/shard_map/gather_and_swap/pallas_call | solution.py:885
  96.7 3.0 slice_convert_fusion.1
  103.5 4.2 fusion.2
  109.5 3.5 multiply_cosine_fusion
  114.8 21.8 %all-gather.7.cloned.1.call-done = bf16[704,2048]{1,0:T(8,128)(2,1)} async-done(((bf16[176,2048]{1,0:T(8,128)(2,1)}), bf16[704,2048]{1,0:T(8,128)(2,1)}) %all-gather.7.cloned.1.call-update) | async-done | bytes 2883600 | tf_op jit(solution)/shard_map/all_gather | solution.py:1307
  136.6 3.9 pad.35.down_ref
  140.5 62.5 %all-gather.5.cloned.1.call-done.cot_ref.right_ref = bf16[1536,2048]{1,0:T(8,128)(2,1)} async-done(((bf16[192,2048]{1,0:T(8,128)(2,1)}), bf16[1536,2048]{1,0:T(8,128)(2,1)}) %all-gather.5.cloned.1.call-update) | async-done | bytes 6291472 | tf_op jit(solution)/shard_map/all_gather | solution.py:1304
  203.0 43.2 %gather_head.3 = bf16[8,192,1536]{2,1,0:T(8,128)(2,1)} custom-call(bf16[192,1536]{1,0:T(8,128)(2,1)} %pad_maximum_fusion.piece_ref), custom_call_target="tpu_custom_call" | custom-call | bytes 94371840 | tf_op jit(solution)/shard_map/gather_head/pallas_call | solution.py:506
  247.4 21.4 %attention_forward.1 = (bf16[1536,2048]{1,0:T(8,128)(2,1)}, bf16[1536,512]{1,0:T(8,128)(2,1)S(1)}, bf16[1536,512]{1,0:T(8,128)(2,1)}, f32[3072,128]{1,0:T(8,128)}) custom-call(s32[3]{0:T(128)S(1)} %and_select_fusion.first_ref, bf16[1536,1536]{1,0:T(8,128)(2,1)} %bitcast.52, s32[1536,1]{1,0:T(8,128)S(1)} %bitcast.58, ...), custom_call_target="tpu_custom_call" | custom-call | flops 6039797760 | bytes 20447232 | tf_op jit(solution)/shard_map/attention_forward/pallas_call | solution.py:158
  270.0 56.4 %reduce_head.3 = f32[192,2048]{1,0:T(8,128)S(1)} custom-call(bf16[8,192,2048]{2,1,0:T(8,128)(2,1)} %bitcast.67), custom_call_target="tpu_custom_call" | custom-call | bytes 125829120 | tf_op jit(solution)/shard_map/reduce_head/pallas_call | solution.py:683
  329.0 62.1 %gather_head.4 = bf16[8,192,2048]{2,1,0:T(8,128)(2,1)} custom-call(bf16[192,2048]{1,0:T(8,128)(2,1)} %multiply_convert_fusion.piece_ref), custom_call_target="tpu_custom_call" | custom-call | bytes 125829120 | tf_op jit(solution)/shard_map/gather_head/pallas_call | solution.py:506
  391.1 38.6 %feed_forward.1 = (bf16[1536,2048]{1,0:T(8,128)(2,1)}, bf16[1536,2048]{1,0:T(8,128)(2,1)}, bf16[1536,768]{1,0:T(8,128)(2,1)}, bf16[1536,768]{1,0:T(8,128)(2,1)}, bf16[1536,768]{1,0:T(8,128)(2,1)}) custom-call(bf16[1536,2048]{1,0:T(8,128)(2,1)} %bitcast.64, bf16[1536,2048]{1,0:T(8,128)(2,1)} %all-gather.5.cloned.1.call-done.cot_ref.right_ref, ...), custom_call_target="tpu_custom_call" | custom-call | flops 28991029248 | bytes 41680896 | tf_op jit(solution)/shard_map/feed_forward/pallas_call | solution.py:1147
  429.8 56.5 %reduce_head.4 = f32[192,2048]{1,0:T(8,128)S(1)} custom-call(bf16[8,192,2048]{2,1,0:T(8,128)(2,1)} %bitcast.66), custom_call_target="tpu_custom_call" | custom-call | bytes 125829120 | tf_op jit(solution)/shard_map/reduce_head/pallas_call | solution.py:683
  490.1 12.9 %gu_product.1 = bf16[4,2,512,768]{3,2,1,0:T(8,128)(2,1)S(1)} custom-call(bf16[1536,2048]{1,0:T(8,128)(2,1)} %bitcast.65, bf16[1536,768]{1,0:T(8,128)(2,1)S(1)} %copy-done.17, bf16[1536,768]{1,0:T(8,128)(2,1)S(1)} %copy-done.18), custom_call_target="tpu_custom_call" | custom-call | flops 9663676416 | bytes 17301504 | tf_op jit(solution)/shard_map/gu_product/pallas_call | solution.py:1249
  510.1 5.9 weight_product.3
  517.6 62.1 %gather_head.5 = bf16[8,192,2048]{2,1,0:T(8,128)(2,1)} custom-call(bf16[192,2048]{1,0:T(8,128)(2,1)} %fusion.18.piece_ref), custom_call_target="tpu_custom_call" | custom-call | bytes 125829120 | tf_op jit(solution)/shard_map/gather_head/pallas_call | solution.py:506
  579.8 22.4 %attention_backward.1 = (bf16[1536,1536]{1,0:T(8,128)(2,1)}, bf16[1536,512]{1,0:T(8,128)(2,1)}) custom-call(s32[3]{0:T(128)} %copy-done.14, bf16[1536,1536]{1,0:T(8,128)(2,1)} %bitcast.53, s32[1536,1]{1,0:T(8,128)} %bitcast.59, f32[1536,128]{1,0:T(8,128)} %copy-done.8, f32[1536,128]{1,0:T(8,128)} %copy-done.9, bf16[1024,512]{1,0:T(8,128)(2,1)} %queryup_ref.3, ...), custom_call_target="tpu_custom_call" | custom-call | flops 7851737088 | bytes 26738688 | tf_op jit(solution)/shard_map/attention_backward/pallas_call | solution.py:291
  606.0 3.4 weight_product.4
  613.6 4.6 weight_product.5
  624.0 50.7 %reduce_head.5 = f32[192,1536]{1,0:T(8,128)S(1)} custom-call(bf16[8,192,1536]{2,1,0:T(8,128)(2,1)S(1)} %bitcast.57), custom_call_target="tpu_custom_call" | custom-call | bytes 94371840 | tf_op jit(solution)/shard_map/reduce_head/pallas_call | solution.py:683
  676.5 6.2 reduce-scatter.19.cloned.1.call-done
  684.9 43.1 %reduce-scatter.15.cloned.1.call-done = bf16[1,176,2048]{2,1,0:T(8,128)(2,1)} async-done(((bf16[4,176,2048]{2,1,0:T(8,128)(2,1)}), bf16[1,176,2048]{2,1,0:T(8,128)(2,1)}) %reduce-scatter.15.cloned.1.call-update) | async-done | bytes 720912
  730.3 70.8 %reduce-scatter.13.cloned.1.call-done = bf16[1,2,512,768]{3,2,1,0:T(8,128)(2,1)} async-done(((bf16[4,2,512,768]{3,2,1,0:T(8,128)(2,1)}), bf16[1,2,512,768]{3,2,1,0:T(8,128)(2,1)}) %reduce-scatter.13.cloned.1.call-update) | async-done | bytes 1572880
  805.3 6.2 fusion.11
  814.7 2.8 copy-done
  817.6 116.4 %reduce_and_swap.1 = (f32[64,1664]{1,0:T(8,128)}, f32[192,2048]{1,0:T(8,128)}, bf16[8,2,64,768]{3,2,1,0:T(8,128)(2,1)}) custom-call(bf16[4,4,2,64,1664]{4,3,2,1,0:T(8,128)(2,1)} %bitcast.51, bf16[8,192,2048]{2,1,0:T(8,128)(2,1)} %bitcast.63, bf16[2,512,768]{2,1,0:T(8,128)(2,1)} %bitcast.68), custom_call_target="tpu_custom_call" | custom-call | bytes 188743680 | tf_op jit(solution)/shard_map/reduce_and_swap/pallas_call | solution.py:1088
  938.7 3.4 slice_convert_fusion
  942.2 6.2 reshape.226
  948.4 6.6 copy.47
  955.0 5.6 reshape.224
  960.6 4.5 fusion.9
  (178 shorter events, 70.8 us)
Async XLA Ops:
  7.2 129.4 %all-gather.7.cloned.1.call-start = ((), (), s32[]{:S(2)}) async-start(), calls=%async_computation.5 | async-start | bytes 3604480 | tf_op jit(solution)/shard_map/all_gather | solution.py:1307
  92.8 110.2 %all-gather.5.cloned.1.call-start = ((), (), s32[]{:S(2)}) async-start(), calls=%async_computation.4 | async-start | bytes 7077888 | tf_op jit(solution)/shard_map/all_gather | solution.py:1304
  93.6 235.4 %all-gather.9.cloned.1.call-start = ((), (), s32[]{:S(2)}) async-start(), calls=%async_computation.6 | async-start | bytes 7864320 | tf_op jit(solution)/shard_map/all_gather | solution.py:1306
  94.3 580.4 %reduce-scatter.17.cloned.1.call-start = ((), (), s32[]{:S(2)}) async-start(), calls=%async_computation.9 | async-start | bytes 1310720
  96.7 149.5 %copy-start.10 = (s32[1,1536]{0,1:T(8,128)}, s32[1,1536]{0,1:T(8,128)S(1)}, u32[]{:S(2)}) copy-start(s32[1,1536]{0,1:T(8,128)S(1)} %copy.53) | copy-start | bytes 18436
  103.5 5.4 copy-start.49
  108.9 4.1 copy-start.26
  108.9 137.2 %copy-start.14 = (s32[3]{0:T(128)}, s32[3]{0:T(128)S(1)}, u32[]{:S(2)}) copy-start(s32[3]{0:T(128)S(1)} %and_select_fusion.first_ref) | copy-start | bytes 40
  109.5 4.4 copy-start.37
  109.5 4.4 copy-start.30
  113.0 133.2 %copy-start.8 = (f32[1536,128]{1,0:T(8,128)}, f32[1536,128]{1,0:T(8,128)S(1)}, u32[]{:S(2)}) copy-start(f32[1536,128]{1,0:T(8,128)S(1)} %get-tuple-element.75.cos_ref) | copy-start | bytes 2359300
  113.0 133.2 %copy-start.9 = (f32[1536,128]{1,0:T(8,128)}, f32[1536,128]{1,0:T(8,128)S(1)}, u32[]{:S(2)}) copy-start(f32[1536,128]{1,0:T(8,128)S(1)} %get-tuple-element.76.sin_ref) | copy-start | bytes 2359300
  270.0 56.5 %copy-start.22 = (bf16[192,2048]{1,0:T(8,128)(2,1)S(1)}, bf16[192,2048]{1,0:T(8,128)(2,1)}, u32[]{:S(2)}) copy-start(bf16[192,2048]{1,0:T(8,128)(2,1)} %param.11) | copy-start | bytes 2359300
  326.7 159.9 %copy-start.34 = (f32[192]{0:T(256)}, f32[192]{0:T(256)S(1)}, u32[]{:S(2)}) copy-start(f32[192]{0:T(256)S(1)} %fusion.17) | copy-start | bytes 2308
  429.8 56.5 %copy-start.20 = (f32[192,2048]{1,0:T(8,128)S(1)}, f32[192,2048]{1,0:T(8,128)}, u32[]{:S(2)}) copy-start(f32[192,2048]{1,0:T(8,128)} %copy-done.19) | copy-start | bytes 4718596
  609.4 73.3 %reduce-scatter.19.cloned.1.call-start = ((), (), s32[]{:S(2)}) async-start(), calls=%async_computation.10 | async-start | bytes 2621440
  609.4 2.8 copy-start.3
  619.5 108.5 %reduce-scatter.15.cloned.1.call-start = ((), (), s32[]{:S(2)}) async-start(), calls=%async_computation.8 | async-start | bytes 3604480
  620.1 181.1 %reduce-scatter.13.cloned.1.call-start = ((), (), s32[]{:S(2)}) async-start(), calls=%async_computation.7 | async-start | bytes 7864320
  801.2 3.0 copy-start.44
  801.2 3.0 copy-start.27
  801.2 3.0 copy-start.32
  801.2 3.0 copy-start.38
  805.3 6.2 copy-start.48
  805.3 6.4 copy-start.33
  814.7 2.8 copy-start
  817.6 121.1 %copy-start.42 = (f32[192]{0:T(256)S(1)}, f32[192]{0:T(256)}, u32[]{:S(2)}) copy-start(f32[192]{0:T(256)} %copy-done.41) | copy-start | bytes 2308
  955.0 5.6 copy-start.24
  955.0 5.6 copy-start.29
  955.0 5.6 copy-start.35
  955.0 5.6 copy-start.40
  955.0 5.6 copy-start.47
  (25 other events, 40.4 us)
Sparse Core Ops, SparseCore 0:
  92.9 43.5 all-gather.6
  138.2 64.7 all-gather.4
  204.8 68.7 all-gather.8
  609.5 34.8 reduce-scatter.16
  647.5 35.2 reduce-scatter.18
  686.2 41.7 reduce-scatter.14
  731.0 70.1 reduce-scatter.12
